TPU v7x, 32 devices: a whole 2x2x4 slice. The times are simulated.
32 devices in a mesh: grp: 2 (over x), spec: 16 (over z, y, core).
Axes of the slice: x: 2, y: 2, z: 4, core: 2. Of those that a mesh axis runs over, the one named last changes fastest.
Arguments:
- vorticity: bfloat16 [128, 1280, 2560], P('grp', 'spec'), parts along dimension 0, may hold values from -32 to 32
- lat_order: int32 [1280], replicated, may hold values from 0 to 1279, as said below
- storm_labels: int32 [128, 256, 720], P('grp', 'spec'), parts along dimension 0, may hold values from 0 to 511, as said below
- storm_owner: int32 [512], P('grp'), parts along dimension 0, may hold values from 0 to 255, each once
Outputs:
- filtered: bfloat16 [128, 256, 720], P('grp', 'spec'), parts along dimension 0
- storm_peak: float32 [512], P(('grp', 'spec')), parts along dimension 0
There are 2 independent parts, one for each index of `grp`. A program takes and returns all parts, laid end to end along the dimension named above; an argument that names none is the same for every part. Nothing has to cross between parts.
Inputs may be any that keep to these rules, and one draw needn't show every extreme that they name: `storm_labels`: labels 256 and above mark points outside every storm; every storm number below 256 labels at least one point of the window. Row j of vorticity lies on latitude lat_order[j], counted from the north; each latitude once. In each block of 80 rows, the second half holds the latitudes 1280 - 1 minus those of the first half, in the same order. `storm_owner`: each slot is owned by one storm.
All inputs are finite; a program needn't handle non-finite values.
Results may differ from a plain program's by a relative error of at most 0.0054.
Values may be sent and summed in bfloat16 or wider, within the bound.
No kernel may reach another device: no remote copies, remote signals or barrier semaphores. Data moves between devices by JAX's collectives and lax.ppermute only.
A program may use at most 192 MiB of HBM per device.

v0:
```python
import math

import jax
import jax.numpy as jnp
from jax import lax
from jax.sharding import PartitionSpec as P

MW = 256
OUT_LAT = 256
OUT_LON = 720


HIGHEST = lax.Precision.HIGHEST
FLOOR = -1e30


def fourier_table(wave_numbers, lon_count):
    longitudes = jnp.arange(lon_count, dtype=jnp.int32)
    phase_steps = longitudes[:, None] * wave_numbers[None, :] % lon_count
    angles = phase_steps.astype(jnp.float32) * (2.0 * math.pi / lon_count)
    stacked = jnp.stack([jnp.cos(angles), -jnp.sin(angles)], axis=-1) / lon_count
    return stacked.astype(jnp.bfloat16)


def synthesis_table(wave_numbers, lon_count):
    longitudes = jnp.arange(lon_count, dtype=jnp.int32)
    phase_steps = wave_numbers[:, None] * longitudes[None, :] % lon_count
    angles = phase_steps.astype(jnp.float32) * (2.0 * math.pi / lon_count)
    factor = jnp.where(wave_numbers == 0, 1.0, 2.0).astype(jnp.float32)[:, None]
    stacked = jnp.stack([factor * jnp.cos(angles), -factor * jnp.sin(angles)], axis=1)
    return stacked.astype(jnp.bfloat16)


def node_values(lat_order, lat_count, band_count, lon_count):
    colatitude = math.pi * (4.0 * lat_order.astype(jnp.float32) + 3.0) / (4.0 * lat_count + 2.0)
    weights = math.pi / lat_count * jnp.sin(colatitude)
    band_index = jnp.arange(band_count, dtype=jnp.float32)
    latitude = ((band_count - 1) / 2.0 - band_index) * (360.0 / lon_count) * (math.pi / 180.0)
    sine_values = jnp.concatenate([jnp.sin(colatitude), jnp.cos(latitude)])
    cosines = jnp.concatenate([jnp.cos(colatitude), jnp.sin(latitude)])
    return (sine_values, cosines, weights)


def legendre(orders, sine_values, cosines, degree_count):
    counters = jnp.arange(1, degree_count, dtype=jnp.float32)
    increments = jnp.log((2.0 * counters + 1.0) / (2.0 * counters))
    partial_value = jnp.sum(
        jnp.where(counters[None, :] <= orders[:, None], increments[None, :], 0.0), axis=1
    )
    diagonal_start = jnp.exp(
        0.5 * math.log(0.5)
        + 0.5 * partial_value[:, None]
        + orders[:, None] * jnp.log(sine_values)[None, :]
    )
    squared = orders * orders

    def advance(state_pair, degree):
        previous, earlier = state_pair
        degree_value = degree.astype(jnp.float32)
        first_scale = jnp.sqrt(
            jnp.maximum(4.0 * degree_value * degree_value - 1.0, 1.0)
            / jnp.maximum(degree_value * degree_value - squared, 1.0)
        )
        shifted = (degree_value - 1.0) * (degree_value - 1.0)
        second_scale = jnp.sqrt(
            jnp.maximum(shifted - squared, 0.0) / jnp.maximum(4.0 * shifted - 1.0, 1.0)
        )
        recurred = first_scale[:, None] * (
            cosines[None, :] * previous - second_scale[:, None] * earlier
        )
        current = jnp.where(
            degree_value < orders[:, None],
            0.0,
            jnp.where(degree_value == orders[:, None], diagonal_start, recurred),
        )
        return ((current, previous), current)

    zero_rows = jnp.zeros((orders.shape[0], sine_values.shape[0]), jnp.float32)
    final_state, degree_rows = lax.scan(
        advance, (zero_rows, zero_rows), jnp.arange(degree_count, dtype=jnp.int32), unroll=16
    )
    return jnp.transpose(degree_rows, (1, 0, 2))


def masked_peaks(grid_values, storm_labels, storm_count):
    field_count = grid_values.shape[0]
    point_count = grid_values.shape[1] * grid_values.shape[2]
    block_fields = math.gcd(field_count, 4)
    values_flat = grid_values.reshape(field_count, point_count)
    labels_flat = storm_labels.reshape(field_count, point_count)
    storms = jnp.arange(storm_count, dtype=jnp.int32)

    def per_block(block_index, running):
        start = block_index * block_fields
        values_block = lax.dynamic_slice_in_dim(values_flat, start, block_fields, 0).reshape(
            block_fields * point_count
        )
        labels_block = lax.dynamic_slice_in_dim(labels_flat, start, block_fields, 0).reshape(
            block_fields * point_count
        )
        matched = labels_block[:, None] == storms[None, :]
        block_max = jnp.max(jnp.where(matched, values_block[:, None], FLOOR), axis=0)
        return jnp.maximum(running, block_max)

    return lax.fori_loop(
        0, field_count // block_fields, per_block, jnp.full((storm_count,), FLOOR, jnp.float32)
    )


def local(vorticity, lat_order, storm_labels, storm_owner):
    field_count, lat_rows, lon_count = vorticity.shape
    lat_count = lat_order.shape[0]
    spec_count = lax.axis_size("spec")
    device_rank = lax.axis_index("spec")
    wave_count = MW
    slot_count = wave_count // spec_count
    band_count = OUT_LAT
    band_rows = storm_labels.shape[1]
    storm_count = storm_owner.shape[0]
    positions = jnp.arange(wave_count, dtype=jnp.int32)
    forward = fourier_table(positions, lon_count)
    coefficients = jnp.einsum(
        "fjl,lqr->qjrf", vorticity, forward, preferred_element_type=jnp.float32
    )
    coefficients = coefficients.reshape(wave_count, lat_rows, 2 * field_count)
    sine_values, cosines, weights = node_values(lat_order, lat_count, band_count, OUT_LON)
    local_waves = device_rank * slot_count + jnp.arange(slot_count, dtype=jnp.int32)
    tables = legendre(local_waves.astype(jnp.float32), sine_values, cosines, wave_count)
    tile_rows = min(64, wave_count)
    tile_count = wave_count // tile_rows
    weighted = (tables[:, :, :lat_count] * weights[None, None, :]).reshape(
        slot_count * tile_count, tile_rows, lat_count
    )
    evaluated = tables[:, :, lat_count:].reshape(slot_count * tile_count, tile_rows, band_count)
    first_tiles = local_waves // tile_rows
    received = lax.all_to_all(coefficients, "spec", split_axis=0, concat_axis=1, tiled=True)
    column_count = received.shape[2]

    def per_slot(slot_index, collected):
        columns = lax.dynamic_index_in_dim(received, slot_index, 0, keepdims=False)

        def per_tile(tile_index, running):
            flat_index = slot_index * tile_count + tile_index
            rows_in = lax.dynamic_index_in_dim(weighted, flat_index, 0, keepdims=False)
            rows_out = lax.dynamic_index_in_dim(evaluated, flat_index, 0, keepdims=False)
            spectral = jnp.dot(
                rows_in, columns, precision=HIGHEST, preferred_element_type=jnp.float32
            )
            return running + lax.dot_general(
                rows_out,
                spectral,
                (((0,), (0,)), ((), ())),
                precision=HIGHEST,
                preferred_element_type=jnp.float32,
            )

        band_part = lax.fori_loop(
            first_tiles[slot_index],
            jnp.int32(tile_count),
            per_tile,
            jnp.zeros((band_count, column_count), jnp.float32),
        )
        return lax.dynamic_update_index_in_dim(
            collected, band_part.astype(jnp.bfloat16), slot_index, 0
        )

    collected = lax.fori_loop(
        0, slot_count, per_slot, jnp.zeros((slot_count, band_count, column_count), jnp.bfloat16)
    )
    gathered = lax.all_to_all(collected, "spec", split_axis=1, concat_axis=0, tiled=True)
    gathered = gathered.reshape(wave_count, band_rows, 2, field_count)
    synthesis = synthesis_table(positions, OUT_LON)
    grid_values = jnp.einsum(
        "qorf,qrl->fol", gathered, synthesis, preferred_element_type=jnp.float32
    )
    filtered = grid_values.astype(jnp.bfloat16)
    local_peaks = masked_peaks(grid_values, storm_labels, storm_count)
    slot_share = storm_count // spec_count
    merged = lax.pmax(local_peaks, "spec")
    own_slots = device_rank * slot_share + jnp.arange(slot_share, dtype=jnp.int32)
    selected = storm_owner[:, None] == own_slots[None, :]
    storm_peak = jnp.max(jnp.where(selected, merged[:, None], FLOOR), axis=0)
    return (filtered, storm_peak)


def solution(mesh):
    return jax.shard_map(
        local,
        mesh=mesh,
        in_specs=(P("grp", "spec", None), P(), P("grp", "spec", None), P("grp")),
        out_specs=(P("grp", "spec", None), P(("grp", "spec"))),
        check_vma=False,
    )
```

profile of v0, /device:TPU:0, one launch (start us, length us, event | category | flops | bytes accessed | tf_op | source)
XLA Modules:
  0.0 1166.3 jit_solution(5770569432625255367)
XLA Ops:
  0.6 11.6 sine_negate_fusion
  12.2 20.7 %fusion.49 = f32[256,2,64,80]{0,3,2,1:T(8,128)} fusion(bf16[64,80,2560]{2,1,0:T(8,128)(2,1)} %param.12, f32[2560,256,1]{1,0,2:T(8,128)S(1)} %get-tuple-element.748, f32[2560,256,1]{1,0,2:T(8,128)} %get-tuple-element.749), kind=kOutput, calls=%fused_computation.139 | convolution fusion | flops 13425704960 | bytes 41943040 | tf_op jit(solution)/shard_map/fjl,lqr->qjrf/dot_general | solution.py:122
  32.9 12.2 %copy.35 = f32[256,80,128]{2,1,0:T(8,128)} copy(f32[256,80,128]{0,1,2:T(8,128)} %bitcast.184) | data formatting | bytes 20971520 | tf_op jit(solution)/shard_map/reshape | solution.py:125
  45.1 7.6 all-to-all-start
  53.1 240.2 %while.74 = (s32[]{:T(128)}, f32[16,1536]{1,0:T(8,128)S(1)}, f32[16,1536]{1,0:T(8,128)S(1)}, f32[16,16,16,1536]{3,2,1,0:T(8,128)}, s32[16,16]{1,0:T(8,128)S(1)},...) while((s32[]{:T(128)}, f32[16,1536]{1,0:T(8,128)S(1)}, ...), condition=%wide.region_2.3_spmd.clone.clone.clone, body=%wide.region_1.2_spmd.clone.clone.clone.sunk | while | flops 5262770 | bytes 9675402 | solution.py:79
  293.3 2.6 slice.184
  295.9 4.4 copy.37
  300.3 8.5 slice_multiply_fusion
  308.9 14.3 %copy.38 = f32[16,256,1280]{2,1,0:T(8,128)} copy(f32[16,256,1280]{2,0,1:T(8,128)S(1)} %slice_multiply_fusion) | data formatting | bytes 41943040 | tf_op jit(solution)/shard_map/mul | solution.py:131
  323.2 9.0 copy.36
  332.2 330.1 %while.72 = (s32[]{:T(128)}, bf16[16,256,128]{2,1,0:T(8,128)(2,1)S(1)}, s32[16]{0:T(128)S(1)}, f32[16,1280,128]{2,1,0:T(8,128)}, f32[64,64,256]{2,1,0:T(8,128)},...) while((s32[]{:T(128)}, ...), condition=%wide.region_6.7_spmd, body=%wide.region_3.6_spmd.sunk | while | flops 151060480 | bytes 3015044 | solution.py:167
  333.9 18.8 %while.75 = (s32[]{:T(128)}, f32[256,128]{1,0:T(8,128)S(1)}, s32[]{:T(128)}, f32[64,64,256]{2,1,0:T(8,128)}, f32[64,64,1280]{2,1,0:T(8,128)}, /*index=5*/f32[1280,128]{1,0:T(8,128)S(1)}, s32[]{:T(128)}, s32[]{:T(128)}, s32[]{:T(128)}) while((s32[]{:T(128)}, f32[256,128]{1,0:T(8,128)S(1)}, s32[]{:T(128)}, f32[64,64,256]{2,1,0:T(8,128)}, ...), condition=%wide.region_5.5_spmd, body=%wide.region_4.4_spmd.sunk | while | flops 151027712 | bytes 1376411 | solution.py:157
  335.2 1.5 fusion.108
  339.8 1.5 fusion.108
  344.3 1.5 fusion.108
  348.9 1.5 fusion.108
  354.5 18.8 %while.75 = (s32[]{:T(128)}, f32[256,128]{1,0:T(8,128)S(1)}, s32[]{:T(128)}, f32[64,64,256]{2,1,0:T(8,128)}, f32[64,64,1280]{2,1,0:T(8,128)}, /*index=5*/f32[1280,128]{1,0:T(8,128)S(1)}, s32[]{:T(128)}, s32[]{:T(128)}, s32[]{:T(128)}) while((s32[]{:T(128)}, f32[256,128]{1,0:T(8,128)S(1)}, s32[]{:T(128)}, f32[64,64,256]{2,1,0:T(8,128)}, ...), condition=%wide.region_5.5_spmd, body=%wide.region_4.4_spmd.sunk | while | flops 151027712 | bytes 1376411 | solution.py:157
  375.2 18.8 %while.75 = (s32[]{:T(128)}, f32[256,128]{1,0:T(8,128)S(1)}, s32[]{:T(128)}, f32[64,64,256]{2,1,0:T(8,128)}, f32[64,64,1280]{2,1,0:T(8,128)}, /*index=5*/f32[1280,128]{1,0:T(8,128)S(1)}, s32[]{:T(128)}, s32[]{:T(128)}, s32[]{:T(128)}) while((s32[]{:T(128)}, f32[256,128]{1,0:T(8,128)S(1)}, s32[]{:T(128)}, f32[64,64,256]{2,1,0:T(8,128)}, ...), condition=%wide.region_5.5_spmd, body=%wide.region_4.4_spmd.sunk | while | flops 151027712 | bytes 1376411 | solution.py:157
  395.8 18.8 %while.75 = (s32[]{:T(128)}, f32[256,128]{1,0:T(8,128)S(1)}, s32[]{:T(128)}, f32[64,64,256]{2,1,0:T(8,128)}, f32[64,64,1280]{2,1,0:T(8,128)}, /*index=5*/f32[1280,128]{1,0:T(8,128)S(1)}, s32[]{:T(128)}, s32[]{:T(128)}, s32[]{:T(128)}) while((s32[]{:T(128)}, f32[256,128]{1,0:T(8,128)S(1)}, s32[]{:T(128)}, f32[64,64,256]{2,1,0:T(8,128)}, ...), condition=%wide.region_5.5_spmd, body=%wide.region_4.4_spmd.sunk | while | flops 151027712 | bytes 1376411 | solution.py:157
  397.1 1.5 fusion.108
  401.6 1.5 fusion.108
  416.4 18.8 %while.75 = (s32[]{:T(128)}, f32[256,128]{1,0:T(8,128)S(1)}, s32[]{:T(128)}, f32[64,64,256]{2,1,0:T(8,128)}, f32[64,64,1280]{2,1,0:T(8,128)}, /*index=5*/f32[1280,128]{1,0:T(8,128)S(1)}, s32[]{:T(128)}, s32[]{:T(128)}, s32[]{:T(128)}) while((s32[]{:T(128)}, f32[256,128]{1,0:T(8,128)S(1)}, s32[]{:T(128)}, f32[64,64,256]{2,1,0:T(8,128)}, ...), condition=%wide.region_5.5_spmd, body=%wide.region_4.4_spmd.sunk | while | flops 151027712 | bytes 1376411 | solution.py:157
  417.7 1.5 fusion.108
  422.3 1.5 fusion.108
  437.0 18.8 %while.75 = (s32[]{:T(128)}, f32[256,128]{1,0:T(8,128)S(1)}, s32[]{:T(128)}, f32[64,64,256]{2,1,0:T(8,128)}, f32[64,64,1280]{2,1,0:T(8,128)}, /*index=5*/f32[1280,128]{1,0:T(8,128)S(1)}, s32[]{:T(128)}, s32[]{:T(128)}, s32[]{:T(128)}) while((s32[]{:T(128)}, f32[256,128]{1,0:T(8,128)S(1)}, s32[]{:T(128)}, f32[64,64,256]{2,1,0:T(8,128)}, ...), condition=%wide.region_5.5_spmd, body=%wide.region_4.4_spmd.sunk | while | flops 151027712 | bytes 1376411 | solution.py:157
  438.4 1.5 fusion.108
  457.7 18.8 %while.75 = (s32[]{:T(128)}, f32[256,128]{1,0:T(8,128)S(1)}, s32[]{:T(128)}, f32[64,64,256]{2,1,0:T(8,128)}, f32[64,64,1280]{2,1,0:T(8,128)}, /*index=5*/f32[1280,128]{1,0:T(8,128)S(1)}, s32[]{:T(128)}, s32[]{:T(128)}, s32[]{:T(128)}) while((s32[]{:T(128)}, f32[256,128]{1,0:T(8,128)S(1)}, s32[]{:T(128)}, f32[64,64,256]{2,1,0:T(8,128)}, ...), condition=%wide.region_5.5_spmd, body=%wide.region_4.4_spmd.sunk | while | flops 151027712 | bytes 1376411 | solution.py:157
  478.3 18.8 %while.75 = (s32[]{:T(128)}, f32[256,128]{1,0:T(8,128)S(1)}, s32[]{:T(128)}, f32[64,64,256]{2,1,0:T(8,128)}, f32[64,64,1280]{2,1,0:T(8,128)}, /*index=5*/f32[1280,128]{1,0:T(8,128)S(1)}, s32[]{:T(128)}, s32[]{:T(128)}, s32[]{:T(128)}) while((s32[]{:T(128)}, f32[256,128]{1,0:T(8,128)S(1)}, s32[]{:T(128)}, f32[64,64,256]{2,1,0:T(8,128)}, ...), condition=%wide.region_5.5_spmd, body=%wide.region_4.4_spmd.sunk | while | flops 151027712 | bytes 1376411 | solution.py:157
  498.9 18.8 %while.75 = (s32[]{:T(128)}, f32[256,128]{1,0:T(8,128)S(1)}, s32[]{:T(128)}, f32[64,64,256]{2,1,0:T(8,128)}, f32[64,64,1280]{2,1,0:T(8,128)}, /*index=5*/f32[1280,128]{1,0:T(8,128)S(1)}, s32[]{:T(128)}, s32[]{:T(128)}, s32[]{:T(128)}) while((s32[]{:T(128)}, f32[256,128]{1,0:T(8,128)S(1)}, s32[]{:T(128)}, f32[64,64,256]{2,1,0:T(8,128)}, ...), condition=%wide.region_5.5_spmd, body=%wide.region_4.4_spmd.sunk | while | flops 151027712 | bytes 1376411 | solution.py:157
  519.6 18.8 %while.75 = (s32[]{:T(128)}, f32[256,128]{1,0:T(8,128)S(1)}, s32[]{:T(128)}, f32[64,64,256]{2,1,0:T(8,128)}, f32[64,64,1280]{2,1,0:T(8,128)}, /*index=5*/f32[1280,128]{1,0:T(8,128)S(1)}, s32[]{:T(128)}, s32[]{:T(128)}, s32[]{:T(128)}) while((s32[]{:T(128)}, f32[256,128]{1,0:T(8,128)S(1)}, s32[]{:T(128)}, f32[64,64,256]{2,1,0:T(8,128)}, ...), condition=%wide.region_5.5_spmd, body=%wide.region_4.4_spmd.sunk | while | flops 151027712 | bytes 1376411 | solution.py:157
  540.2 18.8 %while.75 = (s32[]{:T(128)}, f32[256,128]{1,0:T(8,128)S(1)}, s32[]{:T(128)}, f32[64,64,256]{2,1,0:T(8,128)}, f32[64,64,1280]{2,1,0:T(8,128)}, /*index=5*/f32[1280,128]{1,0:T(8,128)S(1)}, s32[]{:T(128)}, s32[]{:T(128)}, s32[]{:T(128)}) while((s32[]{:T(128)}, f32[256,128]{1,0:T(8,128)S(1)}, s32[]{:T(128)}, f32[64,64,256]{2,1,0:T(8,128)}, ...), condition=%wide.region_5.5_spmd, body=%wide.region_4.4_spmd.sunk | while | flops 151027712 | bytes 1376411 | solution.py:157
  560.8 18.8 %while.75 = (s32[]{:T(128)}, f32[256,128]{1,0:T(8,128)S(1)}, s32[]{:T(128)}, f32[64,64,256]{2,1,0:T(8,128)}, f32[64,64,1280]{2,1,0:T(8,128)}, /*index=5*/f32[1280,128]{1,0:T(8,128)S(1)}, s32[]{:T(128)}, s32[]{:T(128)}, s32[]{:T(128)}) while((s32[]{:T(128)}, f32[256,128]{1,0:T(8,128)S(1)}, s32[]{:T(128)}, f32[64,64,256]{2,1,0:T(8,128)}, ...), condition=%wide.region_5.5_spmd, body=%wide.region_4.4_spmd.sunk | while | flops 151027712 | bytes 1376411 | solution.py:157
  581.5 18.8 %while.75 = (s32[]{:T(128)}, f32[256,128]{1,0:T(8,128)S(1)}, s32[]{:T(128)}, f32[64,64,256]{2,1,0:T(8,128)}, f32[64,64,1280]{2,1,0:T(8,128)}, /*index=5*/f32[1280,128]{1,0:T(8,128)S(1)}, s32[]{:T(128)}, s32[]{:T(128)}, s32[]{:T(128)}) while((s32[]{:T(128)}, f32[256,128]{1,0:T(8,128)S(1)}, s32[]{:T(128)}, f32[64,64,256]{2,1,0:T(8,128)}, ...), condition=%wide.region_5.5_spmd, body=%wide.region_4.4_spmd.sunk | while | flops 151027712 | bytes 1376411 | solution.py:157
  602.1 18.8 %while.75 = (s32[]{:T(128)}, f32[256,128]{1,0:T(8,128)S(1)}, s32[]{:T(128)}, f32[64,64,256]{2,1,0:T(8,128)}, f32[64,64,1280]{2,1,0:T(8,128)}, /*index=5*/f32[1280,128]{1,0:T(8,128)S(1)}, s32[]{:T(128)}, s32[]{:T(128)}, s32[]{:T(128)}) while((s32[]{:T(128)}, f32[256,128]{1,0:T(8,128)S(1)}, s32[]{:T(128)}, f32[64,64,256]{2,1,0:T(8,128)}, ...), condition=%wide.region_5.5_spmd, body=%wide.region_4.4_spmd.sunk | while | flops 151027712 | bytes 1376411 | solution.py:157
  622.7 18.8 %while.75 = (s32[]{:T(128)}, f32[256,128]{1,0:T(8,128)S(1)}, s32[]{:T(128)}, f32[64,64,256]{2,1,0:T(8,128)}, f32[64,64,1280]{2,1,0:T(8,128)}, /*index=5*/f32[1280,128]{1,0:T(8,128)S(1)}, s32[]{:T(128)}, s32[]{:T(128)}, s32[]{:T(128)}) while((s32[]{:T(128)}, f32[256,128]{1,0:T(8,128)S(1)}, s32[]{:T(128)}, f32[64,64,256]{2,1,0:T(8,128)}, ...), condition=%wide.region_5.5_spmd, body=%wide.region_4.4_spmd.sunk | while | flops 151027712 | bytes 1376411 | solution.py:157
  643.3 18.8 %while.75 = (s32[]{:T(128)}, f32[256,128]{1,0:T(8,128)S(1)}, s32[]{:T(128)}, f32[64,64,256]{2,1,0:T(8,128)}, f32[64,64,1280]{2,1,0:T(8,128)}, /*index=5*/f32[1280,128]{1,0:T(8,128)S(1)}, s32[]{:T(128)}, s32[]{:T(128)}, s32[]{:T(128)}) while((s32[]{:T(128)}, f32[256,128]{1,0:T(8,128)S(1)}, s32[]{:T(128)}, f32[64,64,256]{2,1,0:T(8,128)}, ...), condition=%wide.region_5.5_spmd, body=%wide.region_4.4_spmd.sunk | while | flops 151027712 | bytes 1376411 | solution.py:157
  662.2 1.6 copy.39
  663.9 3.9 all-to-all-start.1
  667.8 4.7 reshape.683
  672.5 4.1 multiply_convert_fusion
  676.6 13.8 %all-to-all-done.1 = bf16[16,256,128]{2,0,1:T(8,128)(2,1)S(1)} async-done(((bf16[16,256,128]{2,0,1:T(8,128)(2,1)}), bf16[16,256,128]{2,0,1:T(8,128)(2,1)S(1)}, u32[]{:S(2)}, u32[]{:S(2)}) %all-to-all-start.1) | async-done | bytes 1048608 | tf_op jit(solution)/shard_map/all_to_all | solution.py:170
  690.7 1.9 reshape.682
  692.6 3.6 fusion.94
  696.2 2.0 copy.43
  698.2 3.5 copy.42
  701.7 4.8 reshape.684
  706.4 424.4 %while.73 = (s32[]{:T(128)}, f32[256]{0:T(256)S(1)}, s32[64,11520]{1,0:T(8,128)}, f32[64,11520]{1,0:T(8,128)}, s32[]{:T(128)}, /*index=5*/s32[]{:T(128)}, s32[]{:T(128)}, s32[]{:T(128)}) while((s32[]{:T(128)}, f32[256]{0:T(256)S(1)}, s32[64,11520]{1,0:T(8,128)}, f32[64,11520]{1,0:T(8,128)}, s32[]{:T(128)}, /*index=5*/s32[]{:T(128)}, ...), condition=%wide.region_9.10_spmd.clone, body=%wide.region_7.9_spmd.clone.sunk | while | flops 35389700 | bytes 1847453 | solution.py:105
  708.7 24.3 %select_reduce_fusion.4 = f32[256]{0:T(256)S(1)} fusion(f32[46080]{0:T(1024)S(1)} %broadcast_in_dim.1063, s32[46080]{0:T(1024)S(1)} %eq.384), kind=kLoop, calls=%fused_computation.15.clone.1 | loop fusion | flops 35389184 | bytes 369664 | tf_op jit(solution)/shard_map/while/body/eval_jaxpr/reduce_max | solution.py:102
  735.2 24.3 %select_reduce_fusion.4 = f32[256]{0:T(256)S(1)} fusion(f32[46080]{0:T(1024)S(1)} %broadcast_in_dim.1063, s32[46080]{0:T(1024)S(1)} %eq.384), kind=kLoop, calls=%fused_computation.15.clone.1 | loop fusion | flops 35389184 | bytes 369664 | tf_op jit(solution)/shard_map/while/body/eval_jaxpr/reduce_max | solution.py:102
  761.7 24.3 %select_reduce_fusion.4 = f32[256]{0:T(256)S(1)} fusion(f32[46080]{0:T(1024)S(1)} %broadcast_in_dim.1063, s32[46080]{0:T(1024)S(1)} %eq.384), kind=kLoop, calls=%fused_computation.15.clone.1 | loop fusion | flops 35389184 | bytes 369664 | tf_op jit(solution)/shard_map/while/body/eval_jaxpr/reduce_max | solution.py:102
  788.2 24.3 %select_reduce_fusion.4 = f32[256]{0:T(256)S(1)} fusion(f32[46080]{0:T(1024)S(1)} %broadcast_in_dim.1063, s32[46080]{0:T(1024)S(1)} %eq.384), kind=kLoop, calls=%fused_computation.15.clone.1 | loop fusion | flops 35389184 | bytes 369664 | tf_op jit(solution)/shard_map/while/body/eval_jaxpr/reduce_max | solution.py:102
  814.8 24.3 %select_reduce_fusion.4 = f32[256]{0:T(256)S(1)} fusion(f32[46080]{0:T(1024)S(1)} %broadcast_in_dim.1063, s32[46080]{0:T(1024)S(1)} %eq.384), kind=kLoop, calls=%fused_computation.15.clone.1 | loop fusion | flops 35389184 | bytes 369664 | tf_op jit(solution)/shard_map/while/body/eval_jaxpr/reduce_max | solution.py:102
  841.3 24.3 %select_reduce_fusion.4 = f32[256]{0:T(256)S(1)} fusion(f32[46080]{0:T(1024)S(1)} %broadcast_in_dim.1063, s32[46080]{0:T(1024)S(1)} %eq.384), kind=kLoop, calls=%fused_computation.15.clone.1 | loop fusion | flops 35389184 | bytes 369664 | tf_op jit(solution)/shard_map/while/body/eval_jaxpr/reduce_max | solution.py:102
  867.8 24.3 %select_reduce_fusion.4 = f32[256]{0:T(256)S(1)} fusion(f32[46080]{0:T(1024)S(1)} %broadcast_in_dim.1063, s32[46080]{0:T(1024)S(1)} %eq.384), kind=kLoop, calls=%fused_computation.15.clone.1 | loop fusion | flops 35389184 | bytes 369664 | tf_op jit(solution)/shard_map/while/body/eval_jaxpr/reduce_max | solution.py:102
  894.3 24.3 %select_reduce_fusion.4 = f32[256]{0:T(256)S(1)} fusion(f32[46080]{0:T(1024)S(1)} %broadcast_in_dim.1063, s32[46080]{0:T(1024)S(1)} %eq.384), kind=kLoop, calls=%fused_computation.15.clone.1 | loop fusion | flops 35389184 | bytes 369664 | tf_op jit(solution)/shard_map/while/body/eval_jaxpr/reduce_max | solution.py:102
  920.9 24.3 %select_reduce_fusion.4 = f32[256]{0:T(256)S(1)} fusion(f32[46080]{0:T(1024)S(1)} %broadcast_in_dim.1063, s32[46080]{0:T(1024)S(1)} %eq.384), kind=kLoop, calls=%fused_computation.15.clone.1 | loop fusion | flops 35389184 | bytes 369664 | tf_op jit(solution)/shard_map/while/body/eval_jaxpr/reduce_max | solution.py:102
  947.4 24.3 %select_reduce_fusion.4 = f32[256]{0:T(256)S(1)} fusion(f32[46080]{0:T(1024)S(1)} %broadcast_in_dim.1063, s32[46080]{0:T(1024)S(1)} %eq.384), kind=kLoop, calls=%fused_computation.15.clone.1 | loop fusion | flops 35389184 | bytes 369664 | tf_op jit(solution)/shard_map/while/body/eval_jaxpr/reduce_max | solution.py:102
  973.9 24.3 %select_reduce_fusion.4 = f32[256]{0:T(256)S(1)} fusion(f32[46080]{0:T(1024)S(1)} %broadcast_in_dim.1063, s32[46080]{0:T(1024)S(1)} %eq.384), kind=kLoop, calls=%fused_computation.15.clone.1 | loop fusion | flops 35389184 | bytes 369664 | tf_op jit(solution)/shard_map/while/body/eval_jaxpr/reduce_max | solution.py:102
  1000.4 24.3 %select_reduce_fusion.4 = f32[256]{0:T(256)S(1)} fusion(f32[46080]{0:T(1024)S(1)} %broadcast_in_dim.1063, s32[46080]{0:T(1024)S(1)} %eq.384), kind=kLoop, calls=%fused_computation.15.clone.1 | loop fusion | flops 35389184 | bytes 369664 | tf_op jit(solution)/shard_map/while/body/eval_jaxpr/reduce_max | solution.py:102
  1027.0 24.3 %select_reduce_fusion.4 = f32[256]{0:T(256)S(1)} fusion(f32[46080]{0:T(1024)S(1)} %broadcast_in_dim.1063, s32[46080]{0:T(1024)S(1)} %eq.384), kind=kLoop, calls=%fused_computation.15.clone.1 | loop fusion | flops 35389184 | bytes 369664 | tf_op jit(solution)/shard_map/while/body/eval_jaxpr/reduce_max | solution.py:102
  1053.5 24.3 %select_reduce_fusion.4 = f32[256]{0:T(256)S(1)} fusion(f32[46080]{0:T(1024)S(1)} %broadcast_in_dim.1063, s32[46080]{0:T(1024)S(1)} %eq.384), kind=kLoop, calls=%fused_computation.15.clone.1 | loop fusion | flops 35389184 | bytes 369664 | tf_op jit(solution)/shard_map/while/body/eval_jaxpr/reduce_max | solution.py:102
  1080.0 24.3 %select_reduce_fusion.4 = f32[256]{0:T(256)S(1)} fusion(f32[46080]{0:T(1024)S(1)} %broadcast_in_dim.1063, s32[46080]{0:T(1024)S(1)} %eq.384), kind=kLoop, calls=%fused_computation.15.clone.1 | loop fusion | flops 35389184 | bytes 369664 | tf_op jit(solution)/shard_map/while/body/eval_jaxpr/reduce_max | solution.py:102
  1106.5 24.3 %select_reduce_fusion.4 = f32[256]{0:T(256)S(1)} fusion(f32[46080]{0:T(1024)S(1)} %broadcast_in_dim.1063, s32[46080]{0:T(1024)S(1)} %eq.384), kind=kLoop, calls=%fused_computation.15.clone.1 | loop fusion | flops 35389184 | bytes 369664 | tf_op jit(solution)/shard_map/while/body/eval_jaxpr/reduce_max | solution.py:102
  1130.8 34.8 %pmax.7 = f32[256]{0:T(256)S(1)} all-reduce(f32[256]{0:T(256)S(1)} %get-tuple-element.462), channel_id=1, replica_groups=mesh['grp'=2,'spec'=16] {'spec'}, use_global_device_ids=true, to_apply=%region_10.11 | all-reduce | flops 256 | bytes 2048 | tf_op jit(solution)/shard_map/pmax | solution.py:179
  (1105 shorter events, 296.2 us)
Async XLA Ops:
  45.1 7.8 copy-start.1
  45.1 278.1 %all-to-all-start = ((f32[256,80,128]{2,1,0:T(8,128)}), f32[256,80,128]{2,1,0:T(8,128)}, u32[]{:S(2)}, u32[]{:S(2)}) async-start(f32[256,80,128]{2,1,0:T(8,128)} %copy.35), calls=%async_computation | async-start | bytes 20971520 | tf_op jit(solution)/shard_map/all_to_all | solution.py:136
  663.9 26.6 %all-to-all-start.1 = ((bf16[16,256,128]{2,0,1:T(8,128)(2,1)}), bf16[16,256,128]{2,0,1:T(8,128)(2,1)S(1)}, u32[]{:S(2)}, u32[]{:S(2)}) async-start(bf16[16,256,128]{2,0,1:T(8,128)(2,1)} %copy.39), calls=%async_computation.1 | async-start | bytes 2097152 | tf_op jit(solution)/shard_map/all_to_all | solution.py:170
  690.7 1.9 copy-start
  706.4 459.2 %copy-start.2 = (s32[256]{0:T(256)S(1)}, s32[256]{0:T(256)}, u32[]{:S(2)}) copy-start(s32[256]{0:T(256)} %param.15) | copy-start | bytes 3076
where the time goes:
time: 1180 us; the launch traced here: 1170 us
  other arithmetic  452 us (38%)
  loops' own time  298 us (25%)
  matrix products  198 us (17%)
  local copies, waits for them, and re-layouts  157 us (13%)
  blocking collectives  34.8 us (3%)
  waiting for transfers between devices  13.8 us (1%)
    reduce_max x16, other arithmetic, per_block(): jnp.max(jnp.where(matched, values_block[:, None], FLOOR), axis=0)  388 us
    another operation x1, loops' own time, legendre(): lax.scan(advance, (zero_rows, zero_rows), jnp.arange(degree_count, dtype=...  169 us
    another operation x16, loops' own time, per_slot(): lax.fori_loop(first_tiles[slot_index], jnp.int32(tile_count), per_tile, j...  128 us
    dot_general x64, matrix products, per_tile(): jnp.dot(rows_in, columns, precision=HIGHEST, preferred_element_type=jnp.f...  94.5 us
    dot_general x64, matrix products, per_tile(): lax.dot_general(rows_out, spectral, (((0,), (0,)), ((), ())), precision=H...  79.3 us
    pmax x1, blocking collectives, local(): merged = lax.pmax(local_peaks, 'spec')  34.8 us
    while x240, other arithmetic  29.9 us
  transfers between devices with their start and end apart: 2, of which 1 were waited for; matrix products, arithmetic and copies ran while one was open for 9% of the time, Pallas kernels for 0%

commit v1 on v0

v1 whole, which is shorter than its diff:
```python
import functools
import math

import jax
import jax.numpy as jnp
import numpy as np
from jax import lax
from jax.experimental import pallas as pl
from jax.experimental.pallas import tpu as pltpu
from jax.sharding import Mesh
from jax.sharding import PartitionSpec as P

MW = 256
OUT_LAT = 256
OUT_LON = 720
FLOOR = -1e30
CHUNKS = 2
LANES = 128


def fourier_table(lon_count):
    steps = np.arange(lon_count)[:, None] * np.arange(MW)[None, :] % lon_count
    angles = steps * (2.0 * math.pi / lon_count)
    return np.stack([np.cos(angles), -np.sin(angles)], axis=-1) / lon_count


def synthesis_table(lon_count):
    steps = np.arange(MW)[:, None] * np.arange(lon_count)[None, :] % lon_count
    angles = steps * (2.0 * math.pi / lon_count)
    factor = np.where(np.arange(MW) == 0, 1.0, 2.0)[:, None]
    return np.stack([factor * np.cos(angles), -factor * np.sin(angles)], axis=1)


def diagonal_logs():
    counters = np.arange(1, MW, dtype=np.float64)
    increments = np.log((2.0 * counters + 1.0) / (2.0 * counters))
    sums = np.concatenate([[0.0], np.cumsum(increments)])
    return (0.5 * math.log(0.5) + 0.5 * sums).astype(np.float32)


def kernel_table(orders, start, cosines, weights, out_rows):
    slots, columns = start.shape
    in_rows = columns - out_rows
    degrees = MW
    group = 8
    tiles = columns // LANES
    out_tiles = out_rows // LANES

    def body(order_ref, start_ref, cos_ref, weight_ref, out_ref, table_ref):
        m = jnp.broadcast_to(order_ref[...], (group, LANES))
        cosine = [cos_ref[0:1, t * LANES : (t + 1) * LANES] for t in range(tiles)]

        def step(k, carry):
            previous, earlier = carry
            offset = k.astype(jnp.float32)
            degree = m + offset
            below = degree - 1.0
            first = jnp.sqrt((4.0 * degree * degree - 1.0) / (offset * (2.0 * m + offset)))
            second = jnp.sqrt(
                (offset - 1.0) * (2.0 * m + offset - 1.0) / jnp.maximum(4.0 * below * below - 1.0, 1.0)
            )
            keep = degree <= degrees - 1.0
            row = pl.multiple_of(k * group, group)
            current = []
            for t in range(tiles):
                value = first * (cosine[t] * previous[t] - second * earlier[t])
                current.append(value)
                stored = jnp.where(keep, value, 0.0) if t < out_tiles else value
                table_ref[t, pl.ds(row, group), :] = stored
            return (tuple(current), previous)

        first_rows = tuple(start_ref[:, t * LANES : (t + 1) * LANES] for t in range(tiles))
        for t in range(tiles):
            table_ref[t, 0:group, :] = first_rows[t]
        zeros = tuple(jnp.zeros((group, LANES), jnp.float32) for _ in range(tiles))
        lax.fori_loop(1, degrees, step, (first_rows, zeros))
        weight = weight_ref[...]
        for s in range(group):
            values = [table_ref[t, pl.ds(s, degrees, stride=group), :] for t in range(tiles)]
            product = lax.dot_general(
                jnp.concatenate(values[:out_tiles], axis=1),
                jnp.concatenate(values[out_tiles:], axis=1),
                (((0,), (0,)), ((), ())),
                precision=lax.Precision.HIGHEST,
                preferred_element_type=jnp.float32,
            )
            out_ref[s] = (product * weight).astype(jnp.bfloat16)

    return pl.pallas_call(
        body,
        out_shape=jax.ShapeDtypeStruct((slots, out_rows, in_rows), jnp.bfloat16),
        grid=(slots // group,),
        in_specs=[
            pl.BlockSpec((group, 1), lambda g: (g, 0)),
            pl.BlockSpec((group, columns), lambda g: (g, 0)),
            pl.BlockSpec((1, columns), lambda g: (0, 0)),
            pl.BlockSpec((1, in_rows), lambda g: (0, 0)),
        ],
        out_specs=pl.BlockSpec((group, out_rows, in_rows), lambda g: (g, 0, 0)),
        scratch_shapes=[pltpu.VMEM((columns // LANES, degrees * group, LANES), jnp.float32)],
        compiler_params=pltpu.CompilerParams(vmem_limit_bytes=56 << 20),
    )(orders, start, cosines, weights)


def apply_table(table, received, slot_base):
    senders, slots, rows, columns = received.shape
    out_rows = table.shape[1]
    half = out_rows // 2

    def body(table_ref, data_ref, own_ref, other_ref):
        data = data_ref[...].reshape(senders * rows, columns)
        product = jnp.dot(table_ref[...], data, preferred_element_type=jnp.float32)
        own_ref[...] = product[:half]
        other_ref[...] = product[half:].astype(jnp.bfloat16)

    return pl.pallas_call(
        body,
        out_shape=(
            jax.ShapeDtypeStruct((slots, half, columns), jnp.float32),
            jax.ShapeDtypeStruct((slots, half, columns), jnp.bfloat16),
        ),
        grid=(slots,),
        in_specs=[
            pl.BlockSpec((None, out_rows, senders * rows), lambda s: (s + slot_base, 0, 0)),
            pl.BlockSpec((senders, None, rows, columns), lambda s: (0, s, 0, 0)),
        ],
        out_specs=(
            pl.BlockSpec((None, half, columns), lambda s: (s, 0, 0)),
            pl.BlockSpec((None, half, columns), lambda s: (s, 0, 0)),
        ),
        compiler_params=pltpu.CompilerParams(vmem_limit_bytes=56 << 20),
    )(table, received)


def storm_maxima(values, labels, storm_count):
    rows, lon_count = values.shape
    block = math.gcd(rows, 64)
    lane_starts = range(0, lon_count, LANES)

    def body(value_ref, label_ref, out_ref):
        @pl.when(pl.program_id(0) == 0)
        def _():
            out_ref[...] = jnp.full(out_ref.shape, FLOOR, jnp.float32)

        for lane in lane_starts:
            width = min(LANES, lon_count - lane)
            cells = [
                (
                    value_ref[r : r + 8, lane : lane + width],
                    label_ref[r : r + 8, lane : lane + width],
                )
                for r in range(0, block, 8)
            ]

            def per_storm(storm, carry):
                picked = [jnp.where(label == storm, value, FLOOR) for value, label in cells]
                while len(picked) > 1:
                    picked = [jnp.maximum(a, b) for a, b in zip(picked[::2], picked[1::2])]
                out_ref[storm, :, 0:width] = jnp.maximum(out_ref[storm, :, 0:width], picked[0])
                return carry

            lax.fori_loop(0, storm_count, per_storm, 0, unroll=8)

    return pl.pallas_call(
        body,
        out_shape=jax.ShapeDtypeStruct((storm_count, 8, LANES), jnp.float32),
        grid=(rows // block,),
        in_specs=[
            pl.BlockSpec((block, lon_count), lambda i: (i, 0)),
            pl.BlockSpec((block, lon_count), lambda i: (i, 0)),
        ],
        out_specs=pl.BlockSpec((storm_count, 8, LANES), lambda i: (0, 0, 0)),
        compiler_params=pltpu.CompilerParams(vmem_limit_bytes=56 << 20),
    )(values, labels)


def local(vorticity, lat_order, storm_labels, storm_owner):
    field_count, lat_rows, lon_count = vorticity.shape
    lat_count = lat_order.shape[0]
    halves = lax.axis_size("half")
    ranks = lax.axis_size("rest")
    half_index = lax.axis_index("half")
    rank = lax.axis_index("rest")
    band_rows = storm_labels.shape[1]
    storm_count = storm_owner.shape[0]
    slots = MW // ranks
    chunk_slots = slots // CHUNKS
    columns = 2 * field_count
    out_half = OUT_LAT // halves

    table = fourier_table(lon_count).reshape(lon_count, CHUNKS, chunk_slots, ranks, 2)
    table = table.transpose(1, 0, 3, 2, 4).reshape(CHUNKS, lon_count, ranks * chunk_slots, 2)
    table = table.astype(jnp.bfloat16)

    received = []
    for c in range(CHUNKS):
        coefficients = jnp.einsum(
            "fjl,lqr->qjrf", vorticity, jnp.asarray(table[c]), preferred_element_type=jnp.float32
        )
        coefficients = coefficients.astype(jnp.bfloat16).reshape(
            ranks, chunk_slots, lat_rows, columns
        )
        received.append(
            lax.all_to_all(coefficients, "rest", split_axis=0, concat_axis=0, tiled=True)
        )

    half_rows = ranks * lat_rows
    own_order = lax.dynamic_slice_in_dim(lat_order, half_index * half_rows, half_rows)
    colatitude = math.pi * (4.0 * own_order.astype(jnp.float32) + 3.0) / (4.0 * lat_count + 2.0)
    weights = math.pi / lat_count * jnp.sin(colatitude)
    band_index = jnp.arange(OUT_LAT, dtype=jnp.int32)
    band_index = ((band_index + half_index * out_half) % OUT_LAT).astype(jnp.float32)
    latitude = ((OUT_LAT - 1) / 2.0 - band_index) * (360.0 / OUT_LON) * (math.pi / 180.0)
    sine_values = jnp.concatenate([jnp.cos(latitude), jnp.sin(colatitude)])
    cosines = jnp.concatenate([jnp.sin(latitude), jnp.cos(colatitude)])
    orders = jnp.arange(slots, dtype=jnp.int32) * ranks + rank
    start_logs = jnp.asarray(diagonal_logs().reshape(slots, ranks))
    start_logs = lax.dynamic_slice_in_dim(start_logs, rank, 1, axis=1)
    orders = orders.astype(jnp.float32)[:, None]
    start = jnp.exp(start_logs + orders * jnp.log(sine_values)[None, :])
    kernel = kernel_table(orders, start, cosines[None, :], weights[None, :], OUT_LAT)

    gathered = []
    swap = [(0, 1), (1, 0)]
    for c in range(CHUNKS):
        own, other = apply_table(kernel, received[c], c * chunk_slots)
        mirrored = lax.ppermute(other, "half", swap)
        band = (own + mirrored.astype(jnp.float32)).astype(jnp.bfloat16)
        band = lax.all_to_all(band, "rest", split_axis=1, concat_axis=0, tiled=True)
        gathered.append(band.reshape(ranks, chunk_slots, band_rows, 2, field_count))

    gathered = jnp.concatenate(gathered, axis=1)
    synthesis = synthesis_table(OUT_LON).reshape(slots, ranks, 2, OUT_LON)
    synthesis = jnp.asarray(synthesis.transpose(1, 0, 2, 3).astype(jnp.bfloat16))
    grid_values = jnp.einsum(
        "qsorf,qsrl->fol", gathered, synthesis, preferred_element_type=jnp.float32
    )
    filtered = grid_values.astype(jnp.bfloat16)
    point_rows = field_count * band_rows
    partial_peaks = storm_maxima(
        grid_values.reshape(point_rows, OUT_LON),
        storm_labels.reshape(point_rows, OUT_LON),
        storm_count,
    )
    local_peaks = jnp.max(partial_peaks, axis=(1, 2))
    slot_ids = jnp.arange(storm_count, dtype=jnp.int32)
    by_slot = jnp.max(
        jnp.where(storm_owner[:, None] == slot_ids[None, :], local_peaks[:, None], FLOOR), axis=0
    )
    spec_count = halves * ranks
    shares = lax.all_to_all(
        by_slot.reshape(spec_count, storm_count // spec_count),
        ("half", "rest"),
        split_axis=0,
        concat_axis=0,
        tiled=True,
    )
    return (filtered, jnp.max(shares, axis=0))


def solution(mesh):
    groups = mesh.shape["grp"]
    spec_count = mesh.shape["spec"]
    split = Mesh(
        mesh.devices.reshape(groups, 2, spec_count // 2), axis_names=("grp", "half", "rest")
    )
    both = ("half", "rest")
    return jax.shard_map(
        local,
        mesh=split,
        in_specs=(P("grp", both, None), P(), P("grp", both, None), P("grp")),
        out_specs=(P("grp", both, None), P(("grp", "half", "rest"))),
        check_vma=False,
    )
```

time: 1180 us -> 343 us (0.29); the launches traced: 1170 us -> 342 us
  other arithmetic: 452 us -> 7.23 us
  loops' own time: 298 us -> 0 us
  Pallas kernels: 0 us -> 175 us
  matrix products: 198 us -> 27.1 us
  local copies, waits for them, and re-layouts: 157 us -> 39.2 us
  waiting for transfers between devices: 13.8 us -> 65 us
  blocking collectives: 34.8 us -> 0 us
  starting transfers between devices: 11.4 us -> 27.1 us
    reduce_max x17 -> x3, other arithmetic: 389 us -> 2.93 us  [the longest x1 2.25 us: local(): local_peaks = jnp.max(partial_peaks, axis=(1, 2))]
    another operation x19 -> x0, loops' own time: 298 us -> none  [the longest x1 169 us: legendre(): lax.scan(advance, (zero_rows, zero_rows), jnp.arange(degree_count, dtype=...]
    pallas_call x0 -> x4, Pallas kernels: none -> 175 us  [the longest x1 96.3 us: storm_maxima(): pl.pallas_call(body, out_shape=jax.ShapeDtypeStruct((storm_count, 8, LANE...]
    dot_general x130 -> x3, matrix products: 198 us -> 27.1 us  [the longest x2 26.1 us: local(): jnp.einsum('fjl,lqr->qjrf', vorticity, jnp.asarray(table[c]), preferred_e...]
    ppermute x0 -> x2, waiting for transfers between devices: none -> 47.8 us  [local(): mirrored = lax.ppermute(other, 'half', swap)]
    dynamic_slice x64 -> x0, local copies, waits for them, and re-layouts: 42.4 us -> none  [the longest x16 16.5 us: per_block(): lax.dynamic_slice_in_dim(labels_flat, start, block_fields, 0)]
    pmax x1 -> x0, blocking collectives: 34.8 us -> none  [local(): merged = lax.pmax(local_peaks, 'spec')]
    while x240 -> x0, other arithmetic: 29.9 us -> none
  transfers between devices with their start and end apart: 2 -> 7, of which waited for: 1 -> 5; matrix products, arithmetic and copies ran while one was open for 9% -> 11% of each run, Pallas kernels for 0% -> 23%
where the time goes in v1:
time: 343 us; the launch traced here: 342 us
  Pallas kernels  175 us (51%)
  waiting for transfers between devices  65 us (19%)
  local copies, waits for them, and re-layouts  39.2 us (11%)
  matrix products  27.1 us (8%)
  starting transfers between devices  27.1 us (8%)
  other arithmetic  7.23 us (2%)
    pallas_call x1, Pallas kernels, storm_maxima(): pl.pallas_call(body, out_shape=jax.ShapeDtypeStruct((storm_count, 8, LANE...  96.3 us
    pallas_call x1, Pallas kernels, kernel_table(): pl.pallas_call(body, out_shape=jax.ShapeDtypeStruct((slots, out_rows, in_...  55.4 us
    ppermute x2, waiting for transfers between devices, local(): mirrored = lax.ppermute(other, 'half', swap)  47.8 us
    dot_general x2, matrix products, local(): jnp.einsum('fjl,lqr->qjrf', vorticity, jnp.asarray(table[c]), preferred_e...  26.1 us
    pallas_call x2, Pallas kernels, apply_table(): pl.pallas_call(body, out_shape=(jax.ShapeDtypeStruct((slots, half, column...  23.4 us
    reshape x2, local copies, waits for them, and re-layouts, local(): coefficients.astype(jnp.bfloat16)  12.1 us
    convert_element_type x2, local copies, waits for them, and re-layouts, local(): coefficients.astype(jnp.bfloat16)  11.9 us
    all_to_all x2, starting transfers between devices, local(): lax.all_to_all(coefficients, 'rest', split_axis=0, concat_axis=0, tiled=T...  9.06 us
  transfers between devices with their start and end apart: 7, of which 5 were waited for; matrix products, arithmetic and copies ran while one was open for 11% of the time, Pallas kernels for 23%

profile of v1, /device:TPU:0, one launch (start us, length us, event | category | flops | bytes accessed | tf_op | source)
XLA Modules:
  0.0 341.6 jit_solution(6617292270177697500)
XLA Ops:
  0.6 12.5 %convert_bitcast_fusion = bf16[128,80,2,64]{0,1,3,2:T(8,128)(2,1)S(1)} fusion(bf16[2560,128,2,1]{1,0,3,2:T(8,128)(2,1)} %constant.68, bf16[64,80,2560]{2,1,0:T(8,128)(2,1)} %param.8), kind=kOutput, calls=%fused_computation.4 | convolution fusion | flops 6712197120 | bytes 30146560 | tf_op jit(solution)/shard_map/fjl,lqr->qjrf/dot_general | solution.py:197
  13.1 5.6 %copy.52 = bf16[128,80,2,64]{1,3,2,0:T(8,128)(2,1)} copy(bf16[128,80,2,64]{0,1,3,2:T(8,128)(2,1)S(1)} %convert_bitcast_fusion) | data formatting | bytes 5242880 | tf_op jit(solution)/shard_map/convert_element_type | solution.py:200
  18.7 6.1 %copy.53 = bf16[8,16,80,128]{3,2,1,0:T(8,128)(2,1)} copy(bf16[8,16,80,128]{2,3,1,0:T(8,128)(2,1)} %bitcast.50) | data formatting | bytes 5242880 | tf_op jit(solution)/shard_map/reshape | solution.py:200
  24.8 5.3 %all-to-all-start.2 = ((bf16[8,16,80,128]{3,2,1,0:T(8,128)(2,1)}), bf16[8,16,80,128]{3,2,1,0:T(8,128)(2,1)S(1)}, u32[]{:S(2)}, u32[]{:S(2)}) async-start(bf16[8,16,80,128]{3,2,1,0:T(8,128)(2,1)} %copy.53), calls=%async_computation.2 | async-start | bytes 5242880 | tf_op jit(solution)/shard_map/all_to_all | solution.py:204
  30.0 13.6 %convert_bitcast_fusion.1 = bf16[128,80,2,64]{0,1,3,2:T(8,128)(2,1)} fusion(bf16[2560,128,2,1]{1,0,3,2:T(8,128)(2,1)} %constant.67, bf16[64,80,2560]{2,1,0:T(8,128)(2,1)} %param.8), kind=kOutput, calls=%fused_computation.5 | convolution fusion | flops 6712197120 | bytes 30146560 | tf_op jit(solution)/shard_map/fjl,lqr->qjrf/dot_general | solution.py:197
  43.6 6.3 %copy.48 = bf16[128,80,2,64]{1,3,2,0:T(8,128)(2,1)} copy(bf16[128,80,2,64]{0,1,3,2:T(8,128)(2,1)} %convert_bitcast_fusion.1) | data formatting | bytes 5242880 | tf_op jit(solution)/shard_map/convert_element_type | solution.py:200
  49.9 6.0 %copy.49 = bf16[8,16,80,128]{3,2,1,0:T(8,128)(2,1)} copy(bf16[8,16,80,128]{2,3,1,0:T(8,128)(2,1)} %bitcast.51) | data formatting | bytes 5242880 | tf_op jit(solution)/shard_map/reshape | solution.py:200
  55.9 0.0 copy-start.3
  55.9 5.4 %all-to-all-done.2.data_ref = bf16[8,16,80,128]{3,2,1,0:T(8,128)(2,1)S(1)} async-done(((bf16[8,16,80,128]{3,2,1,0:T(8,128)(2,1)}), bf16[8,16,80,128]{3,2,1,0:T(8,128)(2,1)S(1)}, u32[]{:S(2)}, u32[]{:S(2)}) %all-to-all-start.2) | async-done | bytes 2621472 | tf_op jit(solution)/shard_map/all_to_all | solution.py:204
  61.3 0.0 copy-start.1
  61.3 1.5 copy-done.1
  62.8 3.8 %all-to-all-start = ((bf16[8,16,80,128]{3,2,1,0:T(8,128)(2,1)}), bf16[8,16,80,128]{3,2,1,0:T(8,128)(2,1)S(1)}, u32[]{:S(2)}, u32[]{:S(2)}) async-start(bf16[8,16,80,128]{3,2,1,0:T(8,128)(2,1)} %copy.49), calls=%async_computation | async-start | bytes 5242880 | tf_op jit(solution)/shard_map/all_to_all | solution.py:204
  66.6 0.0 copy-done.3
  66.6 0.1 broadcast_multiply_fusion
  66.7 0.6 broadcast_in_dim.24.weight_ref
  67.3 0.1 fusion.21
  67.4 0.1 fusion.22
  67.5 0.6 broadcast_in_dim.23.cos_ref
  68.0 0.7 dynamic-slice_bitcast_fusion
  68.7 0.6 add_convert_fusion.2.order_ref
  69.3 0.7 add_exponential_fusion.start_ref
  70.1 55.4 %shard_map.95.table_ref = bf16[32,256,640]{2,1,0:T(8,128)(2,1)} custom-call(f32[32,1]{1,0:T(8,128)} %add_convert_fusion.2.order_ref, f32[32,896]{1,0:T(8,128)} %add_exponential_fusion.start_ref, f32[1,896]{1,0:T(1,128)} %broadcast_in_dim.23.cos_ref, f32[1,640]{1,0:T(1,128)} %broadcast_in_dim.24.weight_ref), custom_call_target="tpu_custom_call" | custom-call | tf_op jit(solution)/shard_map/pallas_call | solution.py:89
  125.5 11.7 %shard_map.97 = (f32[16,128,128]{2,1,0:T(8,128)}, bf16[16,128,128]{2,1,0:T(8,128)(2,1)}) custom-call(bf16[32,256,640]{2,1,0:T(8,128)(2,1)} %shard_map.95.table_ref, bf16[8,16,80,128]{3,2,1,0:T(8,128)(2,1)} %copy-done.1), custom_call_target="tpu_custom_call" | custom-call | tf_op jit(solution)/shard_map/pallas_call | solution.py:116
  137.2 2.6 collective-permute-start.1
  139.8 23.8 %collective-permute-done.1 = bf16[16,128,128]{2,1,0:T(8,128)(2,1)S(1)} collective-permute-done((bf16[16,128,128]{2,1,0:T(8,128)(2,1)}, bf16[16,128,128]{2,1,0:T(8,128)(2,1)S(1)}, u32[]{:S(2)}, u32[]{:S(2)}) %collective-permute-start.1) | collective-permute-done | bytes 524320 | tf_op jit(solution)/shard_map/ppermute | solution.py:227
  163.6 1.4 add_convert_fusion
  164.9 1.2 copy.54
  166.1 0.0 all-to-all-done.data_ref
  166.1 0.0 copy-start
  166.1 3.5 %all-to-all-start.3 = ((bf16[16,128,128]{2,0,1:T(8,128)(2,1)}), bf16[16,128,128]{2,0,1:T(8,128)(2,1)S(1)}, u32[]{:S(2)}, u32[]{:S(2)}) async-start(bf16[16,128,128]{2,0,1:T(8,128)(2,1)} %copy.54), calls=%async_computation.3 | async-start | bytes 1048576 | tf_op jit(solution)/shard_map/all_to_all | solution.py:229
  169.6 0.0 copy-done
  169.6 11.7 %shard_map.96 = (f32[16,128,128]{2,1,0:T(8,128)}, bf16[16,128,128]{2,1,0:T(8,128)(2,1)}) custom-call(bf16[32,256,640]{2,1,0:T(8,128)(2,1)} %shard_map.95.table_ref, bf16[8,16,80,128]{3,2,1,0:T(8,128)(2,1)} %copy-done), custom_call_target="tpu_custom_call" | custom-call | tf_op jit(solution)/shard_map/pallas_call | solution.py:116
  181.3 2.9 collective-permute-start
  184.2 24.0 %collective-permute-done = bf16[16,128,128]{2,1,0:T(8,128)(2,1)S(1)} collective-permute-done((bf16[16,128,128]{2,1,0:T(8,128)(2,1)}, bf16[16,128,128]{2,1,0:T(8,128)(2,1)S(1)}, u32[]{:S(2)}, u32[]{:S(2)}) %collective-permute-start) | collective-permute-done | bytes 524320 | tf_op jit(solution)/shard_map/ppermute | solution.py:227
  208.3 1.4 add_convert_fusion.1
  209.7 1.1 copy.50
  210.8 0.0 all-to-all-done.3
  210.8 4.4 %all-to-all-start.1 = ((bf16[16,128,128]{2,0,1:T(8,128)(2,1)}), bf16[16,128,128]{2,0,1:T(8,128)(2,1)}, u32[]{:S(2)}, u32[]{:S(2)}) async-start(bf16[16,128,128]{2,0,1:T(8,128)(2,1)} %copy.50), calls=%async_computation.1 | async-start | bytes 1048576 | tf_op jit(solution)/shard_map/all_to_all | solution.py:229
  215.2 0.1 copy.67
  215.3 0.4 reshape.61
  215.7 0.7 copy.57
  216.4 0.0 copy-start.2
  216.4 7.4 %all-to-all-done.1 = bf16[16,128,128]{2,0,1:T(8,128)(2,1)} async-done(((bf16[16,128,128]{2,0,1:T(8,128)(2,1)}), bf16[16,128,128]{2,0,1:T(8,128)(2,1)}, u32[]{:S(2)}, u32[]{:S(2)}) %all-to-all-start.1) | async-done | bytes 524320 | tf_op jit(solution)/shard_map/all_to_all | solution.py:229
  223.8 1.2 copy.68
  225.0 0.4 reshape.59
  225.4 0.7 copy.56
  226.1 0.0 copy-done.2
  226.1 1.0 fusion.25
  227.1 3.5 %copy.58 = f32[64,16,720]{2,1,0:T(8,128)} copy(f32[64,16,720]{2,0,1:T(8,128)S(1)} %get-tuple-element.24) | data formatting | bytes 5898240 | tf_op jit(solution)/shard_map/qsorf,qsrl->fol/transpose | solution.py:235
  230.6 0.0 copy-start.4
  230.6 96.3 %shard_map.98 = f32[256,8,128]{2,1,0:T(8,128)} custom-call(f32[1024,720]{1,0:T(8,128)} %bitcast.52, s32[1024,720]{1,0:T(8,128)} %bitcast.53), custom_call_target="tpu_custom_call" | custom-call | tf_op jit(solution)/shard_map/pallas_call | solution.py:164
  326.9 2.3 reduce_max.27
  329.1 0.0 copy-done.4
  329.1 0.1 select_reduce_fusion
  329.3 0.7 all_to_all.42
  330.0 4.7 %all-to-all-start.4 = ((f32[16,1,16]{2,1,0:T(1,128)}), f32[16,1,16]{2,1,0:T(1,128)S(1)}, u32[]{:S(2)}, u32[]{:S(2)}) async-start(f32[16,1,16]{2,1,0:T(1,128)} %all_to_all.42), calls=%async_computation.4 | async-start | bytes 16384 | tf_op jit(solution)/shard_map/all_to_all | solution.py:251
  334.7 2.0 copy.60
  336.7 4.4 %all-to-all-done.4 = f32[16,1,16]{2,1,0:T(1,128)S(1)} async-done(((f32[16,1,16]{2,1,0:T(1,128)}), f32[16,1,16]{2,1,0:T(1,128)S(1)}, u32[]{:S(2)}, u32[]{:S(2)}) %all-to-all-start.4) | async-done | bytes 1056 | tf_op jit(solution)/shard_map/all_to_all | solution.py:251
  341.1 0.5 reduce_max.29
  (2 shorter events, 0.0 us)
Async XLA Ops:
  24.8 36.6 %all-to-all-start.2 = ((bf16[8,16,80,128]{3,2,1,0:T(8,128)(2,1)}), bf16[8,16,80,128]{3,2,1,0:T(8,128)(2,1)S(1)}, u32[]{:S(2)}, u32[]{:S(2)}) async-start(bf16[8,16,80,128]{3,2,1,0:T(8,128)(2,1)} %copy.53), calls=%async_computation.2 | async-start | bytes 5242880 | tf_op jit(solution)/shard_map/all_to_all | solution.py:204
  55.9 10.7 %copy-start.3 = (s32[1280]{0:T(1024)S(1)}, s32[1280]{0:T(1024)}, u32[]{:S(2)}) copy-start(s32[1280]{0:T(1024)} %param.9) | copy-start | bytes 15364
  61.3 1.5 copy-start.1
  62.8 103.3 %all-to-all-start = ((bf16[8,16,80,128]{3,2,1,0:T(8,128)(2,1)}), bf16[8,16,80,128]{3,2,1,0:T(8,128)(2,1)S(1)}, u32[]{:S(2)}, u32[]{:S(2)}) async-start(bf16[8,16,80,128]{3,2,1,0:T(8,128)(2,1)} %copy.49), calls=%async_computation | async-start | bytes 5242880 | tf_op jit(solution)/shard_map/all_to_all | solution.py:204
  137.2 26.4 %collective-permute-start.1 = (bf16[16,128,128]{2,1,0:T(8,128)(2,1)}, bf16[16,128,128]{2,1,0:T(8,128)(2,1)S(1)}, u32[]{:S(2)}, u32[]{:S(2)}) collective-permute-start(bf16[16,128,128]{2,1,0:T(8,128)(2,1)} %get-tuple-element.9), channel_id=1, source_target_pairs={{0,8},{8,0},{1,9},{9,1},{2,10},{10,2},{3,11},{11,3},{4,12},{12,4},... | collective-permute-start | bytes 1572872 | tf_op jit(solution)/shard_map/ppermute | solution.py:227
  166.1 3.5 %copy-start = (bf16[8,16,80,128]{3,2,1,0:T(8,128)(2,1)}, bf16[8,16,80,128]{3,2,1,0:T(8,128)(2,1)S(1)}, u32[]{:S(2)}) copy-start(bf16[8,16,80,128]{3,2,1,0:T(8,128)(2,1)S(1)} %all-to-all-done.data_ref) | copy-start | bytes 7864324
  166.1 44.7 %all-to-all-start.3 = ((bf16[16,128,128]{2,0,1:T(8,128)(2,1)}), bf16[16,128,128]{2,0,1:T(8,128)(2,1)S(1)}, u32[]{:S(2)}, u32[]{:S(2)}) async-start(bf16[16,128,128]{2,0,1:T(8,128)(2,1)} %copy.54), calls=%async_computation.3 | async-start | bytes 1048576 | tf_op jit(solution)/shard_map/all_to_all | solution.py:229
  181.3 27.0 %collective-permute-start = (bf16[16,128,128]{2,1,0:T(8,128)(2,1)}, bf16[16,128,128]{2,1,0:T(8,128)(2,1)S(1)}, u32[]{:S(2)}, u32[]{:S(2)}) collective-permute-start(bf16[16,128,128]{2,1,0:T(8,128)(2,1)} %get-tuple-element.7), channel_id=1, source_target_pairs={{0,8},{8,0},{1,9},{9,1},{2,10},{10,2},{3,11},{11,3},{4,12},{12,4},... | collective-permute-start | bytes 1572872 | tf_op jit(solution)/shard_map/ppermute | solution.py:227
  210.8 13.0 %all-to-all-start.1 = ((bf16[16,128,128]{2,0,1:T(8,128)(2,1)}), bf16[16,128,128]{2,0,1:T(8,128)(2,1)}, u32[]{:S(2)}, u32[]{:S(2)}) async-start(bf16[16,128,128]{2,0,1:T(8,128)(2,1)} %copy.50), calls=%async_computation.1 | async-start | bytes 1048576 | tf_op jit(solution)/shard_map/all_to_all | solution.py:229
  216.4 9.7 %copy-start.2 = (bf16[8,32,2,720,1]{3,1,2,4,0:T(8,128)(2,1)S(1)}, bf16[8,32,2,720,1]{3,1,2,4,0:T(8,128)(2,1)}, u32[]{:S(2)}) copy-start(bf16[8,32,2,720,1]{3,1,2,4,0:T(8,128)(2,1)} %constant.69) | copy-start | bytes 2211844
  230.6 98.5 %copy-start.4 = (s32[256]{0:T(256)S(1)}, s32[256]{0:T(256)}, u32[]{:S(2)}) copy-start(s32[256]{0:T(256)} %param.11) | copy-start | bytes 3076
  330.0 11.1 %all-to-all-start.4 = ((f32[16,1,16]{2,1,0:T(1,128)}), f32[16,1,16]{2,1,0:T(1,128)S(1)}, u32[]{:S(2)}, u32[]{:S(2)}) async-start(f32[16,1,16]{2,1,0:T(1,128)} %all_to_all.42), calls=%async_computation.4 | async-start | bytes 16384 | tf_op jit(solution)/shard_map/all_to_all | solution.py:251

commit v2 on v1

v2 whole, which is shorter than its diff:
```python
import math

import jax
import jax.numpy as jnp
import numpy as np
from jax import lax
from jax.experimental import pallas as pl
from jax.experimental.pallas import tpu as pltpu
from jax.sharding import Mesh
from jax.sharding import PartitionSpec as P

MW = 256
OUT_LAT = 256
OUT_LON = 720
FLOOR = -1e30
GROUP = 8
LANES = 128
SCAN_ROWS = 4


def fourier_table(lon_count):
    steps = np.arange(lon_count)[:, None] * np.arange(MW)[None, :] % lon_count
    angles = steps * (2.0 * math.pi / lon_count)
    return np.stack([np.cos(angles), -np.sin(angles)], axis=-1) / lon_count


def synthesis_table(lon_count):
    steps = np.arange(MW)[:, None] * np.arange(lon_count)[None, :] % lon_count
    angles = steps * (2.0 * math.pi / lon_count)
    factor = np.where(np.arange(MW) == 0, 1.0, 2.0)[:, None]
    return np.stack([factor * np.cos(angles), -factor * np.sin(angles)], axis=1)


def diagonal_logs():
    counters = np.arange(1, MW, dtype=np.float64)
    increments = np.log((2.0 * counters + 1.0) / (2.0 * counters))
    sums = np.concatenate([[0.0], np.cumsum(increments)])
    return (0.5 * math.log(0.5) + 0.5 * sums).astype(np.float32)


def params(mebibytes):
    return pltpu.CompilerParams(vmem_limit_bytes=mebibytes << 20)


def whole(shape, dtype):
    return jax.ShapeDtypeStruct(shape, dtype)


IN_VMEM = pl.BlockSpec(memory_space=pltpu.VMEM)


def fourier(vorticity, table, senders, parts):
    fields, rows, lon_count = vorticity.shape
    waves = table.shape[1] // 2
    block = 16 if rows % 16 == 0 else 8
    wave_block = waves // parts

    def body(data_ref, table_ref, *refs):
        out_refs, (product_ref, turned_ref) = refs[:parts], refs[parts:]
        data = data_ref[...].reshape(fields * block, lon_count)
        product = jnp.dot(data, table_ref[...], preferred_element_type=jnp.float32)
        for t in range(2 * waves // LANES):
            product_ref[t] = product[:, t * LANES : (t + 1) * LANES]
        for j in range(block):
            for t in range(waves // LANES):
                pair = [
                    product_ref[r * (waves // LANES) + t, pl.ds(j, fields, stride=block), :]
                    for r in range(2)
                ]
                start = t * LANES * block + j
                turned_ref[pl.ds(start, LANES, stride=block), :] = jnp.concatenate(pair, axis=0).T
        for p in range(parts):
            size = wave_block * block
            part = turned_ref[p * size : (p + 1) * size, :]
            out_refs[p][...] = part.astype(jnp.bfloat16).reshape(out_refs[p].shape)

    shape = (senders, wave_block // senders, rows, 2 * fields)
    return pl.pallas_call(
        body,
        out_shape=[whole(shape, jnp.bfloat16)] * parts,
        grid=(rows // block,),
        in_specs=[
            pl.BlockSpec((fields, block, lon_count), lambda i: (0, i, 0)),
            pl.BlockSpec(table.shape, lambda i: (0, 0), pipeline_mode=pl.Buffered(1)),
        ],
        out_specs=[
            pl.BlockSpec((shape[0], shape[1], block, shape[3]), lambda i: (0, 0, i, 0))
        ] * parts,
        scratch_shapes=[
            pltpu.VMEM((2 * waves // LANES, fields * block, LANES), jnp.float32),
            pltpu.VMEM((waves * block, 2 * fields), jnp.float32),
        ],
        compiler_params=params(24),
    )(vorticity, table)


def halves_of(x):
    high = x.astype(jnp.bfloat16)
    return high, (x - high.astype(jnp.float32)).astype(jnp.bfloat16)


def kernel_table(orders, start, cosines, weights, out_rows, offsets):
    columns = start.shape[1]
    in_rows = columns - out_rows
    tiles = columns // LANES
    out_tiles = out_rows // LANES

    def body(order_ref, start_ref, cos_ref, weight_ref, out_ref, table_ref):
        m = jnp.broadcast_to(order_ref[...], (GROUP, LANES))
        cosine = [
            jnp.broadcast_to(cos_ref[:, t * LANES : (t + 1) * LANES], (GROUP, LANES))
            for t in range(tiles)
        ]

        def step(k, carry):
            previous, earlier = carry
            offset = k.astype(jnp.float32)
            degree = m + offset
            below = degree - 1.0
            first = jnp.sqrt((4.0 * degree * degree - 1.0) / (offset * (2.0 * m + offset)))
            second = jnp.sqrt(
                (offset - 1.0)
                * (2.0 * m + offset - 1.0)
                / jnp.maximum(4.0 * below * below - 1.0, 1.0)
            )
            keep = degree <= MW - 1.0
            row = pl.multiple_of(k * GROUP, GROUP)
            current = []
            for t in range(tiles):
                value = first * (cosine[t] * previous[t] - second * earlier[t])
                current.append(value)
                stored = jnp.where(keep, value, 0.0) if t < out_tiles else value
                table_ref[t, pl.ds(row, GROUP), :] = stored
            return (tuple(current), previous)

        first_rows = tuple(start_ref[:, t * LANES : (t + 1) * LANES] for t in range(tiles))
        for t in range(tiles):
            table_ref[t, 0:GROUP, :] = first_rows[t]
        zeros = tuple(jnp.zeros((GROUP, LANES), jnp.float32) for _ in range(tiles))
        first_step = step(jnp.int32(1), (first_rows, zeros))
        second_step = step(jnp.int32(2), first_step)
        third_step = step(jnp.int32(3), second_step)
        lax.fori_loop(4, offsets, step, third_step, unroll=4)
        weight = weight_ref[...]
        for s in range(GROUP):
            values = [table_ref[t, pl.ds(s, offsets, stride=GROUP), :] for t in range(tiles)]
            out_high, out_low = halves_of(jnp.concatenate(values[:out_tiles], axis=1))
            in_high, in_low = halves_of(jnp.concatenate(values[out_tiles:], axis=1))
            product = lax.dot_general(
                jnp.concatenate([out_high, out_high, out_low], axis=0),
                jnp.concatenate([in_high, in_low, in_high], axis=0),
                (((0,), (0,)), ((), ())),
                preferred_element_type=jnp.float32,
            )
            out_ref[s] = (product * weight).astype(jnp.bfloat16)

    return pl.pallas_call(
        body,
        out_shape=whole((GROUP, out_rows, in_rows), jnp.bfloat16),
        in_specs=[IN_VMEM] * 4,
        out_specs=IN_VMEM,
        scratch_shapes=[pltpu.VMEM((tiles, offsets * GROUP, LANES), jnp.float32)],
        compiler_params=params(24),
    )(orders, start, cosines, weights)


def apply_table(table, received):
    senders, slots, rows, columns = received.shape
    out_rows = table.shape[1]
    half = out_rows // 2

    def body(table_ref, data_ref, own_ref, other_ref, wide_ref):
        for s in range(slots):
            data = data_ref[:, s].reshape(senders * rows, columns)
            product = jnp.dot(table_ref[s], data, preferred_element_type=jnp.float32)
            own_ref[pl.ds(s, half, stride=slots), :] = product[:half]
            wide_ref[pl.ds(s, half, stride=slots), :] = product[half:]
        other_ref[...] = wide_ref[...].astype(jnp.bfloat16)

    return pl.pallas_call(
        body,
        out_shape=(
            whole((half * slots, columns), jnp.float32),
            whole((half * slots, columns), jnp.bfloat16),
        ),
        in_specs=[IN_VMEM] * 2,
        out_specs=(IN_VMEM, IN_VMEM),
        scratch_shapes=[pltpu.VMEM((half * slots, columns), jnp.float32)],
        compiler_params=params(16),
    )(table, received)


def storm_maxima(values, labels, storm_count):
    rows, lon_count = values.shape
    block = math.gcd(rows, 512)
    steps = rows // block
    tiles = -(-lon_count // LANES)
    tail = lon_count - (tiles - 1) * LANES
    span = math.gcd(block, 256)
    sets = [(t, r) for t in range(tiles) for r in range(0, block, span)]
    chosen = steps * len(sets)

    def body(value_ref, label_ref, out_ref, kept_ref, name_ref, best_ref, storm_ref, top_ref):
        step = pl.program_id(0)

        @pl.when(step == 0)
        def _():
            kept_ref[tiles - 1] = jnp.full((rows, LANES), FLOOR, jnp.float32)
            name_ref[tiles - 1] = jnp.full((rows, LANES), storm_count, jnp.int32)

        base = pl.multiple_of(step * block, block)
        for t in range(tiles):
            width = LANES if t < tiles - 1 else tail
            columns = slice(t * LANES, t * LANES + width)
            name = label_ref[:, columns]
            value = jnp.where(name < storm_count, value_ref[:, columns], FLOOR)
            kept_ref[t, pl.ds(base, block), 0:width] = value
            name_ref[t, pl.ds(base, block), 0:width] = name
        for s, (t, r) in enumerate(sets):
            best = jnp.full((8, LANES), FLOOR, jnp.float32)
            storm = jnp.zeros((8, LANES), jnp.int32)
            for i in range(r, r + span, 8):
                value = kept_ref[t, pl.ds(base + i, 8), :]
                name = name_ref[t, pl.ds(base + i, 8), :]
                higher = value > best
                best = jnp.where(higher, value, best)
                storm = jnp.where(higher, name, storm)
            best_ref[step * len(sets) + s] = best
            storm_ref[step * len(sets) + s] = storm

        def raise_tops(bests, storms):
            def per_storm(i, carry):
                picked = [jnp.where(storm == i, best, FLOOR) for best, storm in zip(bests, storms)]
                while len(picked) > 1:
                    paired = [jnp.maximum(a, b) for a, b in zip(picked[::2], picked[1::2])]
                    picked = paired + picked[2 * len(paired):]
                top = jnp.max(picked[0], axis=0, keepdims=True)
                top_ref[pl.ds(i, 1), :] = jnp.maximum(top_ref[pl.ds(i, 1), :], top)
                return carry

            lax.fori_loop(0, storm_count, per_storm, 0, unroll=8)

        def merge(a, b):
            higher = b[0] > a[0]
            return (jnp.where(higher, b[0], a[0]), jnp.where(higher, b[1], a[1]), a[2] + b[2])

        def tops():
            return jnp.max(top_ref[...].T, axis=0, keepdims=True)

        @pl.when(step == steps - 1)
        def _():
            top_ref[...] = jnp.full(top_ref.shape, FLOOR, jnp.float32)
            raise_tops([best_ref[c] for c in range(chosen)], [storm_ref[c] for c in range(chosen)])

            def scan(carry):
                top = tops()
                table = [
                    jnp.broadcast_to(top[:, h * LANES : (h + 1) * LANES], (8, LANES))
                    for h in range(storm_count // LANES)
                ]
                tiny = jnp.zeros((8, LANES), jnp.float32)

                def per_rows(i, state):
                    row = pl.multiple_of(i * (8 * SCAN_ROWS), 8 * SCAN_ROWS)
                    found = []
                    for r in range(SCAN_ROWS):
                        for t in range(tiles):
                            value = kept_ref[t, pl.ds(row + 8 * r, 8), :]
                            name = name_ref[t, pl.ds(row + 8 * r, 8), :]
                            place = jnp.bitwise_and(name, LANES - 1)
                            known = jnp.take_along_axis(table[0], place, axis=1)
                            for h in range(1, len(table)):
                                other = jnp.take_along_axis(table[h], place, axis=1)
                                known = jnp.where(name >= h * LANES, other, known)
                            open_ = value > known
                            found.append(
                                (jnp.where(open_, value, FLOOR), name, jnp.where(open_, 1.0, 0.0))
                            )
                    while len(found) > 1:
                        paired = [merge(a, b) for a, b in zip(found[::2], found[1::2])]
                        found = paired + found[2 * len(paired):]
                    return merge(state, found[0])

                init = (jnp.full((8, LANES), FLOOR, jnp.float32), jnp.zeros((8, LANES), jnp.int32), tiny)
                best, storm, count = lax.fori_loop(0, rows // (8 * SCAN_ROWS), per_rows, init)
                most = jnp.max(count)

                @pl.when(most > 0.0)
                def _():
                    raise_tops([best], [storm])

                return most

            lax.while_loop(lambda most: most > 1.0, scan, jnp.float32(2.0))
            out_ref[...] = tops()

    return pl.pallas_call(
        body,
        out_shape=jax.ShapeDtypeStruct((1, storm_count), jnp.float32),
        grid=(steps,),
        in_specs=[
            pl.BlockSpec((block, lon_count), lambda i: (i, 0)),
            pl.BlockSpec((block, lon_count), lambda i: (i, 0)),
        ],
        out_specs=pl.BlockSpec((1, storm_count), lambda i: (0, 0)),
        scratch_shapes=[
            pltpu.VMEM((tiles, rows, LANES), jnp.float32),
            pltpu.VMEM((tiles, rows, LANES), jnp.int32),
            pltpu.VMEM((chosen, 8, LANES), jnp.float32),
            pltpu.VMEM((chosen, 8, LANES), jnp.int32),
            pltpu.VMEM((storm_count, LANES), jnp.float32),
        ],
        compiler_params=params(32),
    )(values, labels)

def local(vorticity, lat_order, storm_labels, storm_owner):
    field_count, lat_rows, lon_count = vorticity.shape
    lat_count = lat_order.shape[0]
    halves = lax.axis_size("half")
    ranks = lax.axis_size("rest")
    half_index = lax.axis_index("half")
    rank = lax.axis_index("rest")
    band_rows = storm_labels.shape[1]
    storm_count = storm_owner.shape[0]
    slots = MW // ranks
    chunks = slots // GROUP
    columns = 2 * field_count
    out_half = OUT_LAT // halves

    parts = min(2, chunks)
    calls = chunks // parts
    table = fourier_table(lon_count).reshape(lon_count, calls, parts, GROUP, ranks, 2)
    table = table.transpose(1, 0, 5, 2, 4, 3).reshape(calls, lon_count, 2 * MW // calls)
    table = table.astype(jnp.bfloat16)

    received = []
    for c in range(calls):
        for coefficients in fourier(vorticity, jnp.asarray(table[c]), ranks, parts):
            received.append(
                lax.all_to_all(coefficients, "rest", split_axis=0, concat_axis=0, tiled=True)
            )

    half_rows = ranks * lat_rows
    own_order = lax.dynamic_slice_in_dim(lat_order, half_index * half_rows, half_rows)
    colatitude = math.pi * (4.0 * own_order.astype(jnp.float32) + 3.0) / (4.0 * lat_count + 2.0)
    weights = math.pi / lat_count * jnp.sin(colatitude)
    band_index = jnp.arange(OUT_LAT, dtype=jnp.int32)
    band_index = ((band_index + half_index * out_half) % OUT_LAT).astype(jnp.float32)
    latitude = ((OUT_LAT - 1) / 2.0 - band_index) * (360.0 / OUT_LON) * (math.pi / 180.0)
    sine_values = jnp.concatenate([jnp.cos(latitude), jnp.sin(colatitude)])
    cosines = jnp.concatenate([jnp.sin(latitude), jnp.cos(colatitude)])
    orders = jnp.arange(slots, dtype=jnp.int32) * ranks + rank
    start_logs = jnp.asarray(diagonal_logs().reshape(slots, ranks))
    start_logs = lax.dynamic_slice_in_dim(start_logs, rank, 1, axis=1)
    orders = orders.astype(jnp.float32)[:, None]
    start = jnp.exp(start_logs + orders * jnp.log(sine_values)[None, :])
    kernels = [
        kernel_table(
            orders[c * GROUP : (c + 1) * GROUP],
            start[c * GROUP : (c + 1) * GROUP],
            cosines[None, :],
            weights[None, :],
            OUT_LAT,
            MW - c * GROUP * ranks,
        )
        for c in range(chunks)
    ]

    partial = [apply_table(kernels[c], received[c]) for c in range(chunks)]
    gathered = []
    swap = [(0, 1), (1, 0)]
    for own, other in partial:
        mirrored = lax.ppermute(other, "half", swap)
        band = (own + mirrored.astype(jnp.float32)).astype(jnp.bfloat16)
        band = band.reshape(ranks, band_rows * GROUP, columns)
        band = lax.all_to_all(band, "rest", split_axis=0, concat_axis=0, tiled=True)
        gathered.append(band.reshape(ranks, band_rows, GROUP, 2, field_count))

    gathered = jnp.stack(gathered)
    synthesis = synthesis_table(OUT_LON).reshape(chunks, GROUP, ranks, 2, OUT_LON)
    synthesis = jnp.asarray(synthesis.transpose(0, 2, 1, 3, 4).astype(jnp.bfloat16))
    grid_values = jnp.einsum(
        "cqosrf,cqsrl->fol", gathered, synthesis, preferred_element_type=jnp.float32
    )
    filtered = grid_values.astype(jnp.bfloat16)
    point_rows = field_count * band_rows
    local_peaks = storm_maxima(
        grid_values.reshape(point_rows, OUT_LON),
        storm_labels.reshape(point_rows, OUT_LON),
        storm_count,
    )[0]
    slot_ids = jnp.arange(storm_count, dtype=jnp.int32)
    by_slot = jnp.max(
        jnp.where(storm_owner[:, None] == slot_ids[None, :], local_peaks[:, None], FLOOR), axis=0
    )
    spec_count = halves * ranks
    shares = lax.all_to_all(
        by_slot.reshape(spec_count, storm_count // spec_count),
        ("half", "rest"),
        split_axis=0,
        concat_axis=0,
        tiled=True,
    )
    return (filtered, jnp.max(shares, axis=0))


def solution(mesh):
    groups = mesh.shape["grp"]
    spec_count = mesh.shape["spec"]
    split = Mesh(
        mesh.devices.reshape(groups, 2, spec_count // 2), axis_names=("grp", "half", "rest")
    )
    both = ("half", "rest")
    return jax.shard_map(
        local,
        mesh=split,
        in_specs=(P("grp", both, None), P(), P("grp", both, None), P("grp")),
        out_specs=(P("grp", both, None), P(("grp", "half", "rest"))),
        check_vma=False,
    )
```

time: 343 us -> 208 us (0.61); the launches traced: 342 us -> 210 us
  Pallas kernels: 175 us -> 58.9 us
  blocking collectives: 0 us -> 44.3 us
  waiting for transfers between devices: 65 us -> 27.5 us
  matrix products: 27.1 us -> 2.62 us
  starting transfers between devices: 27.1 us -> 40.1 us
  local copies, waits for them, and re-layouts: 39.2 us -> 30.1 us
    pallas_call x4 -> x11, Pallas kernels: 175 us -> 58.9 us  [the longest x2 25.8 us: fourier(): pl.pallas_call(body, out_shape=[whole(shape, jnp.bfloat16)] * parts, grid...]
    all_to_all x0 -> x2, blocking collectives: none -> 44.3 us  [local(): lax.all_to_all(coefficients, 'rest', split_axis=0, concat_axis=0, tiled=T...]
    ppermute x2 -> x4, waiting for transfers between devices: 47.8 us -> 15.3 us  [local(): mirrored = lax.ppermute(other, 'half', swap)]
    dot_general x3 -> x1, matrix products: 27.1 us -> 2.62 us  [local(): jnp.einsum('cqosrf,cqsrl->fol', gathered, synthesis, preferred_element_ty...]
    unnamed x11 -> x29, local copies, waits for them, and re-layouts: 3.48 us -> 23.2 us
    reshape x6 -> x0, local copies, waits for them, and re-layouts: 14.2 us -> none  [the longest x2 12.1 us: local(): coefficients.astype(jnp.bfloat16)]
    convert_element_type x4 -> x0, local copies, waits for them, and re-layouts: 14.2 us -> none  [the longest x2 11.9 us: local(): coefficients.astype(jnp.bfloat16)]
    all_to_all x2 -> x4, starting transfers between devices: 7.86 us -> 16.5 us  [local(): band = lax.all_to_all(band, 'rest', split_axis=0, concat_axis=0, tiled=True)]
  transfers between devices with their start and end apart: 7 -> 11, of which waited for: 5 -> 6; matrix products, arithmetic and copies ran while one was open for 11% -> 5% of each run, Pallas kernels for 23% -> 17%
where the time goes in v2:
time: 208 us; the launch traced here: 210 us
  Pallas kernels  58.9 us (28%)
  blocking collectives  44.3 us (21%)
  starting transfers between devices  40.1 us (19%)
  local copies, waits for them, and re-layouts  30.1 us (14%)
  waiting for transfers between devices  27.5 us (13%)
  other arithmetic  5.96 us (3%)
  matrix products  2.62 us (1%)
    all_to_all x2, blocking collectives, local(): lax.all_to_all(coefficients, 'rest', split_axis=0, concat_axis=0, tiled=T...  44.3 us
    pallas_call x2, Pallas kernels, fourier(): pl.pallas_call(body, out_shape=[whole(shape, jnp.bfloat16)] * parts, grid...  25.8 us
    unnamed x29, local copies, waits for them, and re-layouts  23.2 us
    pallas_call x4, Pallas kernels, kernel_table(): pl.pallas_call(body, out_shape=whole((GROUP, out_rows, in_rows), jnp.bflo...  17.8 us
    all_to_all x4, starting transfers between devices, local(): band = lax.all_to_all(band, 'rest', split_axis=0, concat_axis=0, tiled=True)  16.5 us
    ppermute x4, waiting for transfers between devices, local(): mirrored = lax.ppermute(other, 'half', swap)  15.3 us
    pallas_call x1, Pallas kernels, storm_maxima(): pl.pallas_call(body, out_shape=jax.ShapeDtypeStruct((1, storm_count), jnp...  10.9 us
    all_to_all x1, starting transfers between devices, local(): lax.all_to_all(by_slot.reshape(spec_count, storm_count // spec_count), ('...  9.97 us
  transfers between devices with their start and end apart: 11, of which 6 were waited for; matrix products, arithmetic and copies ran while one was open for 5% of the time, Pallas kernels for 17%

profile of v2, /device:TPU:0, one launch (start us, length us, event | category | flops | bytes accessed | tf_op | source)
XLA Modules:
  0.0 210.3 jit_solution(8647325809576426367)
XLA Ops:
  0.6 8.4 %copy-done = bf16[64,80,2560]{2,1,0:T(8,128)(2,1)S(1)} copy-done((bf16[64,80,2560]{2,1,0:T(8,128)(2,1)S(1)}, bf16[64,80,2560]{2,1,0:T(8,128)(2,1)}, u32[]{:S(2)}) %copy-start) | copy-done | bytes 26214424
  9.1 1.3 copy-done.9
  10.4 13.2 %shard_map.101 = (bf16[8,8,80,128]{3,2,1,0:T(8,128)(2,1)}, bf16[8,8,80,128]{3,2,1,0:T(8,128)(2,1)S(1)}) custom-call(bf16[64,80,2560]{2,1,0:T(8,128)(2,1)S(1)} %copy-done, bf16[2560,256]{1,0:T(8,128)(2,1)S(1)} %copy-done.9), custom_call_target="tpu_custom_call" | custom-call | tf_op jit(solution)/shard_map/pallas_call | solution.py:78
  23.6 22.6 %all_to_all.49.data_ref = bf16[8,8,80,128]{3,2,1,0:T(8,128)(2,1)} all-to-all(bf16[8,8,80,128]{3,2,1,0:T(8,128)(2,1)S(1)} %get-tuple-element.23), channel_id=1, replica_groups=mesh['grp'=2,'half'=2,'rest'=8] {'rest'}, dimensions={0} | all-to-all | bytes 2621440 | tf_op jit(solution)/shard_map/all_to_all | solution.py:340
  46.2 3.7 %all-to-all-start.4 = ((bf16[8,8,80,128]{3,2,1,0:T(8,128)(2,1)}), bf16[8,8,80,128]{3,2,1,0:T(8,128)(2,1)S(1)}, u32[]{:S(2)}, u32[]{:S(2)}) async-start(bf16[8,8,80,128]{3,2,1,0:T(8,128)(2,1)} %get-tuple-element.20), calls=%async_computation.4 | async-start | bytes 2621440 | tf_op jit(solution)/shard_map/all_to_all | solution.py:340
  49.9 8.4 %copy-done.1 = bf16[64,80,2560]{2,1,0:T(8,128)(2,1)S(1)} copy-done((bf16[64,80,2560]{2,1,0:T(8,128)(2,1)S(1)}, bf16[64,80,2560]{2,1,0:T(8,128)(2,1)}, u32[]{:S(2)}) %copy-start.1) | copy-done | bytes 26214424
  58.4 12.6 %shard_map.96 = (bf16[8,8,80,128]{3,2,1,0:T(8,128)(2,1)S(1)}, bf16[8,8,80,128]{3,2,1,0:T(8,128)(2,1)S(1)}) custom-call(bf16[64,80,2560]{2,1,0:T(8,128)(2,1)S(1)} %copy-done.1, bf16[2560,256]{1,0:T(8,128)(2,1)S(1)} %copy-done.8), custom_call_target="tpu_custom_call" | custom-call | tf_op jit(solution)/shard_map/pallas_call | solution.py:78
  71.0 1.1 copy-done.6
  72.0 1.1 copy-done.7
  73.1 21.7 %all_to_all.50.data_ref = bf16[8,8,80,128]{3,2,1,0:T(8,128)(2,1)S(1)} all-to-all(bf16[8,8,80,128]{3,2,1,0:T(8,128)(2,1)} %copy-done.7), channel_id=1, replica_groups=mesh['grp'=2,'half'=2,'rest'=8] {'rest'}, dimensions={0} | all-to-all | bytes 2621440 | tf_op jit(solution)/shard_map/all_to_all | solution.py:340
  94.8 3.6 %all-to-all-start = ((bf16[8,8,80,128]{3,2,1,0:T(8,128)(2,1)}), bf16[8,8,80,128]{3,2,1,0:T(8,128)(2,1)S(1)}, u32[]{:S(2)}, u32[]{:S(2)}) async-start(bf16[8,8,80,128]{3,2,1,0:T(8,128)(2,1)} %copy-done.6), calls=%async_computation | async-start | bytes 2621440 | tf_op jit(solution)/shard_map/all_to_all | solution.py:340
  98.4 0.1 slice_bitcast_fusion.3
  98.5 0.1 copy.39.order_ref
  98.6 0.1 fusion.18
  98.6 0.1 fusion.17
  98.7 0.1 broadcast_multiply_fusion
  98.9 0.8 dynamic-slice_bitcast_fusion
  99.7 0.1 add_exponential_fusion
  99.8 1.9 shard_map.103.table_ref
  101.7 0.9 shard_map.104
  102.6 2.7 %collective-permute-start.3 = (bf16[1024,128]{1,0:T(8,128)(2,1)S(1)}, bf16[1024,128]{1,0:T(8,128)(2,1)}, u32[]{:S(2)}, u32[]{:S(2)}) collective-permute-start(bf16[1024,128]{1,0:T(8,128)(2,1)S(1)} %get-tuple-element.25), channel_id=1, source_target_pairs={{0,8},{8,0},{1,9},{9,1},{2,10},{10,2},{3,11},{11,3},{4,12},{12,4},... | collective-permute-start | bytes 786440 | tf_op jit(solution)/shard_map/ppermute | solution.py:373
  105.3 0.1 copy.38.order_ref
  105.4 3.7 %shard_map.100.table_ref = bf16[8,256,640]{2,1,0:T(8,128)(2,1)S(1)} custom-call(f32[8,1]{1,0:T(8,128)S(1)} %copy.38.order_ref, f32[8,896]{1,0:T(8,128)S(1)} %get-tuple-element.38.start_ref, f32[1,896]{1,0:T(1,128)S(1)} %broadcast_in_dim.14.cos_ref, f32[1,640]{1,0:T(1,128)S(1)} %broadcast_in_dim.15.weight_ref), custom_call_target="tpu_custom_call" | custom-call | tf_op jit(solution)/shard_map/pallas_call | solution.py:157
  109.1 1.6 shard_map.102
  110.7 0.8 copy-done.10
  111.5 0.3 collective-permute-start.2
  111.8 7.6 %collective-permute-done.3 = bf16[1024,128]{1,0:T(8,128)(2,1)} collective-permute-done((bf16[1024,128]{1,0:T(8,128)(2,1)S(1)}, bf16[1024,128]{1,0:T(8,128)(2,1)}, u32[]{:S(2)}, u32[]{:S(2)}) %collective-permute-start.3) | collective-permute-done | bytes 262176 | tf_op jit(solution)/shard_map/ppermute | solution.py:373
  119.4 1.7 add_convert_fusion
  121.1 2.5 %all-to-all-done.data_ref = bf16[8,8,80,128]{3,2,1,0:T(8,128)(2,1)S(1)} async-done(((bf16[8,8,80,128]{3,2,1,0:T(8,128)(2,1)}), bf16[8,8,80,128]{3,2,1,0:T(8,128)(2,1)S(1)}, u32[]{:S(2)}, u32[]{:S(2)}) %all-to-all-start) | async-done | bytes 1310752 | tf_op jit(solution)/shard_map/all_to_all | solution.py:340
  123.6 4.7 %all-to-all-start.7 = ((bf16[8,128,128]{2,1,0:T(8,128)(2,1)}), bf16[8,128,128]{2,1,0:T(8,128)(2,1)}, u32[]{:S(2)}, u32[]{:S(2)}) async-start(bf16[8,128,128]{2,1,0:T(8,128)(2,1)} %bitcast.8), calls=%async_computation.7 | async-start | bytes 524288 | tf_op jit(solution)/shard_map/all_to_all | solution.py:376
  128.4 0.1 copy.37.order_ref
  128.4 5.4 %shard_map.98.table_ref = bf16[8,256,640]{2,1,0:T(8,128)(2,1)S(1)} custom-call(f32[8,1]{1,0:T(8,128)S(1)} %copy.37.order_ref, f32[8,896]{1,0:T(8,128)S(1)} %get-tuple-element.39.start_ref, f32[1,896]{1,0:T(1,128)S(1)} %broadcast_in_dim.14.cos_ref, f32[1,640]{1,0:T(1,128)S(1)} %broadcast_in_dim.15.weight_ref), custom_call_target="tpu_custom_call" | custom-call | tf_op jit(solution)/shard_map/pallas_call | solution.py:157
  133.9 0.9 shard_map.99
  134.8 0.6 collective-permute-start.1
  135.4 1.7 add_convert_fusion.1
  137.1 3.9 %all-to-all-start.5 = ((bf16[8,128,128]{2,1,0:T(8,128)(2,1)}), bf16[8,128,128]{2,1,0:T(8,128)(2,1)S(1)}, u32[]{:S(2)}, u32[]{:S(2)}) async-start(bf16[8,128,128]{2,1,0:T(8,128)(2,1)} %bitcast.6), calls=%async_computation.5 | async-start | bytes 524288 | tf_op jit(solution)/shard_map/all_to_all | solution.py:376
  141.0 0.1 copy.36.order_ref
  141.1 6.8 %shard_map.95.table_ref = bf16[8,256,640]{2,1,0:T(8,128)(2,1)S(1)} custom-call(f32[8,1]{1,0:T(8,128)S(1)} %copy.36.order_ref, f32[8,896]{1,0:T(8,128)S(1)} %get-tuple-element.36.start_ref, f32[1,896]{1,0:T(1,128)S(1)} %broadcast_in_dim.14.cos_ref, f32[1,640]{1,0:T(1,128)S(1)} %broadcast_in_dim.15.weight_ref), custom_call_target="tpu_custom_call" | custom-call | tf_op jit(solution)/shard_map/pallas_call | solution.py:157
  147.9 0.9 shard_map.97
  148.9 2.8 %collective-permute-start = (bf16[1024,128]{1,0:T(8,128)(2,1)S(1)}, bf16[1024,128]{1,0:T(8,128)(2,1)S(1)}, u32[]{:S(2)}, u32[]{:S(2)}) collective-permute-start(bf16[1024,128]{1,0:T(8,128)(2,1)S(1)} %get-tuple-element.16), channel_id=1, source_target_pairs={{0,8},{8,0},{1,9},{9,1},{2,10},{10,2},{3,11},{11,3},{4,12},{12,4},... | collective-permute-start | bytes 786440 | tf_op jit(solution)/shard_map/ppermute | solution.py:373
  151.6 0.8 add_convert_fusion.2
  152.4 4.2 %all-to-all-start.3 = ((bf16[8,128,128]{2,1,0:T(8,128)(2,1)}), bf16[8,128,128]{2,1,0:T(8,128)(2,1)S(1)}, u32[]{:S(2)}, u32[]{:S(2)}) async-start(bf16[8,128,128]{2,1,0:T(8,128)(2,1)} %bitcast.4), calls=%async_computation.3 | async-start | bytes 524288 | tf_op jit(solution)/shard_map/all_to_all | solution.py:376
  156.6 7.7 %collective-permute-done = bf16[1024,128]{1,0:T(8,128)(2,1)S(1)} collective-permute-done((bf16[1024,128]{1,0:T(8,128)(2,1)S(1)}, bf16[1024,128]{1,0:T(8,128)(2,1)S(1)}, u32[]{:S(2)}, u32[]{:S(2)}) %collective-permute-start) | collective-permute-done | bytes 262176 | tf_op jit(solution)/shard_map/ppermute | solution.py:373
  164.3 0.8 add_convert_fusion.3
  165.1 2.3 %all-to-all-done.3 = bf16[8,128,128]{2,1,0:T(8,128)(2,1)S(1)} async-done(((bf16[8,128,128]{2,1,0:T(8,128)(2,1)}), bf16[8,128,128]{2,1,0:T(8,128)(2,1)S(1)}, u32[]{:S(2)}, u32[]{:S(2)}) %all-to-all-start.3) | async-done | bytes 262176 | tf_op jit(solution)/shard_map/all_to_all | solution.py:376
  167.4 3.6 %all-to-all-start.1 = ((bf16[8,128,128]{2,1,0:T(8,128)(2,1)}), bf16[8,128,128]{2,1,0:T(8,128)(2,1)S(1)}, u32[]{:S(2)}, u32[]{:S(2)}) async-start(bf16[8,128,128]{2,1,0:T(8,128)(2,1)} %bitcast.2), calls=%async_computation.1 | async-start | bytes 524288 | tf_op jit(solution)/shard_map/all_to_all | solution.py:376
  171.0 1.2 stack_reshape.15
  172.2 0.1 copy.43
  172.3 0.2 stack_reshape.14
  172.6 0.1 copy.42
  172.7 0.2 stack_reshape.13
  172.9 0.9 copy.41
  173.8 3.0 %all-to-all-done.1 = bf16[8,128,128]{2,1,0:T(8,128)(2,1)S(1)} async-done(((bf16[8,128,128]{2,1,0:T(8,128)(2,1)}), bf16[8,128,128]{2,1,0:T(8,128)(2,1)S(1)}, u32[]{:S(2)}, u32[]{:S(2)}) %all-to-all-start.1) | async-done | bytes 262176 | tf_op jit(solution)/shard_map/all_to_all | solution.py:376
  176.8 0.2 stack_reshape.12
  177.0 0.1 copy.40
  177.1 2.6 %fusion.22 = (bf16[64,16,720]{2,0,1:T(8,128)(2,1)S(1)}, f32[64,16,720]{2,0,1:T(8,128)S(1)}) fusion(bf16[4,8,8,2,720,1]{4,2,3,5,1,0:T(8,128)(2,1)} %constant.67, bf16[1,8,16,8,2,64]{5,3,4,2,1,0:T(8,128)(2,1)S(1)} %copy.43, bf16[1,8,16,8,2,64]{5,3,4,2,1,0:T(8,128)(2,1)S(1)} %copy.42, bf16[1,8,16,8,2,64]{5,3,4,2,1,0:T(8,128)(2,1)} %copy.41, ...), kind=kOutput, calls=%fused_computation.39 | convolution fusion | flops 757284864 | bytes 6209536 | tf_op jit(solution)/shard_map/cqosrf,cqsrl->fol/dot_general | solution.py:382
  179.8 1.8 copy.44
  181.6 10.9 %shard_map.105 = f32[1,256]{1,0:T(1,128)S(1)} custom-call(f32[1024,720]{1,0:T(8,128)S(1)} %bitcast.28, s32[1024,720]{1,0:T(8,128)S(1)} %bitcast.29), custom_call_target="tpu_custom_call" | custom-call | tf_op jit(solution)/shard_map/pallas_call | solution.py:297
  192.6 0.1 select_reduce_fusion
  192.7 0.7 all_to_all.38
  193.4 10.0 %all-to-all-start.8 = ((f32[16,1,16]{2,1,0:T(1,128)}), f32[16,1,16]{2,1,0:T(1,128)S(1)}, u32[]{:S(2)}, u32[]{:S(2)}) async-start(f32[16,1,16]{2,1,0:T(1,128)} %all_to_all.38), calls=%async_computation.8 | async-start | bytes 16384 | tf_op jit(solution)/shard_map/all_to_all | solution.py:397
  203.4 2.0 copy.46
  205.4 4.4 %all-to-all-done.8 = f32[16,1,16]{2,1,0:T(1,128)S(1)} async-done(((f32[16,1,16]{2,1,0:T(1,128)}), f32[16,1,16]{2,1,0:T(1,128)S(1)}, u32[]{:S(2)}, u32[]{:S(2)}) %all-to-all-start.8) | async-done | bytes 1056 | tf_op jit(solution)/shard_map/all_to_all | solution.py:397
  209.8 0.5 reduce_max.19
  (32 shorter events, 0.1 us)
Async XLA Ops:
  0.6 8.5 %copy-start = (bf16[64,80,2560]{2,1,0:T(8,128)(2,1)S(1)}, bf16[64,80,2560]{2,1,0:T(8,128)(2,1)}, u32[]{:S(2)}) copy-start(bf16[64,80,2560]{2,1,0:T(8,128)(2,1)} %data_ref.3) | copy-start | bytes 78643200
  9.1 1.3 copy-start.9
  46.2 3.7 %copy-start.8 = (bf16[2560,256]{1,0:T(8,128)(2,1)S(1)}, bf16[2560,256]{1,0:T(8,128)(2,1)}, u32[]{:S(2)}) copy-start(bf16[2560,256]{1,0:T(8,128)(2,1)} %constant.63.clone.table_ref) | copy-start | bytes 3932164
  46.2 26.9 %all-to-all-start.4 = ((bf16[8,8,80,128]{3,2,1,0:T(8,128)(2,1)}), bf16[8,8,80,128]{3,2,1,0:T(8,128)(2,1)S(1)}, u32[]{:S(2)}, u32[]{:S(2)}) async-start(bf16[8,8,80,128]{3,2,1,0:T(8,128)(2,1)} %get-tuple-element.20), calls=%async_computation.4 | async-start | bytes 2621440 | tf_op jit(solution)/shard_map/all_to_all | solution.py:340
  49.9 8.5 %copy-start.1 = (bf16[64,80,2560]{2,1,0:T(8,128)(2,1)S(1)}, bf16[64,80,2560]{2,1,0:T(8,128)(2,1)}, u32[]{:S(2)}) copy-start(bf16[64,80,2560]{2,1,0:T(8,128)(2,1)} %data_ref.3) | copy-start | bytes 78643200
  71.0 1.1 copy-start.6
  72.0 1.1 copy-start.7
  73.1 21.7 %copy-start.2 = (bf16[8,8,80,128]{3,2,1,0:T(8,128)(2,1)}, bf16[8,8,80,128]{3,2,1,0:T(8,128)(2,1)S(1)}, u32[]{:S(2)}) copy-start(bf16[8,8,80,128]{3,2,1,0:T(8,128)(2,1)S(1)} %all-to-all-done.4.data_ref) | copy-start | bytes 3932164
  73.1 25.6 %copy-start.12 = (s32[1280]{0:T(1024)S(1)}, s32[1280]{0:T(1024)}, u32[]{:S(2)}) copy-start(s32[1280]{0:T(1024)} %param.9) | copy-start | bytes 15364
  94.8 28.8 %all-to-all-start = ((bf16[8,8,80,128]{3,2,1,0:T(8,128)(2,1)}), bf16[8,8,80,128]{3,2,1,0:T(8,128)(2,1)S(1)}, u32[]{:S(2)}, u32[]{:S(2)}) async-start(bf16[8,8,80,128]{3,2,1,0:T(8,128)(2,1)} %copy-done.6), calls=%async_computation | async-start | bytes 2621440 | tf_op jit(solution)/shard_map/all_to_all | solution.py:340
  98.9 2.8 %copy-start.4 = (bf16[8,8,80,128]{3,2,1,0:T(8,128)(2,1)S(1)}, bf16[8,8,80,128]{3,2,1,0:T(8,128)(2,1)}, u32[]{:S(2)}) copy-start(bf16[8,8,80,128]{3,2,1,0:T(8,128)(2,1)} %all_to_all.49.data_ref) | copy-start | bytes 3932164
  102.6 16.8 %collective-permute-start.3 = (bf16[1024,128]{1,0:T(8,128)(2,1)S(1)}, bf16[1024,128]{1,0:T(8,128)(2,1)}, u32[]{:S(2)}, u32[]{:S(2)}) collective-permute-start(bf16[1024,128]{1,0:T(8,128)(2,1)S(1)} %get-tuple-element.25), channel_id=1, source_target_pairs={{0,8},{8,0},{1,9},{9,1},{2,10},{10,2},{3,11},{11,3},{4,12},{12,4},... | collective-permute-start | bytes 786440 | tf_op jit(solution)/shard_map/ppermute | solution.py:373
  105.4 3.7 %copy-start.3 = (bf16[8,8,80,128]{3,2,1,0:T(8,128)(2,1)S(1)}, bf16[8,8,80,128]{3,2,1,0:T(8,128)(2,1)}, u32[]{:S(2)}) copy-start(bf16[8,8,80,128]{3,2,1,0:T(8,128)(2,1)} %copy-done.2) | copy-start | bytes 3932164
  110.7 0.8 copy-start.10
  111.5 23.9 %collective-permute-start.2 = (bf16[1024,128]{1,0:T(8,128)(2,1)}, bf16[1024,128]{1,0:T(8,128)(2,1)}, u32[]{:S(2)}, u32[]{:S(2)}) collective-permute-start(bf16[1024,128]{1,0:T(8,128)(2,1)} %get-tuple-element.22), channel_id=1, source_target_pairs={{0,8},{8,0},{1,9},{9,1},{2,10},{10,2},{3,11},{11,3},{4,12},{12,4},... | collective-permute-start | bytes 786440 | tf_op jit(solution)/shard_map/ppermute | solution.py:373
  123.6 13.5 %all-to-all-start.7 = ((bf16[8,128,128]{2,1,0:T(8,128)(2,1)}), bf16[8,128,128]{2,1,0:T(8,128)(2,1)}, u32[]{:S(2)}, u32[]{:S(2)}) async-start(bf16[8,128,128]{2,1,0:T(8,128)(2,1)} %bitcast.8), calls=%async_computation.7 | async-start | bytes 524288 | tf_op jit(solution)/shard_map/all_to_all | solution.py:376
  133.9 1.5 copy-start.11
  134.8 16.8 %collective-permute-start.1 = (bf16[1024,128]{1,0:T(8,128)(2,1)S(1)}, bf16[1024,128]{1,0:T(8,128)(2,1)S(1)}, u32[]{:S(2)}, u32[]{:S(2)}) collective-permute-start(bf16[1024,128]{1,0:T(8,128)(2,1)S(1)} %get-tuple-element.19), channel_id=1, source_target_pairs={{0,8},{8,0},{1,9},{9,1},{2,10},{10,2},{3,11},{11,3},{4,12},{12,4},... | collective-permute-start | bytes 786440 | tf_op jit(solution)/shard_map/ppermute | solution.py:373
  137.1 15.2 %all-to-all-start.5 = ((bf16[8,128,128]{2,1,0:T(8,128)(2,1)}), bf16[8,128,128]{2,1,0:T(8,128)(2,1)S(1)}, u32[]{:S(2)}, u32[]{:S(2)}) async-start(bf16[8,128,128]{2,1,0:T(8,128)(2,1)} %bitcast.6), calls=%async_computation.5 | async-start | bytes 524288 | tf_op jit(solution)/shard_map/all_to_all | solution.py:376
  148.9 15.5 %collective-permute-start = (bf16[1024,128]{1,0:T(8,128)(2,1)S(1)}, bf16[1024,128]{1,0:T(8,128)(2,1)S(1)}, u32[]{:S(2)}, u32[]{:S(2)}) collective-permute-start(bf16[1024,128]{1,0:T(8,128)(2,1)S(1)} %get-tuple-element.16), channel_id=1, source_target_pairs={{0,8},{8,0},{1,9},{9,1},{2,10},{10,2},{3,11},{11,3},{4,12},{12,4},... | collective-permute-start | bytes 786440 | tf_op jit(solution)/shard_map/ppermute | solution.py:373
  152.4 15.0 %all-to-all-start.3 = ((bf16[8,128,128]{2,1,0:T(8,128)(2,1)}), bf16[8,128,128]{2,1,0:T(8,128)(2,1)S(1)}, u32[]{:S(2)}, u32[]{:S(2)}) async-start(bf16[8,128,128]{2,1,0:T(8,128)(2,1)} %bitcast.4), calls=%async_computation.3 | async-start | bytes 524288 | tf_op jit(solution)/shard_map/all_to_all | solution.py:376
  167.4 9.4 %all-to-all-start.1 = ((bf16[8,128,128]{2,1,0:T(8,128)(2,1)}), bf16[8,128,128]{2,1,0:T(8,128)(2,1)S(1)}, u32[]{:S(2)}, u32[]{:S(2)}) async-start(bf16[8,128,128]{2,1,0:T(8,128)(2,1)} %bitcast.2), calls=%async_computation.1 | async-start | bytes 524288 | tf_op jit(solution)/shard_map/all_to_all | solution.py:376
  179.7 1.9 copy-start.5
  181.6 10.9 %copy-start.13 = (s32[256]{0:T(256)S(1)}, s32[256]{0:T(256)}, u32[]{:S(2)}) copy-start(s32[256]{0:T(256)} %param.11) | copy-start | bytes 3076
  193.4 16.4 %all-to-all-start.8 = ((f32[16,1,16]{2,1,0:T(1,128)}), f32[16,1,16]{2,1,0:T(1,128)S(1)}, u32[]{:S(2)}, u32[]{:S(2)}) async-start(f32[16,1,16]{2,1,0:T(1,128)} %all_to_all.38), calls=%async_computation.8 | async-start | bytes 16384 | tf_op jit(solution)/shard_map/all_to_all | solution.py:397

commit v3 on v2

--- a/solution.py
+++ b/solution.py
@@ -1,3 +1,4 @@
+import functools
 import math
 
 import jax
@@ -49,11 +50,11 @@
 IN_VMEM = pl.BlockSpec(memory_space=pltpu.VMEM)
 
 
-def fourier(vorticity, table, senders, parts):
+def fourier(vorticity, table, senders, part_slots):
     fields, rows, lon_count = vorticity.shape
     waves = table.shape[1] // 2
     block = 16 if rows % 16 == 0 else 8
-    wave_block = waves // parts
+    parts = len(part_slots)
 
     def body(data_ref, table_ref, *refs):
         out_refs, (product_ref, turned_ref) = refs[:parts], refs[parts:]
@@ -69,29 +70,30 @@
                 ]
                 start = t * LANES * block + j
                 turned_ref[pl.ds(start, LANES, stride=block), :] = jnp.concatenate(pair, axis=0).T
+        start = 0
         for p in range(parts):
-            size = wave_block * block
-            part = turned_ref[p * size : (p + 1) * size, :]
+            size = senders * part_slots[p] * block
+            part = turned_ref[start : start + size, :]
             out_refs[p][...] = part.astype(jnp.bfloat16).reshape(out_refs[p].shape)
-
-    shape = (senders, wave_block // senders, rows, 2 * fields)
+            start += size
+
     return pl.pallas_call(
         body,
-        out_shape=[whole(shape, jnp.bfloat16)] * parts,
+        out_shape=[whole((senders, n, rows, 2 * fields), jnp.bfloat16) for n in part_slots],
         grid=(rows // block,),
         in_specs=[
             pl.BlockSpec((fields, block, lon_count), lambda i: (0, i, 0)),
             pl.BlockSpec(table.shape, lambda i: (0, 0), pipeline_mode=pl.Buffered(1)),
         ],
         out_specs=[
-            pl.BlockSpec((shape[0], shape[1], block, shape[3]), lambda i: (0, 0, i, 0))
-        ] * parts,
+            pl.BlockSpec((senders, n, block, 2 * fields), lambda i: (0, 0, i, 0)) for n in part_slots
+        ],
         scratch_shapes=[
             pltpu.VMEM((2 * waves // LANES, fields * block, LANES), jnp.float32),
             pltpu.VMEM((waves * block, 2 * fields), jnp.float32),
         ],
         compiler_params=params(24),
-    )(vorticity, table)
+    )(pltpu.with_memory_space_constraint(vorticity, pltpu.HBM), table)
 
 
 def halves_of(x):
@@ -164,15 +166,17 @@
     )(orders, start, cosines, weights)
 
 
-def apply_table(table, received):
+def apply_tables(tables, received):
     senders, slots, rows, columns = received.shape
-    out_rows = table.shape[1]
+    out_rows = tables[0].shape[1]
     half = out_rows // 2
 
-    def body(table_ref, data_ref, own_ref, other_ref, wide_ref):
+    def body(*refs):
+        table_refs, (data_ref, own_ref, other_ref, wide_ref) = refs[: len(tables)], refs[len(tables) :]
         for s in range(slots):
             data = data_ref[:, s].reshape(senders * rows, columns)
-            product = jnp.dot(table_ref[s], data, preferred_element_type=jnp.float32)
+            table = table_refs[s // GROUP][s % GROUP]
+            product = jnp.dot(table, data, preferred_element_type=jnp.float32)
             own_ref[pl.ds(s, half, stride=slots), :] = product[:half]
             wide_ref[pl.ds(s, half, stride=slots), :] = product[half:]
         other_ref[...] = wide_ref[...].astype(jnp.bfloat16)
@@ -183,11 +187,11 @@
             whole((half * slots, columns), jnp.float32),
             whole((half * slots, columns), jnp.bfloat16),
         ),
-        in_specs=[IN_VMEM] * 2,
+        in_specs=[IN_VMEM] * (len(tables) + 1),
         out_specs=(IN_VMEM, IN_VMEM),
         scratch_shapes=[pltpu.VMEM((half * slots, columns), jnp.float32)],
         compiler_params=params(16),
-    )(table, received)
+    )(*tables, received)
 
 
 def storm_maxima(values, labels, storm_count):
@@ -262,9 +266,10 @@
 
                 def per_rows(i, state):
                     row = pl.multiple_of(i * (8 * SCAN_ROWS), 8 * SCAN_ROWS)
-                    found = []
-                    for r in range(SCAN_ROWS):
-                        for t in range(tiles):
+                    merged = []
+                    for t in range(tiles):
+                        found = [state[t]]
+                        for r in range(SCAN_ROWS):
                             value = kept_ref[t, pl.ds(row + 8 * r, 8), :]
                             name = name_ref[t, pl.ds(row + 8 * r, 8), :]
                             place = jnp.bitwise_and(name, LANES - 1)
@@ -272,22 +277,29 @@
                             for h in range(1, len(table)):
                                 other = jnp.take_along_axis(table[h], place, axis=1)
                                 known = jnp.where(name >= h * LANES, other, known)
-                            open_ = value > known
+                            is_open = value > known
                             found.append(
-                                (jnp.where(open_, value, FLOOR), name, jnp.where(open_, 1.0, 0.0))
+                                (
+                                    jnp.where(is_open, value, FLOOR),
+                                    name,
+                                    jnp.where(is_open, 1.0, 0.0),
+                                )
                             )
-                    while len(found) > 1:
-                        paired = [merge(a, b) for a, b in zip(found[::2], found[1::2])]
-                        found = paired + found[2 * len(paired):]
-                    return merge(state, found[0])
-
-                init = (jnp.full((8, LANES), FLOOR, jnp.float32), jnp.zeros((8, LANES), jnp.int32), tiny)
-                best, storm, count = lax.fori_loop(0, rows // (8 * SCAN_ROWS), per_rows, init)
+                        while len(found) > 1:
+                            paired = [merge(a, b) for a, b in zip(found[::2], found[1::2])]
+                            found = paired + found[2 * len(paired) :]
+                        merged.append(found[0])
+                    return tuple(merged)
+
+                floor = jnp.full((8, LANES), FLOOR, jnp.float32)
+                init = ((floor, jnp.zeros((8, LANES), jnp.int32), tiny),) * tiles
+                state = lax.fori_loop(0, rows // (8 * SCAN_ROWS), per_rows, init)
+                count = functools.reduce(jnp.maximum, [part[2] for part in state])
                 most = jnp.max(count)
 
                 @pl.when(most > 0.0)
                 def _():
-                    raise_tops([best], [storm])
+                    raise_tops([part[0] for part in state], [part[1] for part in state])
 
                 return most
 
@@ -313,6 +325,10 @@
         compiler_params=params(32),
     )(values, labels)
 
+def after(x, *others):
+    return lax.optimization_barrier((x, *others))[0]
+
+
 def local(vorticity, lat_order, storm_labels, storm_owner):
     field_count, lat_rows, lon_count = vorticity.shape
     lat_count = lat_order.shape[0]
@@ -327,19 +343,21 @@
     columns = 2 * field_count
     out_half = OUT_LAT // halves
 
-    parts = min(2, chunks)
-    calls = chunks // parts
-    table = fourier_table(lon_count).reshape(lon_count, calls, parts, GROUP, ranks, 2)
-    table = table.transpose(1, 0, 5, 2, 4, 3).reshape(calls, lon_count, 2 * MW // calls)
-    table = table.astype(jnp.bfloat16)
-
-    received = []
-    for c in range(calls):
-        for coefficients in fourier(vorticity, jnp.asarray(table[c]), ranks, parts):
-            received.append(
-                lax.all_to_all(coefficients, "rest", split_axis=0, concat_axis=0, tiled=True)
-            )
-
+    calls = [[16], [8, 8]] if slots == 32 else [[slots // 2], [slots // 2]]
+    full_table = fourier_table(lon_count).reshape(lon_count, slots, ranks, 2)
+    coefficients = []
+    first = 0
+    for part_slots in calls:
+        pieces = []
+        base = first
+        for n in part_slots:
+            pieces.append(full_table[:, base : base + n].transpose(0, 2, 1, 3).reshape(lon_count, -1, 2))
+            base += n
+        table = np.concatenate(pieces, axis=1).transpose(0, 2, 1).reshape(lon_count, -1)
+        table = jnp.asarray(table.astype(jnp.bfloat16))
+        coefficients += fourier(vorticity, table, ranks, part_slots)
+        first = base
+    stages = [n for part_slots in calls for n in part_slots]
     half_rows = ranks * lat_rows
     own_order = lax.dynamic_slice_in_dim(lat_order, half_index * half_rows, half_rows)
     colatitude = math.pi * (4.0 * own_order.astype(jnp.float32) + 3.0) / (4.0 * lat_count + 2.0)
@@ -354,33 +372,75 @@
     start_logs = lax.dynamic_slice_in_dim(start_logs, rank, 1, axis=1)
     orders = orders.astype(jnp.float32)[:, None]
     start = jnp.exp(start_logs + orders * jnp.log(sine_values)[None, :])
-    kernels = [
-        kernel_table(
-            orders[c * GROUP : (c + 1) * GROUP],
-            start[c * GROUP : (c + 1) * GROUP],
-            cosines[None, :],
-            weights[None, :],
-            OUT_LAT,
-            MW - c * GROUP * ranks,
-        )
-        for c in range(chunks)
-    ]
-
-    partial = [apply_table(kernels[c], received[c]) for c in range(chunks)]
+    def kernels(begin, end, token):
+        ordered = after(start, token)
+        return [
+            kernel_table(
+                orders[c * GROUP : (c + 1) * GROUP],
+                ordered[c * GROUP : (c + 1) * GROUP],
+                cosines[None, :],
+                weights[None, :],
+                OUT_LAT,
+                MW - c * GROUP * ranks,
+            )
+            for c in range(begin, end)
+        ]
+
+    def exchange(block):
+        return lax.all_to_all(block, "rest", split_axis=0, concat_axis=0, tiled=True)
+
+    def swapped(block):
+        return lax.ppermute(block, "half", [(0, 1), (1, 0)])
+
+    last_stage = len(stages) - 1
+    received = exchange(coefficients[0])
+    first = stages[0] // GROUP
+    tables = kernels(0, first, coefficients[-1][0, 0, 0, :1])
+    done_work = tuple(tables) + tuple(coefficients[1:])
+    bands = []
+    for i, n in enumerate(stages):
+        received = after(received, *done_work)
+        following = None
+        if i == 1 and i < last_stage:
+            received = after(received, early_swap)
+        if i < last_stage:
+            following = exchange(after(coefficients[i + 1], received))
+        own, other = apply_tables(tables, received)
+        cut = other.shape[0] // 2
+        if i == 0:
+            early_swap = swapped(other[:cut])
+            mirrored = jnp.concatenate([early_swap, swapped(other[cut:])])
+            later = kernels(first, slots // GROUP, other[0, :1])
+            done_work = (other, *later)
+        else:
+            mirrored = swapped(other)
+            done_work = (other, *bands)
+        taken = sum(stages[: i + 1]) // GROUP - first
+        if i < last_stage:
+            tables = later[taken : taken + stages[i + 1] // GROUP]
+        band = (own + mirrored.astype(jnp.float32)).astype(jnp.bfloat16)
+        bands.append(band.reshape(ranks, band_rows * n, columns))
+        last_received, received = received, following
+
+    early = jnp.concatenate(bands[:-1], axis=1)
+    early = exchange(after(early, last_received))
+    late = exchange(after(bands[-1], early))
+    early = early.reshape(ranks, -1, columns)
+    late = late.reshape(ranks, -1, columns)
     gathered = []
-    swap = [(0, 1), (1, 0)]
-    for own, other in partial:
-        mirrored = lax.ppermute(other, "half", swap)
-        band = (own + mirrored.astype(jnp.float32)).astype(jnp.bfloat16)
-        band = band.reshape(ranks, band_rows * GROUP, columns)
-        band = lax.all_to_all(band, "rest", split_axis=0, concat_axis=0, tiled=True)
-        gathered.append(band.reshape(ranks, band_rows, GROUP, 2, field_count))
-
-    gathered = jnp.stack(gathered)
-    synthesis = synthesis_table(OUT_LON).reshape(chunks, GROUP, ranks, 2, OUT_LON)
-    synthesis = jnp.asarray(synthesis.transpose(0, 2, 1, 3, 4).astype(jnp.bfloat16))
+    first = 0
+    for i, n in enumerate(stages):
+        block = late
+        if i < last_stage:
+            block = early[:, first : first + band_rows * n]
+            first += band_rows * n
+        gathered.append(block.reshape(ranks, band_rows, n, 2, field_count))
+
+    gathered = jnp.concatenate(gathered, axis=2)
+    synthesis = synthesis_table(OUT_LON).reshape(slots, ranks, 2, OUT_LON)
+    synthesis = jnp.asarray(synthesis.transpose(1, 0, 2, 3).astype(jnp.bfloat16))
     grid_values = jnp.einsum(
-        "cqosrf,cqsrl->fol", gathered, synthesis, preferred_element_type=jnp.float32
+        "qosrf,qsrl->fol", gathered, synthesis, preferred_element_type=jnp.float32
     )
     filtered = grid_values.astype(jnp.bfloat16)
     point_rows = field_count * band_rows

time: 208 us -> 186 us (0.89); the launches traced: 210 us -> 185 us
  blocking collectives: 44.3 us -> 0 us
  waiting for transfers between devices: 27.5 us -> 47.6 us
  local copies, waits for them, and re-layouts: 30.1 us -> 23.6 us
  Pallas kernels: 58.9 us -> 65.2 us
  other arithmetic: 5.96 us -> 2.93 us
  starting transfers between devices: 40.1 us -> 42.3 us
    all_to_all x2 -> x0, blocking collectives: 44.3 us -> none  [local(): lax.all_to_all(coefficients, 'rest', split_axis=0, concat_axis=0, tiled=T...]
    ppermute x4, waiting for transfers between devices: 15.3 us -> 30.4 us  [swapped(): return lax.ppermute(block, 'half', [(0, 1), (1, 0)])]
    pallas_call x6 -> x5, Pallas kernels: 30.1 us -> 36 us  [the longest x2 29.3 us: fourier(): pl.pallas_call(body, out_shape=[whole((senders, n, rows, 2 * fields), jnp...]
    unnamed x29 -> x33, local copies, waits for them, and re-layouts: 23.2 us -> 17.6 us
    all_to_all x6 -> x5, waiting for transfers between devices: 7.78 us -> 12.8 us  [exchange(): lax.all_to_all(block, 'rest', split_axis=0, concat_axis=0, tiled=True)]
    convert_element_type x4 -> x3, other arithmetic: 4.94 us -> 0.97 us  [local(): band = (own + mirrored.astype(jnp.float32)).astype(jnp.bfloat16)]
    another operation x8 -> x0, local copies, waits for them, and re-layouts: 3.1 us -> none  [local(): gathered = jnp.stack(gathered)]
    reshape x0 -> x6, local copies, waits for them, and re-layouts: none -> 2.26 us  [local(): gathered.append(block.reshape(ranks, band_rows, n, 2, field_count))]
  transfers between devices with their start and end apart: 11 -> 10, of which waited for: 6 -> 8; matrix products, arithmetic and copies ran while one was open for 5% -> 4% of each run, Pallas kernels for 17% -> 21%
where the time goes in v3:
time: 186 us; the launch traced here: 185 us
  Pallas kernels  65.2 us (35%)
  waiting for transfers between devices  47.6 us (26%)
  starting transfers between devices  42.3 us (23%)
  local copies, waits for them, and re-layouts  23.6 us (13%)
  other arithmetic  2.93 us (2%)
  matrix products  2.18 us (1%)
    ppermute x4, waiting for transfers between devices, swapped(): return lax.ppermute(block, 'half', [(0, 1), (1, 0)])  30.4 us
    pallas_call x2, Pallas kernels, fourier(): pl.pallas_call(body, out_shape=[whole((senders, n, rows, 2 * fields), jnp...  29.3 us
    all_to_all x5, starting transfers between devices, exchange(): lax.all_to_all(block, 'rest', split_axis=0, concat_axis=0, tiled=True)  23.1 us
    pallas_call x4, Pallas kernels, kernel_table(): pl.pallas_call(body, out_shape=whole((GROUP, out_rows, in_rows), jnp.bflo...  17.7 us
    unnamed x33, local copies, waits for them, and re-layouts  17.6 us
    all_to_all x5, waiting for transfers between devices, exchange(): lax.all_to_all(block, 'rest', split_axis=0, concat_axis=0, tiled=True)  12.8 us
    all_to_all x1, starting transfers between devices, local(): lax.all_to_all(by_slot.reshape(spec_count, storm_count // spec_count), ('...  11.6 us
    pallas_call x1, Pallas kernels, storm_maxima(): pl.pallas_call(body, out_shape=jax.ShapeDtypeStruct((1, storm_count), jnp...  11.4 us
  transfers between devices with their start and end apart: 10, of which 8 were waited for; matrix products, arithmetic and copies ran while one was open for 4% of the time, Pallas kernels for 21%

profile of v3, /device:TPU:0, one launch (start us, length us, event | category | flops | bytes accessed | tf_op | source)
XLA Modules:
  0.0 184.6 jit_solution(6030576250392296225)
XLA Ops:
  0.6 1.3 copy-done.7
  1.9 15.2 %shard_map.97 = bf16[8,16,80,128]{3,2,1,0:T(8,128)(2,1)} custom-call(bf16[64,80,2560]{2,1,0:T(8,128)(2,1)} %data_ref.3, bf16[2560,256]{1,0:T(8,128)(2,1)S(1)} %copy-done.7), custom_call_target="tpu_custom_call" | custom-call | tf_op jit(solution)/shard_map/pallas_call | solution.py:80
  17.1 5.4 %all-to-all-start = ((bf16[8,16,80,128]{3,2,1,0:T(8,128)(2,1)}), bf16[8,16,80,128]{3,2,1,0:T(8,128)(2,1)S(1)}, u32[]{:S(2)}, u32[]{:S(2)}) async-start(bf16[8,16,80,128]{3,2,1,0:T(8,128)(2,1)} %shard_map.97), calls=%async_computation | async-start | bytes 5242880 | tf_op jit(solution)/shard_map/all_to_all | solution.py:390
  22.5 0.7 dynamic-slice_bitcast_fusion
  23.2 0.1 fusion.15
  23.3 0.1 broadcast_multiply_fusion
  23.5 0.1 add_exponential_fusion
  23.6 0.1 slice_bitcast_fusion.1
  23.7 0.1 copy.34.order_ref
  23.7 0.1 copy.35.order_ref
  23.8 1.3 copy-done.10
  25.1 14.2 %shard_map.98 = (bf16[8,8,80,128]{3,2,1,0:T(8,128)(2,1)S(1)}, bf16[8,8,80,128]{3,2,1,0:T(8,128)(2,1)S(1)}) custom-call(bf16[64,80,2560]{2,1,0:T(8,128)(2,1)} %data_ref.3, bf16[2560,256]{1,0:T(8,128)(2,1)S(1)} %copy-done.10), custom_call_target="tpu_custom_call" | custom-call | tf_op jit(solution)/shard_map/pallas_call | solution.py:80
  39.3 1.0 copy-done.8
  40.4 1.1 copy-done.9
  41.6 6.8 %shard_map.95.refs_0_ = bf16[8,256,640]{2,1,0:T(8,128)(2,1)S(1)} custom-call(f32[8,1]{1,0:T(8,128)S(1)} %copy.34.order_ref, f32[8,896]{1,0:T(8,128)S(1)} %get-tuple-element.49.start_ref, f32[1,896]{1,0:T(1,128)S(1)} %broadcast_in_dim.14.cos_ref, f32[1,640]{1,0:T(1,128)S(1)} %broadcast_in_dim.15.weight_ref), custom_call_target="tpu_custom_call" | custom-call | tf_op jit(solution)/shard_map/pallas_call | solution.py:159
  48.3 1.5 copy-done.2
  49.8 5.4 %shard_map.96.refs_1_ = bf16[8,256,640]{2,1,0:T(8,128)(2,1)S(1)} custom-call(f32[8,1]{1,0:T(8,128)S(1)} %copy.35.order_ref, f32[8,896]{1,0:T(8,128)S(1)} %get-tuple-element.48.start_ref, f32[1,896]{1,0:T(1,128)S(1)} %broadcast_in_dim.14.cos_ref, f32[1,640]{1,0:T(1,128)S(1)} %broadcast_in_dim.15.weight_ref), custom_call_target="tpu_custom_call" | custom-call | tf_op jit(solution)/shard_map/pallas_call | solution.py:159
  55.3 1.5 copy-done.4
  56.8 4.5 %all-to-all-start.1 = ((bf16[8,8,80,128]{3,2,1,0:T(8,128)(2,1)}), bf16[8,8,80,128]{3,2,1,0:T(8,128)(2,1)}, u32[]{:S(2)}, u32[]{:S(2)}) async-start(bf16[8,8,80,128]{3,2,1,0:T(8,128)(2,1)} %copy-done.9), calls=%async_computation.1 | async-start | bytes 2621440 | tf_op jit(solution)/shard_map/all_to_all | solution.py:390
  61.3 1.7 copy-done.3
  63.0 1.7 copy-done.5
  64.7 2.1 %shard_map.99 = (f32[2048,128]{1,0:T(8,128)S(1)}, bf16[2048,128]{1,0:T(8,128)(2,1)S(1)}) custom-call(bf16[8,256,640]{2,1,0:T(8,128)(2,1)S(1)} %copy-done.3, bf16[8,256,640]{2,1,0:T(8,128)(2,1)S(1)} %copy-done.5, bf16[8,16,80,128]{3,2,1,0:T(8,128)(2,1)S(1)} %all-to-all-done.refs_2_), custom_call_target="tpu_custom_call" | custom-call | tf_op jit(solution)/shard_map/pallas_call | solution.py:184
  66.9 1.0 copy-done.11
  67.9 2.7 %collective-permute-start = (bf16[1024,128]{1,0:T(8,128)(2,1)S(1)}, bf16[1024,128]{1,0:T(8,128)(2,1)S(1)}, u32[]{:S(2)}, u32[]{:S(2)}) collective-permute-start(bf16[1024,128]{1,0:T(8,128)(2,1)S(1)} %get-tuple-element.45), channel_id=1, source_target_pairs={{0,8},{8,0},{1,9},{9,1},{2,10},{10,2},{3,11},{11,3},{4,12},{12,4},... | collective-permute-start | bytes 786440 | tf_op jit(solution)/shard_map/ppermute | solution.py:393
  70.6 0.1 copy.36.order_ref
  70.7 0.1 copy.37.order_ref
  70.7 3.6 %shard_map.100.refs_0_ = bf16[8,256,640]{2,1,0:T(8,128)(2,1)S(1)} custom-call(f32[8,1]{1,0:T(8,128)S(1)} %copy.36.order_ref, f32[8,896]{1,0:T(8,128)S(1)} %get-tuple-element.46.start_ref, f32[1,896]{1,0:T(1,128)S(1)} %broadcast_in_dim.14.cos_ref, f32[1,640]{1,0:T(1,128)S(1)} %broadcast_in_dim.15.weight_ref), custom_call_target="tpu_custom_call" | custom-call | tf_op jit(solution)/shard_map/pallas_call | solution.py:159
  74.4 1.5 copy-done
  75.9 1.9 %shard_map.101.refs_0_ = bf16[8,256,640]{2,1,0:T(8,128)(2,1)S(1)} custom-call(f32[8,1]{1,0:T(8,128)S(1)} %copy.37.order_ref, f32[8,896]{1,0:T(8,128)S(1)} %get-tuple-element.47.start_ref, f32[1,896]{1,0:T(1,128)S(1)} %broadcast_in_dim.14.cos_ref, f32[1,640]{1,0:T(1,128)S(1)} %broadcast_in_dim.15.weight_ref), custom_call_target="tpu_custom_call" | custom-call | tf_op jit(solution)/shard_map/pallas_call | solution.py:159
  77.8 6.3 %all-to-all-done.1.refs_1_ = bf16[8,8,80,128]{3,2,1,0:T(8,128)(2,1)} async-done(((bf16[8,8,80,128]{3,2,1,0:T(8,128)(2,1)}), bf16[8,8,80,128]{3,2,1,0:T(8,128)(2,1)}, u32[]{:S(2)}, u32[]{:S(2)}) %all-to-all-start.1) | async-done | bytes 1310752 | tf_op jit(solution)/shard_map/all_to_all | solution.py:390
  84.1 4.6 %all-to-all-start.2 = ((bf16[8,8,80,128]{3,2,1,0:T(8,128)(2,1)}), bf16[8,8,80,128]{3,2,1,0:T(8,128)(2,1)}, u32[]{:S(2)}, u32[]{:S(2)}) async-start(bf16[8,8,80,128]{3,2,1,0:T(8,128)(2,1)} %copy-done.8), calls=%async_computation.2 | async-start | bytes 2621440 | tf_op jit(solution)/shard_map/all_to_all | solution.py:390
  88.8 1.0 collective-permute-start.1
  89.8 1.7 copy-done.1
  91.5 2.3 %shard_map.102 = (f32[1024,128]{1,0:T(8,128)S(1)}, bf16[1024,128]{1,0:T(8,128)(2,1)S(1)}) custom-call(bf16[8,256,640]{2,1,0:T(8,128)(2,1)S(1)} %copy-done.1, bf16[8,8,80,128]{3,2,1,0:T(8,128)(2,1)} %all-to-all-done.1.refs_1_), custom_call_target="tpu_custom_call" | custom-call | tf_op jit(solution)/shard_map/pallas_call | solution.py:184
  93.8 2.0 %collective-permute-start.2 = (bf16[1024,128]{1,0:T(8,128)(2,1)S(1)}, bf16[1024,128]{1,0:T(8,128)(2,1)S(1)}, u32[]{:S(2)}, u32[]{:S(2)}) collective-permute-start(bf16[1024,128]{1,0:T(8,128)(2,1)S(1)} %get-tuple-element.27), channel_id=1, source_target_pairs={{0,8},{8,0},{1,9},{9,1},{2,10},{10,2},{3,11},{11,3},{4,12},{12,4},... | collective-permute-start | bytes 786440 | tf_op jit(solution)/shard_map/ppermute | solution.py:393
  95.8 13.9 %collective-permute-done.1 = bf16[1024,128]{1,0:T(8,128)(2,1)S(1)} collective-permute-done((bf16[1024,128]{1,0:T(8,128)(2,1)S(1)}, bf16[1024,128]{1,0:T(8,128)(2,1)S(1)}, u32[]{:S(2)}, u32[]{:S(2)}) %collective-permute-start.1) | collective-permute-done | bytes 262176 | tf_op jit(solution)/shard_map/ppermute | solution.py:393
  109.8 0.1 add_convert_fusion
  109.9 5.3 %collective-permute-done.2 = bf16[1024,128]{1,0:T(8,128)(2,1)S(1)} collective-permute-done((bf16[1024,128]{1,0:T(8,128)(2,1)S(1)}, bf16[1024,128]{1,0:T(8,128)(2,1)S(1)}, u32[]{:S(2)}, u32[]{:S(2)}) %collective-permute-start.2) | collective-permute-done | bytes 262176 | tf_op jit(solution)/shard_map/ppermute | solution.py:393
  115.2 0.1 add_convert_fusion.2
  115.3 0.9 pad_maximum_fusion
  116.2 1.2 all-to-all-done.2.refs_1_
  117.4 3.9 %all-to-all-start.3 = ((bf16[8,384,128]{2,1,0:T(8,128)(2,1)}), bf16[8,384,128]{2,1,0:T(8,128)(2,1)S(1)}, u32[]{:S(2)}, u32[]{:S(2)}) async-start(bf16[8,384,128]{2,1,0:T(8,128)(2,1)} %pad_maximum_fusion), calls=%async_computation.3 | async-start | bytes 1572864 | tf_op jit(solution)/shard_map/all_to_all | solution.py:390
  121.3 2.2 %shard_map.103 = (f32[1024,128]{1,0:T(8,128)S(1)}, bf16[1024,128]{1,0:T(8,128)(2,1)S(1)}) custom-call(bf16[8,256,640]{2,1,0:T(8,128)(2,1)S(1)} %shard_map.101.refs_0_, bf16[8,8,80,128]{3,2,1,0:T(8,128)(2,1)} %all-to-all-done.2.refs_1_), custom_call_target="tpu_custom_call" | custom-call | tf_op jit(solution)/shard_map/pallas_call | solution.py:184
  123.5 1.9 %collective-permute-start.3 = (bf16[1024,128]{1,0:T(8,128)(2,1)S(1)}, bf16[1024,128]{1,0:T(8,128)(2,1)S(1)}, u32[]{:S(2)}, u32[]{:S(2)}) collective-permute-start(bf16[1024,128]{1,0:T(8,128)(2,1)S(1)} %get-tuple-element.32), channel_id=1, source_target_pairs={{0,8},{8,0},{1,9},{9,1},{2,10},{10,2},{3,11},{11,3},{4,12},{12,4},... | collective-permute-start | bytes 786440 | tf_op jit(solution)/shard_map/ppermute | solution.py:393
  125.4 11.1 %collective-permute-done.3 = bf16[1024,128]{1,0:T(8,128)(2,1)S(1)} collective-permute-done((bf16[1024,128]{1,0:T(8,128)(2,1)S(1)}, bf16[1024,128]{1,0:T(8,128)(2,1)S(1)}, u32[]{:S(2)}, u32[]{:S(2)}) %collective-permute-start.3) | collective-permute-done | bytes 262176 | tf_op jit(solution)/shard_map/ppermute | solution.py:393
  136.5 0.8 add_convert_fusion.1
  137.3 1.2 all-to-all-done.3
  138.6 4.7 %all-to-all-start.4 = ((bf16[8,128,128]{2,1,0:T(8,128)(2,1)}), bf16[8,128,128]{2,1,0:T(8,128)(2,1)S(1)}, u32[]{:S(2)}, u32[]{:S(2)}) async-start(bf16[8,128,128]{2,1,0:T(8,128)(2,1)} %bitcast.7), calls=%async_computation.4 | async-start | bytes 524288 | tf_op jit(solution)/shard_map/all_to_all | solution.py:390
  143.4 0.4 reshape.60
  143.8 1.2 copy.38
  145.0 0.2 reshape.61
  145.2 0.1 copy.39
  145.3 4.0 %all-to-all-done.4 = bf16[8,128,128]{2,1,0:T(8,128)(2,1)S(1)} async-done(((bf16[8,128,128]{2,1,0:T(8,128)(2,1)}), bf16[8,128,128]{2,1,0:T(8,128)(2,1)S(1)}, u32[]{:S(2)}, u32[]{:S(2)}) %all-to-all-start.4) | async-done | bytes 262176 | tf_op jit(solution)/shard_map/all_to_all | solution.py:390
  149.4 0.2 reshape.63
  149.6 0.1 copy.40
  149.7 2.2 %fusion.21 = (bf16[64,16,720]{2,0,1:T(8,128)(2,1)S(1)}, f32[64,16,720]{2,0,1:T(8,128)S(1)}) fusion(bf16[8,32,2,720,1]{3,1,2,4,0:T(8,128)(2,1)} %constant.67, bf16[8,16,8,2,64]{4,2,3,1,0:T(8,128)(2,1)S(1)} %copy.40, bf16[8,16,8,2,64]{4,2,3,1,0:T(8,128)(2,1)S(1)} %copy.39, bf16[8,16,16,2,64]{4,2,3,1,0:T(8,128)(2,1)S(1)} %copy-done.13), kind=kOutput, calls=%fused_computation.38 | convolution fusion | flops 758857728 | bytes 6209536 | tf_op jit(solution)/shard_map/qosrf,qsrl->fol/dot_general | solution.py:442
  151.9 1.8 copy.41
  153.8 11.4 %shard_map.104 = f32[1,256]{1,0:T(1,128)S(1)} custom-call(f32[1024,720]{1,0:T(8,128)S(1)} %bitcast.27, s32[1024,720]{1,0:T(8,128)S(1)} %bitcast.28), custom_call_target="tpu_custom_call" | custom-call | tf_op jit(solution)/shard_map/pallas_call | solution.py:309
  165.2 0.1 select_reduce_fusion
  165.4 0.7 all_to_all.26
  166.1 11.6 %all-to-all-start.5 = ((f32[16,1,16]{2,1,0:T(1,128)}), f32[16,1,16]{2,1,0:T(1,128)S(1)}, u32[]{:S(2)}, u32[]{:S(2)}) async-start(f32[16,1,16]{2,1,0:T(1,128)} %all_to_all.26), calls=%async_computation.5 | async-start | bytes 16384 | tf_op jit(solution)/shard_map/all_to_all | solution.py:457
  177.7 2.0 %copy.43 = bf16[64,16,720]{2,1,0:T(8,128)(2,1)} copy(bf16[64,16,720]{2,0,1:T(8,128)(2,1)S(1)} %get-tuple-element.55) | data formatting | bytes 2949120
  179.7 4.4 %all-to-all-done.5 = f32[16,1,16]{2,1,0:T(1,128)S(1)} async-done(((f32[16,1,16]{2,1,0:T(1,128)}), f32[16,1,16]{2,1,0:T(1,128)S(1)}, u32[]{:S(2)}, u32[]{:S(2)}) %all-to-all-start.5) | async-done | bytes 1056 | tf_op jit(solution)/shard_map/all_to_all | solution.py:457
  184.1 0.5 reduce_max.19
  (32 shorter events, 0.3 us)
Async XLA Ops:
  0.6 1.3 copy-start.7
  17.1 6.2 %copy-start.14 = (s32[1280]{0:T(1024)S(1)}, s32[1280]{0:T(1024)}, u32[]{:S(2)}) copy-start(s32[1280]{0:T(1024)} %param.9) | copy-start | bytes 15364
  17.1 39.7 %all-to-all-start = ((bf16[8,16,80,128]{3,2,1,0:T(8,128)(2,1)}), bf16[8,16,80,128]{3,2,1,0:T(8,128)(2,1)S(1)}, u32[]{:S(2)}, u32[]{:S(2)}) async-start(bf16[8,16,80,128]{3,2,1,0:T(8,128)(2,1)} %shard_map.97), calls=%async_computation | async-start | bytes 5242880 | tf_op jit(solution)/shard_map/all_to_all | solution.py:390
  23.8 1.3 copy-start.10
  39.3 1.1 copy-start.8
  40.4 1.2 copy-start.9
  48.3 1.5 copy-start.2
  55.2 1.5 copy-start.4
  56.8 27.3 %all-to-all-start.1 = ((bf16[8,8,80,128]{3,2,1,0:T(8,128)(2,1)}), bf16[8,8,80,128]{3,2,1,0:T(8,128)(2,1)}, u32[]{:S(2)}, u32[]{:S(2)}) async-start(bf16[8,8,80,128]{3,2,1,0:T(8,128)(2,1)} %copy-done.9), calls=%async_computation.1 | async-start | bytes 2621440 | tf_op jit(solution)/shard_map/all_to_all | solution.py:390
  61.3 1.7 copy-start.3
  63.0 1.7 copy-start.5
  66.9 1.0 copy-start.11
  67.9 16.2 %collective-permute-start = (bf16[1024,128]{1,0:T(8,128)(2,1)S(1)}, bf16[1024,128]{1,0:T(8,128)(2,1)S(1)}, u32[]{:S(2)}, u32[]{:S(2)}) collective-permute-start(bf16[1024,128]{1,0:T(8,128)(2,1)S(1)} %get-tuple-element.45), channel_id=1, source_target_pairs={{0,8},{8,0},{1,9},{9,1},{2,10},{10,2},{3,11},{11,3},{4,12},{12,4},... | collective-permute-start | bytes 786440 | tf_op jit(solution)/shard_map/ppermute | solution.py:393
  74.4 1.5 copy-start
  84.1 33.2 %all-to-all-start.2 = ((bf16[8,8,80,128]{3,2,1,0:T(8,128)(2,1)}), bf16[8,8,80,128]{3,2,1,0:T(8,128)(2,1)}, u32[]{:S(2)}, u32[]{:S(2)}) async-start(bf16[8,8,80,128]{3,2,1,0:T(8,128)(2,1)} %copy-done.8), calls=%async_computation.2 | async-start | bytes 2621440 | tf_op jit(solution)/shard_map/all_to_all | solution.py:390
  88.8 21.0 %collective-permute-start.1 = (bf16[1024,128]{1,0:T(8,128)(2,1)S(1)}, bf16[1024,128]{1,0:T(8,128)(2,1)S(1)}, u32[]{:S(2)}, u32[]{:S(2)}) collective-permute-start(bf16[1024,128]{1,0:T(8,128)(2,1)S(1)} %get-tuple-element.44), channel_id=1, source_target_pairs={{0,8},{8,0},{1,9},{9,1},{2,10},{10,2},{3,11},{11,3},{4,12},{12,4},... | collective-permute-start | bytes 786440 | tf_op jit(solution)/shard_map/ppermute | solution.py:393
  89.8 1.7 copy-start.1
  91.5 18.3 %copy-start.12 = (f32[2048,128]{1,0:T(8,128)S(1)}, f32[2048,128]{1,0:T(8,128)}, u32[]{:S(2)}) copy-start(f32[2048,128]{1,0:T(8,128)} %copy-done.11) | copy-start | bytes 3145732
  93.8 21.4 %collective-permute-start.2 = (bf16[1024,128]{1,0:T(8,128)(2,1)S(1)}, bf16[1024,128]{1,0:T(8,128)(2,1)S(1)}, u32[]{:S(2)}, u32[]{:S(2)}) collective-permute-start(bf16[1024,128]{1,0:T(8,128)(2,1)S(1)} %get-tuple-element.27), channel_id=1, source_target_pairs={{0,8},{8,0},{1,9},{9,1},{2,10},{10,2},{3,11},{11,3},{4,12},{12,4},... | collective-permute-start | bytes 786440 | tf_op jit(solution)/shard_map/ppermute | solution.py:393
  117.4 21.2 %all-to-all-start.3 = ((bf16[8,384,128]{2,1,0:T(8,128)(2,1)}), bf16[8,384,128]{2,1,0:T(8,128)(2,1)S(1)}, u32[]{:S(2)}, u32[]{:S(2)}) async-start(bf16[8,384,128]{2,1,0:T(8,128)(2,1)} %pad_maximum_fusion), calls=%async_computation.3 | async-start | bytes 1572864 | tf_op jit(solution)/shard_map/all_to_all | solution.py:390
  123.5 13.0 %collective-permute-start.3 = (bf16[1024,128]{1,0:T(8,128)(2,1)S(1)}, bf16[1024,128]{1,0:T(8,128)(2,1)S(1)}, u32[]{:S(2)}, u32[]{:S(2)}) collective-permute-start(bf16[1024,128]{1,0:T(8,128)(2,1)S(1)} %get-tuple-element.32), channel_id=1, source_target_pairs={{0,8},{8,0},{1,9},{9,1},{2,10},{10,2},{3,11},{11,3},{4,12},{12,4},... | collective-permute-start | bytes 786440 | tf_op jit(solution)/shard_map/ppermute | solution.py:393
  138.6 10.8 %all-to-all-start.4 = ((bf16[8,128,128]{2,1,0:T(8,128)(2,1)}), bf16[8,128,128]{2,1,0:T(8,128)(2,1)S(1)}, u32[]{:S(2)}, u32[]{:S(2)}) async-start(bf16[8,128,128]{2,1,0:T(8,128)(2,1)} %bitcast.7), calls=%async_computation.4 | async-start | bytes 524288 | tf_op jit(solution)/shard_map/all_to_all | solution.py:390
  145.0 4.7 %copy-start.13 = (bf16[8,16,16,2,64]{4,2,3,1,0:T(8,128)(2,1)S(1)}, bf16[8,16,16,2,64]{4,2,3,1,0:T(8,128)(2,1)}, u32[]{:S(2)}) copy-start(bf16[8,16,16,2,64]{4,2,3,1,0:T(8,128)(2,1)} %copy.38) | copy-start | bytes 1572868
  151.9 1.9 %copy-start.6 = (s32[64,16,720]{2,1,0:T(8,128)S(1)}, s32[64,16,720]{2,1,0:T(8,128)}, u32[]{:S(2)}) copy-start(s32[64,16,720]{2,1,0:T(8,128)} %param.10) | copy-start | bytes 8847364
  153.8 11.4 %copy-start.15 = (s32[256]{0:T(256)S(1)}, s32[256]{0:T(256)}, u32[]{:S(2)}) copy-start(s32[256]{0:T(256)} %param.11) | copy-start | bytes 3076
  166.1 18.0 %all-to-all-start.5 = ((f32[16,1,16]{2,1,0:T(1,128)}), f32[16,1,16]{2,1,0:T(1,128)S(1)}, u32[]{:S(2)}, u32[]{:S(2)}) async-start(f32[16,1,16]{2,1,0:T(1,128)} %all_to_all.26), calls=%async_computation.5 | async-start | bytes 16384 | tf_op jit(solution)/shard_map/all_to_all | solution.py:457

commit v4 on v3

v4 whole, which is shorter than its diff:
```python
import functools
import math

import jax
import jax.numpy as jnp
import numpy as np
from jax import lax
from jax.experimental import pallas as pl
from jax.experimental.pallas import tpu as pltpu
from jax.sharding import Mesh
from jax.sharding import PartitionSpec as P

MW = 256
OUT_LAT = 256
OUT_LON = 720
FLOOR = -1e30
GROUP = 8
LANES = 128
SCAN_ROWS = 4


def fourier_table(lon_count):
    steps = np.arange(lon_count)[:, None] * np.arange(MW)[None, :] % lon_count
    angles = steps * (2.0 * math.pi / lon_count)
    return np.stack([np.cos(angles), -np.sin(angles)], axis=-1) / lon_count


def synthesis_table(lon_count):
    steps = np.arange(MW)[:, None] * np.arange(lon_count)[None, :] % lon_count
    angles = steps * (2.0 * math.pi / lon_count)
    factor = np.where(np.arange(MW) == 0, 1.0, 2.0)[:, None]
    return np.stack([factor * np.cos(angles), -factor * np.sin(angles)], axis=1)


def diagonal_logs():
    counters = np.arange(1, MW, dtype=np.float64)
    increments = np.log((2.0 * counters + 1.0) / (2.0 * counters))
    sums = np.concatenate([[0.0], np.cumsum(increments)])
    return (0.5 * math.log(0.5) + 0.5 * sums).astype(np.float32)


def params(mebibytes):
    return pltpu.CompilerParams(vmem_limit_bytes=mebibytes << 20)


def whole(shape, dtype):
    return jax.ShapeDtypeStruct(shape, dtype)


IN_VMEM = pl.BlockSpec(memory_space=pltpu.VMEM)


def fourier(vorticity, table, senders, part_slots):
    fields, rows, lon_count = vorticity.shape
    waves = table.shape[1] // 2
    block = 16 if rows % 16 == 0 else 8
    parts = len(part_slots)

    def body(data_ref, table_ref, *refs):
        out_refs, (product_ref, turned_ref) = refs[:parts], refs[parts:]
        data = data_ref[...].reshape(fields * block, lon_count)
        product = jnp.dot(data, table_ref[...], preferred_element_type=jnp.float32)
        for t in range(2 * waves // LANES):
            product_ref[t] = product[:, t * LANES : (t + 1) * LANES]
        for j in range(block):
            for t in range(waves // LANES):
                pair = [
                    product_ref[r * (waves // LANES) + t, pl.ds(j, fields, stride=block), :]
                    for r in range(2)
                ]
                start = t * LANES * block + j
                turned_ref[pl.ds(start, LANES, stride=block), :] = jnp.concatenate(pair, axis=0).T
        start = 0
        for p in range(parts):
            size = senders * part_slots[p] * block
            part = turned_ref[start : start + size, :]
            out_refs[p][...] = part.astype(jnp.bfloat16).reshape(out_refs[p].shape)
            start += size

    return pl.pallas_call(
        body,
        out_shape=[whole((senders, n, rows, 2 * fields), jnp.bfloat16) for n in part_slots],
        grid=(rows // block,),
        in_specs=[
            pl.BlockSpec((fields, block, lon_count), lambda i: (0, i, 0)),
            pl.BlockSpec(table.shape, lambda i: (0, 0), pipeline_mode=pl.Buffered(1)),
        ],
        out_specs=[
            pl.BlockSpec((senders, n, block, 2 * fields), lambda i: (0, 0, i, 0)) for n in part_slots
        ],
        scratch_shapes=[
            pltpu.VMEM((2 * waves // LANES, fields * block, LANES), jnp.float32),
            pltpu.VMEM((waves * block, 2 * fields), jnp.float32),
        ],
        compiler_params=params(20),
    )(pltpu.with_memory_space_constraint(vorticity, pltpu.HBM), table)


def halves_of(x):
    high = x.astype(jnp.bfloat16)
    return high, (x - high.astype(jnp.float32)).astype(jnp.bfloat16)


def kernel_table(orders, start, cosines, weights, out_rows, offsets, split_rows):
    columns = start.shape[1]
    in_rows = columns - out_rows
    tiles = columns // LANES
    out_tiles = out_rows // LANES

    def body(order_ref, start_ref, cos_ref, weight_ref, *refs):
        out_refs, table_ref = refs[:-1], refs[-1]
        m = jnp.broadcast_to(order_ref[...], (GROUP, LANES))
        cosine = [
            jnp.broadcast_to(cos_ref[:, t * LANES : (t + 1) * LANES], (GROUP, LANES))
            for t in range(tiles)
        ]

        def step(k, carry):
            previous, earlier = carry
            offset = k.astype(jnp.float32)
            degree = m + offset
            below = degree - 1.0
            first = jnp.sqrt((4.0 * degree * degree - 1.0) / (offset * (2.0 * m + offset)))
            second = jnp.sqrt(
                (offset - 1.0)
                * (2.0 * m + offset - 1.0)
                / jnp.maximum(4.0 * below * below - 1.0, 1.0)
            )
            keep = degree <= MW - 1.0
            row = pl.multiple_of(k * GROUP, GROUP)
            current = []
            for t in range(tiles):
                value = first * (cosine[t] * previous[t] - second * earlier[t])
                current.append(value)
                stored = jnp.where(keep, value, 0.0) if t < out_tiles else value
                table_ref[t, pl.ds(row, GROUP), :] = stored
            return (tuple(current), previous)

        first_rows = tuple(start_ref[:, t * LANES : (t + 1) * LANES] for t in range(tiles))
        for t in range(tiles):
            table_ref[t, 0:GROUP, :] = first_rows[t]
        zeros = tuple(jnp.zeros((GROUP, LANES), jnp.float32) for _ in range(tiles))
        first_step = step(jnp.int32(1), (first_rows, zeros))
        second_step = step(jnp.int32(2), first_step)
        third_step = step(jnp.int32(3), second_step)
        lax.fori_loop(4, offsets, step, third_step, unroll=4)
        weight = weight_ref[...]
        for s in range(GROUP):
            values = [table_ref[t, pl.ds(s, offsets, stride=GROUP), :] for t in range(tiles)]
            if split_rows:
                inward = jnp.concatenate(values[out_tiles:], axis=1) * weight
                out_refs[0][s] = inward.astype(jnp.bfloat16)
                outward = jnp.concatenate(values[: split_rows // LANES], axis=1)
                out_refs[1][s] = outward.T.astype(jnp.bfloat16)
                continue
            out_high, out_low = halves_of(jnp.concatenate(values[:out_tiles], axis=1))
            in_high, in_low = halves_of(jnp.concatenate(values[out_tiles:], axis=1))
            product = lax.dot_general(
                jnp.concatenate([out_high, out_high, out_low], axis=0),
                jnp.concatenate([in_high, in_low, in_high], axis=0),
                (((0,), (0,)), ((), ())),
                preferred_element_type=jnp.float32,
            )
            out_refs[0][s] = (product * weight).astype(jnp.bfloat16)

    out_shape = [whole((GROUP, out_rows, in_rows), jnp.bfloat16)]
    if split_rows:
        out_shape = [
            whole((GROUP, offsets, in_rows), jnp.bfloat16),
            whole((GROUP, split_rows, offsets), jnp.bfloat16),
        ]
    return pl.pallas_call(
        body,
        out_shape=out_shape,
        in_specs=[IN_VMEM] * 4,
        out_specs=[IN_VMEM] * len(out_shape),
        scratch_shapes=[pltpu.VMEM((tiles, offsets * GROUP, LANES), jnp.float32)],
        compiler_params=params(14),
    )(orders, start, cosines, weights)


def apply_table(table, received, first):
    senders, _, rows, columns = received.shape
    slots, out_rows, _ = table.shape
    half = out_rows // 2

    def body(table_ref, data_ref, own_ref, other_ref, wide_ref):
        for s in range(slots):
            data = data_ref[:, first + s].reshape(senders * rows, columns)
            product = jnp.dot(table_ref[s], data, preferred_element_type=jnp.float32)
            own_ref[pl.ds(s, half, stride=slots), :] = product[:half]
            wide_ref[pl.ds(s, half, stride=slots), :] = product[half:]
        other_ref[...] = wide_ref[...].astype(jnp.bfloat16)

    return pl.pallas_call(
        body,
        out_shape=(
            whole((half * slots, columns), jnp.float32),
            whole((half * slots, columns), jnp.bfloat16),
        ),
        in_specs=[IN_VMEM] * 2,
        out_specs=(IN_VMEM, IN_VMEM),
        scratch_shapes=[pltpu.VMEM((half * slots, columns), jnp.float32)],
        compiler_params=params(6),
    )(table, received)


def slot_rows(offsets, ranks):
    return [offsets - s * ranks for s in range(GROUP)]


def spectral_part(analysis, received, ranks):
    senders, _, rows, columns = received.shape
    kept = slot_rows(analysis.shape[1], ranks)

    def body(table_ref, data_ref, own_ref, other_ref):
        parts = []
        for s in range(GROUP):
            data = data_ref[:, s].reshape(senders * rows, columns)
            product = jnp.dot(table_ref[s], data, preferred_element_type=jnp.float32)
            parts.append(product[: kept[s]])
        spectral = jnp.concatenate(parts, axis=0)
        own_ref[...] = spectral
        other_ref[...] = spectral.astype(jnp.bfloat16)

    shape = (sum(kept), columns)
    return pl.pallas_call(
        body,
        out_shape=(whole(shape, jnp.float32), whole(shape, jnp.bfloat16)),
        in_specs=[IN_VMEM] * 2,
        out_specs=[IN_VMEM] * 2,
        compiler_params=params(6),
    )(analysis, received)


def spectral_band(evaluation, own, mirrored, ranks):
    _, half, offsets = evaluation.shape
    columns = own.shape[1]
    kept = slot_rows(offsets, ranks)

    def body(table_ref, own_ref, mirrored_ref, out_ref, wide_ref):
        spectral = own_ref[...] + mirrored_ref[...].astype(jnp.float32)
        start = 0
        for s in range(GROUP):
            rows = spectral[start : start + kept[s]].astype(jnp.bfloat16)
            start += kept[s]
            product = jnp.dot(table_ref[s, :, : kept[s]], rows, preferred_element_type=jnp.float32)
            wide_ref[pl.ds(s, half, stride=GROUP), :] = product
        out_ref[...] = wide_ref[...].astype(jnp.bfloat16)

    return pl.pallas_call(
        body,
        out_shape=whole((half * GROUP, columns), jnp.bfloat16),
        in_specs=[IN_VMEM] * 3,
        out_specs=IN_VMEM,
        scratch_shapes=[pltpu.VMEM((half * GROUP, columns), jnp.float32)],
        compiler_params=params(6),
    )(evaluation, own, mirrored)


def grid_maxima(early, late, synthesis, labels, band_rows, fields, storm_count):
    ranks, early_rows, columns = early.shape
    rows, lon_count = labels.shape
    early_groups = early_rows // (band_rows * GROUP)
    groups = early_groups + 1
    waves = ranks * groups * GROUP
    wave_tiles = waves // LANES
    tiles = synthesis.shape[1] // LANES
    tail = lon_count - (tiles - 1) * LANES
    span = math.gcd(rows, 256)
    block = math.gcd(rows, 128)
    sets = [(t, r) for t in range(tiles) for r in range(0, rows, span)]

    def body(early_ref, late_ref, synthesis_ref, label_ref, filtered_ref, out_ref, *scratch):
        wide_ref, left_ref, kept_ref, tail_ref, top_ref = scratch
        tail_ref[...] = jnp.full(tail_ref.shape, storm_count, jnp.int32)
        tail_ref[:, 0:tail] = label_ref[:, lon_count - tail : lon_count]

        def names(t, row):
            if t == tiles - 1:
                return tail_ref[pl.ds(row, 8), :]
            return label_ref[pl.ds(row, 8), t * LANES : (t + 1) * LANES]

        for a in range(ranks):
            wide_ref[a, 0:early_rows] = early_ref[a].astype(jnp.float32)
            wide_ref[a, early_rows:] = late_ref[a].astype(jnp.float32)
        for o in range(band_rows):
            pieces = [
                wide_ref[a, (g * band_rows + o) * GROUP : (g * band_rows + o + 1) * GROUP]
                for a in range(ranks)
                for g in range(groups)
            ]
            turned = jnp.concatenate(pieces, axis=0).T
            for r in range(2):
                for w in range(wave_tiles):
                    left_ref[r * wave_tiles + w, pl.ds(o, fields, stride=band_rows), :] = turned[
                        r * fields : (r + 1) * fields, w * LANES : (w + 1) * LANES
                    ]
        for row in range(0, rows, block):
            left = [left_ref[i, row : row + block, :] for i in range(2 * wave_tiles)]
            left = jnp.concatenate(left, axis=1).astype(jnp.bfloat16)
            values = jnp.dot(left, synthesis_ref[...], preferred_element_type=jnp.float32)
            filtered_ref[row : row + block, :] = values[:, :lon_count].astype(jnp.bfloat16)
            for t in range(tiles):
                for i in range(0, block, 8):
                    kept_ref[t, row + i : row + i + 8, :] = jnp.where(
                        names(t, row + i) < storm_count,
                        values[i : i + 8, t * LANES : (t + 1) * LANES],
                        FLOOR,
                    )
        bests = []
        storms = []
        for t, start in sets:
            best = jnp.full((8, LANES), FLOOR, jnp.float32)
            storm = jnp.zeros((8, LANES), jnp.int32)
            for i in range(start, start + span, 8):
                value = kept_ref[t, i : i + 8, :]
                higher = value > best
                best = jnp.where(higher, value, best)
                storm = jnp.where(higher, names(t, i), storm)
            bests.append(best)
            storms.append(storm)

        def raise_tops(bests, storms):
            def per_storm(i, carry):
                picked = [jnp.where(storm == i, best, FLOOR) for best, storm in zip(bests, storms)]
                while len(picked) > 1:
                    paired = [jnp.maximum(a, b) for a, b in zip(picked[::2], picked[1::2])]
                    picked = paired + picked[2 * len(paired):]
                top = jnp.max(picked[0], axis=0, keepdims=True)
                top_ref[pl.ds(i, 1), :] = jnp.maximum(top_ref[pl.ds(i, 1), :], top)
                return carry

            lax.fori_loop(0, storm_count, per_storm, 0, unroll=8)

        def merge(a, b):
            higher = b[0] > a[0]
            return (jnp.where(higher, b[0], a[0]), jnp.where(higher, b[1], a[1]), a[2] + b[2])

        def tops():
            return jnp.max(top_ref[...].T, axis=0, keepdims=True)

        top_ref[...] = jnp.full(top_ref.shape, FLOOR, jnp.float32)
        raise_tops(bests, storms)

        def scan(carry):
            top = tops()
            table = [
                jnp.broadcast_to(top[:, h * LANES : (h + 1) * LANES], (8, LANES))
                for h in range(storm_count // LANES)
            ]
            tiny = jnp.zeros((8, LANES), jnp.float32)

            def per_rows(i, state):
                row = pl.multiple_of(i * (8 * SCAN_ROWS), 8 * SCAN_ROWS)
                merged = []
                for t in range(tiles):
                    found = [state[t]]
                    for r in range(SCAN_ROWS):
                        value = kept_ref[t, pl.ds(row + 8 * r, 8), :]
                        name = names(t, row + 8 * r)
                        place = jnp.bitwise_and(name, LANES - 1)
                        known = jnp.take_along_axis(table[0], place, axis=1)
                        for h in range(1, len(table)):
                            other = jnp.take_along_axis(table[h], place, axis=1)
                            known = jnp.where(name >= h * LANES, other, known)
                        is_open = value > known
                        found.append(
                            (
                                jnp.where(is_open, value, FLOOR),
                                name,
                                jnp.where(is_open, 1.0, 0.0),
                            )
                        )
                    while len(found) > 1:
                        paired = [merge(a, b) for a, b in zip(found[::2], found[1::2])]
                        found = paired + found[2 * len(paired) :]
                    merged.append(found[0])
                return tuple(merged)

            floor = jnp.full((8, LANES), FLOOR, jnp.float32)
            init = ((floor, jnp.zeros((8, LANES), jnp.int32), tiny),) * tiles
            state = lax.fori_loop(0, rows // (8 * SCAN_ROWS), per_rows, init)
            count = functools.reduce(jnp.maximum, [part[2] for part in state])
            most = jnp.max(count)

            @pl.when(most > 0.0)
            def _():
                raise_tops([part[0] for part in state], [part[1] for part in state])

            return most

        lax.while_loop(lambda most: most > 1.0, scan, jnp.float32(2.0))
        out_ref[...] = tops()

    return pl.pallas_call(
        body,
        out_shape=(whole((rows, lon_count), jnp.bfloat16), whole((1, storm_count), jnp.float32)),
        in_specs=[IN_VMEM] * 4,
        out_specs=(IN_VMEM, IN_VMEM),
        scratch_shapes=[
            pltpu.VMEM((ranks, groups * band_rows * GROUP, columns), jnp.float32),
            pltpu.VMEM((2 * wave_tiles, rows, LANES), jnp.float32),
            pltpu.VMEM((tiles, rows, LANES), jnp.float32),
            pltpu.VMEM((rows, LANES), jnp.int32),
            pltpu.VMEM((storm_count, LANES), jnp.float32),
        ],
        compiler_params=params(24),
    )(early, late, synthesis, labels)


def after(x, *others):
    return lax.optimization_barrier((x, *others))[0]


def local(vorticity, lat_order, storm_labels, storm_owner):
    field_count, lat_rows, lon_count = vorticity.shape
    lat_count = lat_order.shape[0]
    halves = lax.axis_size("half")
    ranks = lax.axis_size("rest")
    half_index = lax.axis_index("half")
    rank = lax.axis_index("rest")
    band_rows = storm_labels.shape[1]
    storm_count = storm_owner.shape[0]
    slots = MW // ranks
    chunks = slots // GROUP
    columns = 2 * field_count
    out_half = OUT_LAT // halves

    calls = [[16], [8, 8]] if slots == 32 else [[slots // 2], [slots // 2]]
    full_table = fourier_table(lon_count).reshape(lon_count, slots, ranks, 2)
    coefficients = []
    first = 0
    for part_slots in calls:
        pieces = []
        base = first
        for n in part_slots:
            pieces.append(full_table[:, base : base + n].transpose(0, 2, 1, 3).reshape(lon_count, -1, 2))
            base += n
        table = np.concatenate(pieces, axis=1).transpose(0, 2, 1).reshape(lon_count, -1)
        table = jnp.asarray(table.astype(jnp.bfloat16))
        coefficients += fourier(vorticity, table, ranks, part_slots)
        first = base
    stages = [n // GROUP for part_slots in calls for n in part_slots]
    group_count = slots // GROUP

    half_rows = ranks * lat_rows
    own_order = lax.dynamic_slice_in_dim(lat_order, half_index * half_rows, half_rows)
    colatitude = math.pi * (4.0 * own_order.astype(jnp.float32) + 3.0) / (4.0 * lat_count + 2.0)
    weights = math.pi / lat_count * jnp.sin(colatitude)
    band_index = jnp.arange(OUT_LAT, dtype=jnp.int32)
    band_index = ((band_index + half_index * out_half) % OUT_LAT).astype(jnp.float32)
    latitude = ((OUT_LAT - 1) / 2.0 - band_index) * (360.0 / OUT_LON) * (math.pi / 180.0)
    sine_values = jnp.concatenate([jnp.cos(latitude), jnp.sin(colatitude)])
    cosines = jnp.concatenate([jnp.sin(latitude), jnp.cos(colatitude)])
    orders = jnp.arange(slots, dtype=jnp.int32) * ranks + rank
    start_logs = jnp.asarray(diagonal_logs().reshape(slots, ranks))
    start_logs = lax.dynamic_slice_in_dim(start_logs, rank, 1, axis=1)
    orders = orders.astype(jnp.float32)[:, None]
    start = jnp.exp(start_logs + orders * jnp.log(sine_values)[None, :])
    def kernel(group, token):
        ordered = start if token is None else after(start, token)
        return kernel_table(
            orders[group * GROUP : (group + 1) * GROUP],
            ordered[group * GROUP : (group + 1) * GROUP],
            cosines[None, :],
            weights[None, :],
            OUT_LAT,
            MW - group * GROUP * ranks,
            out_half if group == group_count - 1 else 0,
        )

    def exchange(block):
        return lax.all_to_all(block, "rest", split_axis=0, concat_axis=0, tiled=True)

    def swapped(block):
        return lax.ppermute(block, "half", [(0, 1), (1, 0)])

    begins = [sum(stages[:i]) for i in range(len(stages) + 1)]
    last_stage = len(stages) - 1
    received = exchange(coefficients[0])
    tables = [kernel(0, coefficients[-1][0, 0, 0, :1])]
    cover = [coefficients[-1], *[part for table in tables for part in table]]
    swaps = []
    bands = []
    for i, count in enumerate(stages):
        received = after(received, *cover)
        if i == 1 and i < last_stage:
            received = after(received, swaps[0])
        following = None
        if i < last_stage:
            following = exchange(after(coefficients[i + 1], received))
        for g in range(begins[i], begins[i + 1]):
            if g == group_count - 1:
                own, other = spectral_part(tables[g][0], received, ranks)
                band = spectral_band(tables[g][1], own, swapped(other), ranks)
            else:
                own, other = apply_table(tables[g][0], received, (g - begins[i]) * GROUP)
                swaps.append(swapped(other))
                band = (own + swaps[-1].astype(jnp.float32)).astype(jnp.bfloat16)
            bands.append(band.reshape(ranks, band_rows * GROUP, columns))
            if i == 0 and g + 1 < stages[0]:
                tables.append(kernel(g + 1, other[0, :1]))
        if i == 0:
            later = [kernel(g, other[0, :1]) for g in range(stages[0], group_count)]
            tables += later
            cover = [other, *[part for table in later for part in table]]
        else:
            cover = [other, *bands]
        last_received, received = received, following

    early = exchange(after(jnp.concatenate(bands[:-1], axis=1), last_received))
    late = exchange(after(bands[-1], early))
    synthesis = synthesis_table(OUT_LON).reshape(group_count, GROUP, ranks, 2, OUT_LON)
    synthesis = synthesis.transpose(3, 2, 0, 1, 4).reshape(2 * MW, OUT_LON)
    synthesis = np.pad(synthesis, ((0, 0), (0, -OUT_LON % LANES)))
    filtered, local_peaks = grid_maxima(
        early,
        late,
        jnp.asarray(synthesis.astype(jnp.bfloat16)),
        storm_labels.reshape(field_count * band_rows, OUT_LON),
        band_rows,
        field_count,
        storm_count,
    )
    filtered = filtered.reshape(field_count, band_rows, OUT_LON)
    local_peaks = local_peaks[0]
    slot_ids = jnp.arange(storm_count, dtype=jnp.int32)
    by_slot = jnp.max(
        jnp.where(storm_owner[:, None] == slot_ids[None, :], local_peaks[:, None], FLOOR), axis=0
    )
    spec_count = halves * ranks
    shares = lax.all_to_all(
        by_slot.reshape(spec_count, storm_count // spec_count),
        ("half", "rest"),
        split_axis=0,
        concat_axis=0,
        tiled=True,
    )
    return (filtered, jnp.max(shares, axis=0))


def solution(mesh):
    groups = mesh.shape["grp"]
    spec_count = mesh.shape["spec"]
    split = Mesh(
        mesh.devices.reshape(groups, 2, spec_count // 2), axis_names=("grp", "half", "rest")
    )
    both = ("half", "rest")
    return jax.shard_map(
        local,
        mesh=split,
        in_specs=(P("grp", both, None), P(), P("grp", both, None), P("grp")),
        out_specs=(P("grp", both, None), P(("grp", "half", "rest"))),
        check_vma=False,
    )
```

time: 186 us -> 174 us (0.935)
  the two profiles are of different devices: /device:TPU:0 before, /device:TPU:2 now
where the time goes in v4:
time: 174 us; the launch traced here: 172 us
  Pallas kernels  65.5 us (38%)
  waiting for transfers between devices  33.9 us (19%)
  blocking collectives  25.7 us (15%)
  starting transfers between devices  24.6 us (14%)
  local copies, waits for them, and re-layouts  18.5 us (11%)
  other arithmetic  3.08 us (2%)
    pallas_call x2, Pallas kernels, fourier(): pl.pallas_call(body, out_shape=[whole((senders, n, rows, 2 * fields), jnp...  28.3 us
    ppermute x4, waiting for transfers between devices, swapped(): return lax.ppermute(block, 'half', [(0, 1), (1, 0)])  27.3 us
    pallas_call x4, Pallas kernels, kernel_table(): pl.pallas_call(body, out_shape=out_shape, in_specs=[IN_VMEM] * 4, out_spe...  17.1 us
    all_to_all x4, starting transfers between devices, exchange(): lax.all_to_all(block, 'rest', split_axis=0, concat_axis=0, tiled=True)  16.8 us
    unnamed x40, local copies, waits for them, and re-layouts  16.7 us
    all_to_all x1, blocking collectives, local(): lax.all_to_all(by_slot.reshape(spec_count, storm_count // spec_count), ('...  15.5 us
    pallas_call x1, Pallas kernels, grid_maxima(): pl.pallas_call(body, out_shape=(whole((rows, lon_count), jnp.bfloat16), w...  13.4 us
    all_to_all x1, blocking collectives, exchange(): lax.all_to_all(block, 'rest', split_axis=0, concat_axis=0, tiled=True)  10.2 us
  transfers between devices with their start and end apart: 8, of which 6 were waited for; matrix products, arithmetic and copies ran while one was open for 2% of the time, Pallas kernels for 22%

profile of v4, /device:TPU:2, one launch (start us, length us, event | category | flops | bytes accessed | tf_op | source)
XLA Modules:
  0.0 172.1 jit_solution(17302943746138106229)
XLA Ops:
  0.6 0.0 copy-start.6
  0.6 1.3 copy-done.6
  1.9 14.2 %shard_map.96 = bf16[8,16,80,128]{3,2,1,0:T(8,128)(2,1)S(1)} custom-call(bf16[64,80,2560]{2,1,0:T(8,128)(2,1)} %data_ref.3, bf16[2560,256]{1,0:T(8,128)(2,1)S(1)} %copy-done.6), custom_call_target="tpu_custom_call" | custom-call | tf_op jit(solution)/shard_map/pallas_call | solution.py:80
  16.1 1.5 copy-done
  17.6 3.9 %all-to-all-start = ((bf16[8,16,80,128]{3,2,1,0:T(8,128)(2,1)}), bf16[8,16,80,128]{3,2,1,0:T(8,128)(2,1)S(1)}, u32[]{:S(2)}, u32[]{:S(2)}) async-start(bf16[8,16,80,128]{3,2,1,0:T(8,128)(2,1)} %copy-done), calls=%async_computation | async-start | bytes 5242880 | tf_op jit(solution)/shard_map/all_to_all | solution.py:474
  21.6 0.7 dynamic-slice_bitcast_fusion
  22.3 0.1 fusion.6
  22.3 0.1 fusion.7
  22.4 0.1 broadcast_multiply_fusion
  22.5 0.1 add_exponential_fusion
  22.7 0.1 slice_bitcast_fusion
  22.7 0.1 copy.18.order_ref
  22.8 1.3 copy-done.9
  24.1 14.2 %shard_map.97 = (bf16[8,8,80,128]{3,2,1,0:T(8,128)(2,1)S(1)}, bf16[8,8,80,128]{3,2,1,0:T(8,128)(2,1)S(1)}) custom-call(bf16[64,80,2560]{2,1,0:T(8,128)(2,1)} %data_ref.3, bf16[2560,256]{1,0:T(8,128)(2,1)S(1)} %copy-done.9), custom_call_target="tpu_custom_call" | custom-call | tf_op jit(solution)/shard_map/pallas_call | solution.py:80
  38.3 1.1 copy-done.7
  39.4 1.1 copy-done.8
  40.5 0.6 fusion.9
  41.1 6.8 %shard_map.95.table_ref = bf16[8,256,640]{2,1,0:T(8,128)(2,1)S(1)} custom-call(f32[8,1]{1,0:T(8,128)S(1)} %copy.18.order_ref, f32[8,896]{1,0:T(8,128)S(1)} %get-tuple-element.51.start_ref, f32[1,896]{1,0:T(1,128)S(1)} %broadcast_in_dim.14.cos_ref, f32[1,640]{1,0:T(1,128)S(1)} %broadcast_in_dim.15.weight_ref), custom_call_target="tpu_custom_call" | custom-call | tf_op jit(solution)/shard_map/pallas_call | solution.py:172
  47.9 1.5 copy-done.3
  49.4 3.5 %all-to-all-done.data_ref = bf16[8,16,80,128]{3,2,1,0:T(8,128)(2,1)S(1)} async-done(((bf16[8,16,80,128]{3,2,1,0:T(8,128)(2,1)}), bf16[8,16,80,128]{3,2,1,0:T(8,128)(2,1)S(1)}, u32[]{:S(2)}, u32[]{:S(2)}) %all-to-all-start) | async-done | bytes 2621472 | tf_op jit(solution)/shard_map/all_to_all | solution.py:474
  52.9 4.5 %all-to-all-start.1 = ((bf16[8,8,80,128]{3,2,1,0:T(8,128)(2,1)}), bf16[8,8,80,128]{3,2,1,0:T(8,128)(2,1)}, u32[]{:S(2)}, u32[]{:S(2)}) async-start(bf16[8,8,80,128]{3,2,1,0:T(8,128)(2,1)} %copy-done.8), calls=%async_computation.1 | async-start | bytes 2621440 | tf_op jit(solution)/shard_map/all_to_all | solution.py:474
  57.4 1.7 %copy-done.4 = bf16[8,256,640]{2,1,0:T(8,128)(2,1)S(1)} copy-done((bf16[8,256,640]{2,1,0:T(8,128)(2,1)S(1)}, bf16[8,256,640]{2,1,0:T(8,128)(2,1)}, u32[]{:S(2)}) %copy-start.4) | copy-done | bytes 2621464
  59.1 1.6 shard_map.98
  60.7 0.8 copy-done.11
  61.5 2.6 %collective-permute-start = (bf16[1024,128]{1,0:T(8,128)(2,1)}, bf16[1024,128]{1,0:T(8,128)(2,1)}, u32[]{:S(2)}, u32[]{:S(2)}) collective-permute-start(bf16[1024,128]{1,0:T(8,128)(2,1)} %get-tuple-element.27), channel_id=1, source_target_pairs={{0,8},{8,0},{1,9},{9,1},{2,10},{10,2},{3,11},{11,3},{4,12},{12,4},... | collective-permute-start | bytes 786440 | tf_op jit(solution)/shard_map/ppermute | solution.py:477
  64.1 0.1 copy.19.order_ref
  64.2 0.1 copy.21.order_ref
  64.2 0.1 copy.20.order_ref
  64.3 5.4 %shard_map.99.table_ref = bf16[8,256,640]{2,1,0:T(8,128)(2,1)S(1)} custom-call(f32[8,1]{1,0:T(8,128)S(1)} %copy.19.order_ref, f32[8,896]{1,0:T(8,128)S(1)} %get-tuple-element.50.start_ref, f32[1,896]{1,0:T(1,128)S(1)} %broadcast_in_dim.14.cos_ref, f32[1,640]{1,0:T(1,128)S(1)} %broadcast_in_dim.15.weight_ref), custom_call_target="tpu_custom_call" | custom-call | tf_op jit(solution)/shard_map/pallas_call | solution.py:172
  69.8 0.7 copy-done.16
  70.5 1.3 shard_map.102
  71.8 0.7 copy-done.15
  72.5 3.7 %shard_map.101.table_ref = bf16[8,256,640]{2,1,0:T(8,128)(2,1)S(1)} custom-call(f32[8,1]{1,0:T(8,128)S(1)} %copy.20.order_ref, f32[8,896]{1,0:T(8,128)S(1)} %copy-done.15, f32[1,896]{1,0:T(1,128)S(1)} %broadcast_in_dim.14.cos_ref, f32[1,640]{1,0:T(1,128)S(1)} %broadcast_in_dim.15.weight_ref), custom_call_target="tpu_custom_call" | custom-call | tf_op jit(solution)/shard_map/pallas_call | solution.py:172
  76.2 1.5 copy-done.1
  77.7 0.9 shard_map.100
  78.6 0.8 copy-done.13
  79.4 0.7 copy-done.17
  80.1 0.0 all-to-all-done.1.data_ref
  80.1 0.0 collective-permute-done
  80.1 4.7 %all-to-all-start.2 = ((bf16[8,8,80,128]{3,2,1,0:T(8,128)(2,1)}), bf16[8,8,80,128]{3,2,1,0:T(8,128)(2,1)}, u32[]{:S(2)}, u32[]{:S(2)}) async-start(bf16[8,8,80,128]{3,2,1,0:T(8,128)(2,1)} %copy-done.7), calls=%async_computation.2 | async-start | bytes 2621440 | tf_op jit(solution)/shard_map/all_to_all | solution.py:474
  84.8 0.0 copy-start.14
  84.9 0.8 collective-permute-start.1
  85.7 2.2 %shard_map.103 = (f32[1024,128]{1,0:T(8,128)S(1)}, bf16[1024,128]{1,0:T(8,128)(2,1)S(1)}) custom-call(bf16[8,256,640]{2,1,0:T(8,128)(2,1)S(1)} %copy-done.2, bf16[8,8,80,128]{3,2,1,0:T(8,128)(2,1)} %all-to-all-done.1.data_ref), custom_call_target="tpu_custom_call" | custom-call | tf_op jit(solution)/shard_map/pallas_call | solution.py:195
  87.9 2.2 %collective-permute-start.2 = (bf16[1024,128]{1,0:T(8,128)(2,1)S(1)}, bf16[1024,128]{1,0:T(8,128)(2,1)S(1)}, u32[]{:S(2)}, u32[]{:S(2)}) collective-permute-start(bf16[1024,128]{1,0:T(8,128)(2,1)S(1)} %get-tuple-element.37), channel_id=1, source_target_pairs={{0,8},{8,0},{1,9},{9,1},{2,10},{10,2},{3,11},{11,3},{4,12},{12,4},... | collective-permute-start | bytes 786440 | tf_op jit(solution)/shard_map/ppermute | solution.py:477
  90.1 1.0 add_convert_fusion.2
  91.2 14.8 %collective-permute-done.1 = bf16[1024,128]{1,0:T(8,128)(2,1)S(1)} collective-permute-done((bf16[1024,128]{1,0:T(8,128)(2,1)}, bf16[1024,128]{1,0:T(8,128)(2,1)S(1)}, u32[]{:S(2)}, u32[]{:S(2)}) %collective-permute-start.1) | collective-permute-done | bytes 262176 | tf_op jit(solution)/shard_map/ppermute | solution.py:477
  105.9 0.1 add_convert_fusion.1
  106.0 5.3 %collective-permute-done.2 = bf16[1024,128]{1,0:T(8,128)(2,1)S(1)} collective-permute-done((bf16[1024,128]{1,0:T(8,128)(2,1)S(1)}, bf16[1024,128]{1,0:T(8,128)(2,1)S(1)}, u32[]{:S(2)}, u32[]{:S(2)}) %collective-permute-start.2) | collective-permute-done | bytes 262176 | tf_op jit(solution)/shard_map/ppermute | solution.py:477
  111.3 0.1 add_convert_fusion
  111.3 0.9 pad_maximum_fusion
  112.3 1.2 all-to-all-done.2.data_ref
  113.5 3.7 %all-to-all-start.3 = ((bf16[8,384,128]{2,1,0:T(8,128)(2,1)}), bf16[8,384,128]{2,1,0:T(8,128)(2,1)S(1)}, u32[]{:S(2)}, u32[]{:S(2)}) async-start(bf16[8,384,128]{2,1,0:T(8,128)(2,1)} %pad_maximum_fusion), calls=%async_computation.3 | async-start | bytes 1572864 | tf_op jit(solution)/shard_map/all_to_all | solution.py:474
  117.2 1.7 %shard_map.104 = (f32[288,128]{1,0:T(8,128)S(1)}, bf16[288,128]{1,0:T(8,128)(2,1)S(1)}) custom-call(bf16[8,64,640]{2,1,0:T(8,128)(2,1)S(1)} %get-tuple-element.32.table_ref, bf16[8,8,80,128]{3,2,1,0:T(8,128)(2,1)} %all-to-all-done.2.data_ref), custom_call_target="tpu_custom_call" | custom-call | tf_op jit(solution)/shard_map/pallas_call | solution.py:227
  118.9 2.1 %collective-permute-start.3 = (bf16[288,128]{1,0:T(8,128)(2,1)S(1)}, bf16[288,128]{1,0:T(8,128)(2,1)S(1)}, u32[]{:S(2)}, u32[]{:S(2)}) collective-permute-start(bf16[288,128]{1,0:T(8,128)(2,1)S(1)} %get-tuple-element.42), channel_id=1, source_target_pairs={{0,8},{8,0},{1,9},{9,1},{2,10},{10,2},{3,11},{11,3},{4,12},{12,4},... | collective-permute-start | bytes 221192 | tf_op jit(solution)/shard_map/ppermute | solution.py:477
  121.1 7.3 %collective-permute-done.3.mirrored_ref = bf16[288,128]{1,0:T(8,128)(2,1)S(1)} collective-permute-done((bf16[288,128]{1,0:T(8,128)(2,1)S(1)}, bf16[288,128]{1,0:T(8,128)(2,1)S(1)}, u32[]{:S(2)}, u32[]{:S(2)}) %collective-permute-start.3) | collective-permute-done | bytes 73760 | tf_op jit(solution)/shard_map/ppermute | solution.py:477
  128.3 0.2 shard_map.105
  128.6 1.9 %all-to-all-done.3.early_ref = bf16[8,384,128]{2,1,0:T(8,128)(2,1)S(1)} async-done(((bf16[8,384,128]{2,1,0:T(8,128)(2,1)}), bf16[8,384,128]{2,1,0:T(8,128)(2,1)S(1)}, u32[]{:S(2)}, u32[]{:S(2)}) %all-to-all-start.3) | async-done | bytes 786464 | tf_op jit(solution)/shard_map/all_to_all | solution.py:474
  130.4 10.2 %all_to_all.34.late_ref = bf16[8,128,128]{2,1,0:T(8,128)(2,1)S(1)} all-to-all(bf16[8,128,128]{2,1,0:T(8,128)(2,1)S(1)} %bitcast.19), channel_id=1, replica_groups=mesh['grp'=2,'half'=2,'rest'=8] {'rest'}, dimensions={0} | all-to-all | bytes 524288 | tf_op jit(solution)/shard_map/all_to_all | solution.py:474
  140.7 1.9 %copy-done.5 = s32[64,16,720]{2,1,0:T(8,128)S(1)} copy-done((s32[64,16,720]{2,1,0:T(8,128)S(1)}, s32[64,16,720]{2,1,0:T(8,128)}, u32[]{:S(2)}) %copy-start.5) | copy-done | bytes 2949144
  142.6 13.4 %shard_map.106 = (bf16[1024,720]{1,0:T(8,128)(2,1)}, f32[1,256]{1,0:T(1,128)S(1)}) custom-call(bf16[8,384,128]{2,1,0:T(8,128)(2,1)S(1)} %all-to-all-done.3.early_ref, bf16[8,128,128]{2,1,0:T(8,128)(2,1)S(1)} %all_to_all.34.late_ref, bf16[512,768]{1,0:T(8,128)(2,1)S(1)} %copy-done.10, s32[1024,720]{1,0:T(8,128)S(1)} %bitcast.18), custom_call_target="tpu_custom_call" | custom-call | tf_op jit(solution)/shard_map/pallas_call | solution.py:396
  155.9 0.1 select_reduce_fusion
  156.1 0.1 all_to_all.26
  156.2 15.5 %all_to_all.35 = f32[16,1,16]{2,1,0:T(1,128)S(1)} all-to-all(f32[16,1,16]{2,1,0:T(1,128)S(1)} %all_to_all.26), channel_id=1, replica_groups=mesh['grp'=2,'half'=2,'rest'=8] {'half','rest'}, dimensions={0} | all-to-all | bytes 2048 | tf_op jit(solution)/shard_map/all_to_all | solution.py:533
  171.6 0.5 reduce_max.19
  (28 shorter events, 0.1 us)
Async XLA Ops:
  0.6 1.3 copy-start.6
  16.1 1.5 copy-start
  17.6 4.8 %copy-start.18 = (s32[1280]{0:T(1024)S(1)}, s32[1280]{0:T(1024)}, u32[]{:S(2)}) copy-start(s32[1280]{0:T(1024)} %param.9) | copy-start | bytes 15364
  17.6 35.3 %all-to-all-start = ((bf16[8,16,80,128]{3,2,1,0:T(8,128)(2,1)}), bf16[8,16,80,128]{3,2,1,0:T(8,128)(2,1)S(1)}, u32[]{:S(2)}, u32[]{:S(2)}) async-start(bf16[8,16,80,128]{3,2,1,0:T(8,128)(2,1)} %copy-done), calls=%async_computation | async-start | bytes 5242880 | tf_op jit(solution)/shard_map/all_to_all | solution.py:474
  22.8 1.3 copy-start.9
  38.3 1.1 copy-start.7
  39.4 1.1 copy-start.8
  47.9 1.5 copy-start.3
  52.9 27.2 %all-to-all-start.1 = ((bf16[8,8,80,128]{3,2,1,0:T(8,128)(2,1)}), bf16[8,8,80,128]{3,2,1,0:T(8,128)(2,1)}, u32[]{:S(2)}, u32[]{:S(2)}) async-start(bf16[8,8,80,128]{3,2,1,0:T(8,128)(2,1)} %copy-done.8), calls=%async_computation.1 | async-start | bytes 2621440 | tf_op jit(solution)/shard_map/all_to_all | solution.py:474
  57.4 1.7 %copy-start.4 = (bf16[8,256,640]{2,1,0:T(8,128)(2,1)S(1)}, bf16[8,256,640]{2,1,0:T(8,128)(2,1)}, u32[]{:S(2)}) copy-start(bf16[8,256,640]{2,1,0:T(8,128)(2,1)} %copy-done.3) | copy-start | bytes 7864324
  60.7 0.8 copy-start.11
  61.5 18.6 %collective-permute-start = (bf16[1024,128]{1,0:T(8,128)(2,1)}, bf16[1024,128]{1,0:T(8,128)(2,1)}, u32[]{:S(2)}, u32[]{:S(2)}) collective-permute-start(bf16[1024,128]{1,0:T(8,128)(2,1)} %get-tuple-element.27), channel_id=1, source_target_pairs={{0,8},{8,0},{1,9},{9,1},{2,10},{10,2},{3,11},{11,3},{4,12},{12,4},... | collective-permute-start | bytes 786440 | tf_op jit(solution)/shard_map/ppermute | solution.py:477
  69.8 0.7 copy-start.16
  71.8 0.7 copy-start.15
  76.2 1.5 copy-start.1
  78.6 0.8 copy-start.13
  79.4 0.7 copy-start.17
  80.1 5.6 %copy-start.2 = (bf16[8,256,640]{2,1,0:T(8,128)(2,1)S(1)}, bf16[8,256,640]{2,1,0:T(8,128)(2,1)}, u32[]{:S(2)}) copy-start(bf16[8,256,640]{2,1,0:T(8,128)(2,1)} %copy-done.1) | copy-start | bytes 7864324
  80.1 33.3 %all-to-all-start.2 = ((bf16[8,8,80,128]{3,2,1,0:T(8,128)(2,1)}), bf16[8,8,80,128]{3,2,1,0:T(8,128)(2,1)}, u32[]{:S(2)}, u32[]{:S(2)}) async-start(bf16[8,8,80,128]{3,2,1,0:T(8,128)(2,1)} %copy-done.7), calls=%async_computation.2 | async-start | bytes 2621440 | tf_op jit(solution)/shard_map/all_to_all | solution.py:474
  84.8 5.3 %copy-start.12 = (f32[1024,128]{1,0:T(8,128)S(1)}, f32[1024,128]{1,0:T(8,128)}, u32[]{:S(2)}) copy-start(f32[1024,128]{1,0:T(8,128)} %copy-done.11) | copy-start | bytes 1572868
  84.8 21.1 %copy-start.14 = (f32[1024,128]{1,0:T(8,128)S(1)}, f32[1024,128]{1,0:T(8,128)}, u32[]{:S(2)}) copy-start(f32[1024,128]{1,0:T(8,128)} %copy-done.13) | copy-start | bytes 1572868
  84.9 21.1 %collective-permute-start.1 = (bf16[1024,128]{1,0:T(8,128)(2,1)}, bf16[1024,128]{1,0:T(8,128)(2,1)S(1)}, u32[]{:S(2)}, u32[]{:S(2)}) collective-permute-start(bf16[1024,128]{1,0:T(8,128)(2,1)} %copy-done.17), channel_id=1, source_target_pairs={{0,8},{8,0},{1,9},{9,1},{2,10},{10,2},{3,11},{11,3},{4,12},{12,4},... | collective-permute-start | bytes 786440 | tf_op jit(solution)/shard_map/ppermute | solution.py:477
  87.9 23.4 %collective-permute-start.2 = (bf16[1024,128]{1,0:T(8,128)(2,1)S(1)}, bf16[1024,128]{1,0:T(8,128)(2,1)S(1)}, u32[]{:S(2)}, u32[]{:S(2)}) collective-permute-start(bf16[1024,128]{1,0:T(8,128)(2,1)S(1)} %get-tuple-element.37), channel_id=1, source_target_pairs={{0,8},{8,0},{1,9},{9,1},{2,10},{10,2},{3,11},{11,3},{4,12},{12,4},... | collective-permute-start | bytes 786440 | tf_op jit(solution)/shard_map/ppermute | solution.py:477
  113.5 17.0 %all-to-all-start.3 = ((bf16[8,384,128]{2,1,0:T(8,128)(2,1)}), bf16[8,384,128]{2,1,0:T(8,128)(2,1)S(1)}, u32[]{:S(2)}, u32[]{:S(2)}) async-start(bf16[8,384,128]{2,1,0:T(8,128)(2,1)} %pad_maximum_fusion), calls=%async_computation.3 | async-start | bytes 1572864 | tf_op jit(solution)/shard_map/all_to_all | solution.py:474
  117.2 23.5 %copy-start.10 = (bf16[512,768]{1,0:T(8,128)(2,1)S(1)}, bf16[512,768]{1,0:T(8,128)(2,1)}, u32[]{:S(2)}) copy-start(bf16[512,768]{1,0:T(8,128)(2,1)} %constant.66.clone.synthesis_ref) | copy-start | bytes 2359300
  118.9 9.4 %collective-permute-start.3 = (bf16[288,128]{1,0:T(8,128)(2,1)S(1)}, bf16[288,128]{1,0:T(8,128)(2,1)S(1)}, u32[]{:S(2)}, u32[]{:S(2)}) collective-permute-start(bf16[288,128]{1,0:T(8,128)(2,1)S(1)} %get-tuple-element.42), channel_id=1, source_target_pairs={{0,8},{8,0},{1,9},{9,1},{2,10},{10,2},{3,11},{11,3},{4,12},{12,4},... | collective-permute-start | bytes 221192 | tf_op jit(solution)/shard_map/ppermute | solution.py:477
  140.7 1.9 %copy-start.5 = (s32[64,16,720]{2,1,0:T(8,128)S(1)}, s32[64,16,720]{2,1,0:T(8,128)}, u32[]{:S(2)}) copy-start(s32[64,16,720]{2,1,0:T(8,128)} %param.10) | copy-start | bytes 8847364
  142.6 13.4 %copy-start.19 = (s32[256]{0:T(256)S(1)}, s32[256]{0:T(256)}, u32[]{:S(2)}) copy-start(s32[256]{0:T(256)} %param.11) | copy-start | bytes 3076
